TPU v7x, 32 devices: a whole 2x2x4 slice. The times are simulated.
32 devices in a mesh: dp: 8 (over y, x, core), tensor: 4 (over z).
Axes of the slice: x: 2, y: 2, z: 4, core: 2. Of those that a mesh axis runs over, the one named last changes fastest.
Arguments:
- activations: bfloat16 [8192, 1024], P(('dp', 'tensor')), may hold values from -6 to 6
- segments: int32 [8192], P('dp'), may hold values from 0 to 31, as said below
- attn_weight: bfloat16 [1, 3, 1024, 1024], P(None, None, 'dp', 'tensor'), may hold values from -0.1875 to 0.1875
- out_weight: bfloat16 [1, 1024, 1024], P(None, 'tensor', 'dp'), may hold values from -0.75 to 0.75
- up_weight: bfloat16 [1, 1024, 4096], P(None, 'dp', 'tensor'), may hold values from -0.1875 to 0.1875
- down_weight: bfloat16 [1, 4096, 1024], P(None, 'tensor', 'dp'), may hold values from -0.09375 to 0.09375
- norm_gains: bfloat16 [1, 2, 1024], P(None, None, 'dp'), may hold values from 0.5 to 1.5
- bias_rows: bfloat16 [1, 10, 1024], P(None, None, 'dp'), may hold values from -1 to 1
- cotangent: float32 [8192, 1024], P(('dp', 'tensor')), may hold values from -6 to 6
Outputs:
- layer_output: float32 [8192, 1024], P(('dp', 'tensor'))
- input_grad: float32 [8192, 1024], P(('dp', 'tensor'))
- attn_weight_grad: float32 [1, 3, 1024, 1024], P(None, None, 'dp', 'tensor')
- out_weight_grad: float32 [1, 1024, 1024], P(None, 'tensor', 'dp')
- up_weight_grad: float32 [1, 1024, 4096], P(None, 'dp', 'tensor')
- down_weight_grad: float32 [1, 4096, 1024], P(None, 'tensor', 'dp')
- gain_grad: float32 [1, 2, 1024], P(None, None, 'dp')
- bias_grad: float32 [1, 10, 1024], P(None, None, 'dp')
Inputs may be any that keep to these rules, and one draw needn't show every extreme that they name: `segments`: within each sequence of 1024 tokens ids never fall; every document has 200 tokens or more; sequences share no id; the last document of sequence j has id 4 j + 3 and ids of sequence j lie in 4 j to 4 j + 3.
All inputs are finite; a program needn't handle non-finite values.
Results may differ from a plain program's by a relative error of at most 0.018.
Values may be sent and summed in bfloat16 or wider, within the bound.
A program may use at most 128 MiB of HBM per device.

v0:
```python
import functools

import jax
import jax.numpy as jnp
from jax import lax
from jax.experimental import pallas as pl
from jax.experimental.pallas import tpu as pltpu
from jax.sharding import PartitionSpec as P

HD = 64
SEQ = 1024
EPSILON = 1e-05
MASKED = -1e30
MESH_ID = pl.DeviceIdType.MESH
BF = jnp.bfloat16
F32 = jnp.float32
ANY = pl.BlockSpec(memory_space=pl.ANY)
VM = pl.BlockSpec(memory_space=pltpu.VMEM)


def layer_norm(values, gain_row, shift_row):
    center = values - jnp.mean(values, axis=-1, keepdims=True)
    spread = jnp.mean(center * center, axis=-1, keepdims=True)
    return center * lax.rsqrt(spread + EPSILON) * gain_row + shift_row


def norm_stats(values):
    center = values - jnp.mean(values, axis=-1, keepdims=True)
    spread = jnp.mean(center * center, axis=-1, keepdims=True)
    scale = lax.rsqrt(spread + EPSILON)
    return center * scale, scale


def norm_back(grad, unit, scale, gain_row):
    u = grad * gain_row
    mean_u = jnp.mean(u, axis=-1, keepdims=True)
    mean_ux = jnp.mean(u * unit, axis=-1, keepdims=True)
    return scale * (u - mean_u - unit * mean_ux)


def gelu_tanh(values):
    return jax.nn.gelu(values, approximate=True)


class Geometry:
    def __init__(self, dp, tensor):
        self.dp, self.tensor = dp, tensor
        self.c_size = 2
        rest = dp // 2
        self.a_size = 1
        while self.a_size * self.a_size < rest:
            self.a_size *= 2
        self.b_size = rest // self.a_size
        assert self.a_size * self.b_size * 2 == dp

    def bind(self):
        spot = Spot()
        spot.geo = self
        spot.d = lax.axis_index("dp")
        spot.t = lax.axis_index("tensor")
        spot.c = lax.rem(spot.d, 2)
        half = lax.div(spot.d, 2)
        spot.a = lax.rem(half, self.a_size)
        spot.b = lax.div(half, self.a_size)
        return spot


class Spot:
    def rank(self, b, a, c):
        return (b * self.geo.a_size + a) * 2 + c

    def at_t(self, t):
        return (self.d, t)

    def at_d(self, d):
        return (d, self.t)


def ring_next(rank, step, size):
    return lax.rem(rank + step, size)


def ring_prev(rank, step, size):
    return lax.rem(rank + size - step, size)


class Wire:
    def __init__(self, send, recv):
        self.send_sems, self.recv_sems = send, recv
        self.count = 0
        self.pending = []

    def take(self, n):
        first = self.count
        self.count += n
        return first

    def copy(self, i, src, dst, device):
        return pltpu.make_async_remote_copy(
            src_ref=src, dst_ref=dst, send_sem=self.send_sems.at[i], recv_sem=self.recv_sems.at[i],
            device_id=device, device_id_type=MESH_ID)

    def start(self, i, src, dst, device, when=None):
        copy = self.copy(i, src, dst, device)
        if when is None:
            copy.start()
        else:
            pl.when(when)(copy.start)
        self.pending.append((copy, when))

    def landed(self, i, dst, device, when=None):
        copy = self.copy(i, dst, dst, device)
        if when is None:
            copy.wait_recv()
        else:
            pl.when(when)(copy.wait_recv)

    def drain(self):
        for copy, when in self.pending:
            if when is None:
                copy.wait_send()
            else:
                pl.when(when)(copy.wait_send)
        self.pending = []


def greet(spot, with_dp=True):
    geo = spot.geo
    barrier = pltpu.get_barrier_semaphore()
    total = 0
    for step in range(1, geo.tensor):
        pl.semaphore_signal(barrier, inc=1, device_id=spot.at_t(ring_next(spot.t, step, geo.tensor)), device_id_type=MESH_ID)
        total += 1
    for step in range(1, geo.dp):
        pl.semaphore_signal(barrier, inc=1, device_id=spot.at_d(ring_next(spot.d, step, geo.dp)), device_id_type=MESH_ID)
        total += 1
    pl.semaphore_wait(barrier, total)


class LineGather:
    def __init__(self, spot, wire, src, slot):
        self.spot, self.wire, self.src, self.slot = spot, wire, src, slot
        self.size = spot.geo.tensor
        self.line = self.size == 4
        self.first = wire.take(6 if self.line else self.size - 1)

    def start(self):
        spot, t = self.spot, self.spot.t
        if not self.line:
            for step in range(1, self.size):
                self.wire.start(self.first + step - 1, self.src, self.slot(t), spot.at_t(ring_next(t, step, self.size)))
            return
        for k, delta in enumerate((2, -2, 1, -1)):
            to = t + delta
            ok = (to >= 0) & (to < self.size)
            self.wire.start(self.first + k, self.src, self.slot(t), spot.at_t(to), when=ok)

    def forward(self):
        if not self.line:
            return
        spot, t = self.spot, self.spot.t
        self.wire.landed(self.first + 0, self.slot(t - 2), spot.at_t(t - 2), when=t == 2)
        self.wire.start(self.first + 4, self.slot(t - 2), self.slot(t - 2), spot.at_t(t + 1), when=t == 2)
        self.wire.landed(self.first + 1, self.slot(t + 2), spot.at_t(t + 2), when=t == 1)
        self.wire.start(self.first + 5, self.slot(t + 2), self.slot(t + 2), spot.at_t(t - 1), when=t == 1)

    def finish(self):
        spot, t = self.spot, self.spot.t
        if not self.line:
            for step in range(1, self.size):
                source = ring_prev(t, step, self.size)
                self.wire.landed(self.first + step - 1, self.slot(source), spot.at_t(source))
            return
        self.wire.landed(self.first + 0, self.slot(t - 2), spot.at_t(t - 2), when=t == 3)
        self.wire.landed(self.first + 1, self.slot(t + 2), spot.at_t(t + 2), when=t == 0)
        self.wire.landed(self.first + 2, self.slot(t - 1), spot.at_t(t - 1), when=t >= 1)
        self.wire.landed(self.first + 3, self.slot(t + 1), spot.at_t(t + 1), when=t <= 2)
        self.wire.landed(self.first + 4, self.slot(t - 3), spot.at_t(t - 1), when=t == 3)
        self.wire.landed(self.first + 5, self.slot(t + 3), spot.at_t(t + 1), when=t == 0)


class LineScatter:
    def __init__(self, spot, wire, part, land, add):
        self.spot, self.wire, self.part, self.land, self.add = spot, wire, part, land, add
        self.size = spot.geo.tensor
        self.line = self.size == 4
        self.first = wire.take(6 if self.line else self.size - 1)

    def start(self):
        spot, t = self.spot, self.spot.t
        if not self.line:
            for step in range(1, self.size):
                to = ring_next(t, step, self.size)
                self.wire.start(self.first + step - 1, self.part(to), self.land(step - 1), spot.at_t(to))
            return
        self.wire.start(self.first + 4, self.part(3), self.land(4), spot.at_t(1), when=t == 0)
        self.wire.start(self.first + 5, self.part(0), self.land(4), spot.at_t(2), when=t == 3)
        self.wire.start(self.first + 0, self.part(2), self.land(0), spot.at_t(2), when=t == 0)
        self.wire.start(self.first + 1, self.part(1), self.land(1), spot.at_t(1), when=t == 3)
        self.wire.start(self.first + 2, self.part(jnp.minimum(t + 1, 3)), self.land(2), spot.at_t(t + 1), when=t <= 2)
        self.wire.start(self.first + 3, self.part(jnp.maximum(t - 1, 0)), self.land(3), spot.at_t(t - 1), when=t >= 1)

    def start_block(self, i):
        spot, t = self.spot, self.spot.t
        if i == 3:
            self.wire.start(self.first + 4, self.part(3), self.land(4), spot.at_t(1), when=t == 0)
        if i == 0:
            self.wire.start(self.first + 5, self.part(0), self.land(4), spot.at_t(2), when=t == 3)
        if i == 2:
            self.wire.start(self.first + 0, self.part(2), self.land(0), spot.at_t(2), when=t == 0)
        if i == 1:
            self.wire.start(self.first + 1, self.part(1), self.land(1), spot.at_t(1), when=t == 3)
        if i >= 1:
            self.wire.start(self.first + 2, self.part(i), self.land(2), spot.at_t(i), when=t == i - 1)
        if i <= 2:
            self.wire.start(self.first + 3, self.part(i), self.land(3), spot.at_t(i), when=t == i + 1)

    def forward(self):
        if not self.line:
            return
        spot, t = self.spot, self.spot.t

        @pl.when(t == 1)
        def _():
            self.wire.landed(self.first + 4, self.land(4), spot.at_t(0))
            self.add(self.part(3), self.land(4))

        @pl.when(t == 2)
        def _():
            self.wire.landed(self.first + 5, self.land(4), spot.at_t(3))
            self.add(self.part(0), self.land(4))

        self.wire.start(self.first + 0, self.part(3), self.land(0), spot.at_t(3), when=t == 1)
        self.wire.start(self.first + 1, self.part(0), self.land(1), spot.at_t(0), when=t == 2)

    def finish(self, total):
        spot, t = self.spot, self.spot.t
        if not self.line:
            for step in range(1, self.size):
                self.wire.landed(self.first + step - 1, self.land(step - 1), spot.at_t(ring_prev(t, step, self.size)))
                total(self.land(step - 1))
            return
        for k, delta in enumerate((2, -2, 1, -1)):
            source = t - delta

            @pl.when((source >= 0) & (source < self.size))
            def _():
                self.wire.landed(self.first + k, self.land(k), spot.at_t(source))
                total(self.land(k))


def add_into(rows):
    def add(dst, src):
        dst[...] = (dst[...].astype(F32) + src[...].astype(F32)).astype(dst.dtype)

    return add


def add_tiled(dst, src, tile):
    count = dst.shape[0] // tile

    def step(i, carry):
        rows = pl.ds(pl.multiple_of(i * tile, tile), tile)
        dst[rows] = (dst[rows].astype(F32) + src[rows].astype(F32)).astype(dst.dtype)
        return carry

    lax.fori_loop(0, count, step, 0)


class WeightGather:
    def __init__(self, spot, wire, piece, full):
        geo = spot.geo
        self.spot, self.wire, self.piece, self.full = spot, wire, piece, full
        self.rows = piece.shape[0]
        self.line = LineGather(spot, wire, piece, lambda t: full.at[t, self.span(spot.d)])
        self.one_a = wire.take(geo.a_size - 1)
        self.one_b = wire.take(geo.b_size - 1)
        self.two_a = wire.take((geo.b_size - 1) * geo.a_size)
        self.two_b = wire.take((geo.a_size - 1) * geo.b_size)
        self.last = wire.take(geo.a_size * geo.b_size)
        self.half = geo.tensor // 2

    def span(self, d):
        return pl.ds(pl.multiple_of(d * self.rows, self.rows), self.rows)

    def low(self, d):
        return self.full.at[pl.ds(0, self.half), self.span(d)]

    def high(self, d):
        return self.full.at[pl.ds(self.half, self.spot.geo.tensor - self.half), self.span(d)]

    def both(self, d):
        return self.full.at[:, self.span(d)]

    def first(self):
        spot, geo = self.spot, self.spot.geo
        mine = spot.d
        for j in range(1, geo.a_size):
            to = spot.rank(spot.b, ring_next(spot.a, j, geo.a_size), spot.c)
            self.wire.start(self.one_a + j - 1, self.low(mine), self.low(mine), spot.at_d(to))
        for j in range(1, geo.b_size):
            to = spot.rank(ring_next(spot.b, j, geo.b_size), spot.a, spot.c)
            self.wire.start(self.one_b + j - 1, self.high(mine), self.high(mine), spot.at_d(to))
        sibling = spot.rank(spot.b, spot.a, 1 - spot.c)
        self.wire.start(self.last, self.both(mine), self.both(mine), spot.at_d(sibling))

    def second(self):
        spot, geo = self.spot, self.spot.geo
        for i in range(geo.a_size):
            held = spot.rank(spot.b, ring_prev(spot.a, i, geo.a_size), spot.c)
            if i:
                self.wire.landed(self.one_a + i - 1, self.low(held), spot.at_d(held))
            for j in range(1, geo.b_size):
                to = spot.rank(ring_next(spot.b, j, geo.b_size), spot.a, spot.c)
                self.wire.start(self.two_a + (j - 1) * geo.a_size + i, self.low(held), self.low(held), spot.at_d(to))
        for i in range(geo.b_size):
            held = spot.rank(ring_prev(spot.b, i, geo.b_size), spot.a, spot.c)
            if i:
                self.wire.landed(self.one_b + i - 1, self.high(held), spot.at_d(held))
            for j in range(1, geo.a_size):
                to = spot.rank(spot.b, ring_next(spot.a, j, geo.a_size), spot.c)
                self.wire.start(self.two_b + (j - 1) * geo.b_size + i, self.high(held), self.high(held), spot.at_d(to))

    def third(self):
        spot, geo = self.spot, self.spot.geo
        for j in range(1, geo.b_size):
            for i in range(geo.a_size):
                held = spot.rank(ring_prev(spot.b, j, geo.b_size), ring_prev(spot.a, i, geo.a_size), spot.c)
                source = spot.rank(ring_prev(spot.b, j, geo.b_size), spot.a, spot.c)
                self.wire.landed(self.two_a + (j - 1) * geo.a_size + i, self.low(held), spot.at_d(source))
        for j in range(1, geo.a_size):
            for i in range(geo.b_size):
                held = spot.rank(ring_prev(spot.b, i, geo.b_size), ring_prev(spot.a, j, geo.a_size), spot.c)
                source = spot.rank(spot.b, ring_prev(spot.a, j, geo.a_size), spot.c)
                self.wire.landed(self.two_b + (j - 1) * geo.b_size + i, self.high(held), spot.at_d(source))
        sibling = spot.rank(spot.b, spot.a, 1 - spot.c)
        for j in range(geo.b_size):
            for i in range(geo.a_size):
                if i or j:
                    held = spot.rank(ring_prev(spot.b, j, geo.b_size), ring_prev(spot.a, i, geo.a_size), spot.c)
                    self.wire.start(self.last + j * geo.a_size + i, self.both(held), self.both(held), spot.at_d(sibling))

    def fourth(self):
        spot, geo = self.spot, self.spot.geo
        sibling = spot.rank(spot.b, spot.a, 1 - spot.c)
        for j in range(geo.b_size):
            for i in range(geo.a_size):
                held = spot.rank(ring_prev(spot.b, j, geo.b_size), ring_prev(spot.a, i, geo.a_size), 1 - spot.c)
                self.wire.landed(self.last + j * geo.a_size + i, self.both(held), spot.at_d(sibling))


def gather_sems(geo):
    ab = geo.a_size * geo.b_size
    return 6 + geo.tensor + geo.a_size + geo.b_size + 3 * ab


class WeightScatter:
    def __init__(self, spot, wire, part, held, mine, one_a, one_b, two_a, two_b, land, sem):
        geo = spot.geo
        self.spot, self.wire, self.part, self.held, self.mine = spot, wire, part, held, mine
        self.one_a_buf, self.one_b_buf, self.two_a_buf, self.two_b_buf = one_a, one_b, two_a, two_b
        self.sem = sem
        self.rows = held.shape[3]
        self.half = geo.tensor // 2
        ab = geo.a_size * geo.b_size
        self.zero = wire.take(ab)
        self.one_a = wire.take(geo.a_size - 1)
        self.one_b = wire.take(geo.b_size - 1)
        self.two_a = wire.take(geo.b_size - 1)
        self.two_b = wire.take(geo.a_size - 1)
        here = held.at[spot.b, spot.a]
        self.line = LineScatter(spot, wire, lambda t: here.at[t], lambda k: land.at[k], lambda dst, src: add_tiled(dst, src, min(64, self.rows)))

    def span(self, d):
        return pl.ds(pl.multiple_of(d * self.rows, self.rows), self.rows)

    def start(self):
        spot, geo = self.spot, self.spot.geo
        sibling = spot.rank(spot.b, spot.a, 1 - spot.c)
        self.loads = []
        for b in range(geo.b_size):
            for a in range(geo.a_size):
                theirs = self.part.at[:, self.span(spot.rank(b, a, 1 - spot.c))]
                self.wire.start(self.zero + b * geo.a_size + a, theirs, self.held.at[b, a], spot.at_d(sibling))
                ours = self.part.at[:, self.span(spot.rank(b, a, spot.c))]
                load = pltpu.make_async_copy(ours, self.mine.at[b, a], self.sem.at[b * geo.a_size + a])
                load.start()
                self.loads.append(load)

    def add(self, dst, src):
        n = dst.shape[0]
        tile = min(64, self.rows)
        per = self.rows // tile

        def step(i, carry):
            rows = pl.ds(pl.multiple_of(lax.rem(i, per) * tile, tile), tile)
            j = lax.div(i, per)
            dst[j, rows] = (dst[j, rows].astype(F32) + src[j, rows].astype(F32)).astype(dst.dtype)
            return carry

        lax.fori_loop(0, n * per, step, 0)

    def first(self):
        spot, geo = self.spot, self.spot.geo
        sibling = spot.rank(spot.b, spot.a, 1 - spot.c)
        for b in range(geo.b_size):
            for a in range(geo.a_size):
                i = b * geo.a_size + a
                self.loads[i].wait()
                self.wire.landed(self.zero + i, self.held.at[b, a], spot.at_d(sibling))
                self.add(self.held.at[b, a], self.mine.at[b, a])
        for j in range(1, geo.a_size):
            a = ring_next(spot.a, j, geo.a_size)
            to = spot.rank(spot.b, a, spot.c)
            self.wire.start(self.one_a + j - 1, self.held.at[:, a, pl.ds(0, self.half)], self.one_a_buf.at[j - 1], spot.at_d(to))
        for j in range(1, geo.b_size):
            b = ring_next(spot.b, j, geo.b_size)
            to = spot.rank(b, spot.a, spot.c)
            self.wire.start(self.one_b + j - 1, self.held.at[b, :, pl.ds(self.half, self.half)], self.one_b_buf.at[j - 1], spot.at_d(to))

    def second(self):
        spot, geo = self.spot, self.spot.geo
        low, high = pl.ds(0, self.half), pl.ds(self.half, self.half)
        for j in range(1, geo.a_size):
            self.wire.landed(self.one_a + j - 1, self.one_a_buf.at[j - 1], spot.at_d(spot.rank(spot.b, ring_prev(spot.a, j, geo.a_size), spot.c)))
            for b in range(geo.b_size):
                self.add(self.held.at[b, spot.a, low], self.one_a_buf.at[j - 1, b])
        for j in range(1, geo.b_size):
            b = ring_next(spot.b, j, geo.b_size)
            self.wire.start(self.two_a + j - 1, self.held.at[b, spot.a, low], self.two_a_buf.at[j - 1], spot.at_d(spot.rank(b, spot.a, spot.c)))
        for j in range(1, geo.b_size):
            self.wire.landed(self.one_b + j - 1, self.one_b_buf.at[j - 1], spot.at_d(spot.rank(ring_prev(spot.b, j, geo.b_size), spot.a, spot.c)))
            for a in range(geo.a_size):
                self.add(self.held.at[spot.b, a, high], self.one_b_buf.at[j - 1, a])
        for j in range(1, geo.a_size):
            a = ring_next(spot.a, j, geo.a_size)
            self.wire.start(self.two_b + j - 1, self.held.at[spot.b, a, high], self.two_b_buf.at[j - 1], spot.at_d(spot.rank(spot.b, a, spot.c)))

    def third(self):
        spot, geo = self.spot, self.spot.geo
        low, high = pl.ds(0, self.half), pl.ds(self.half, self.half)
        for j in range(1, geo.b_size):
            self.wire.landed(self.two_a + j - 1, self.two_a_buf.at[j - 1], spot.at_d(spot.rank(ring_prev(spot.b, j, geo.b_size), spot.a, spot.c)))
            self.add(self.held.at[spot.b, spot.a, low], self.two_a_buf.at[j - 1])
        for j in range(1, geo.a_size):
            self.wire.landed(self.two_b + j - 1, self.two_b_buf.at[j - 1], spot.at_d(spot.rank(spot.b, ring_prev(spot.a, j, geo.a_size), spot.c)))
            self.add(self.held.at[spot.b, spot.a, high], self.two_b_buf.at[j - 1])
        self.line.start()

    def fourth(self, out):
        spot = self.spot
        self.line.forward()
        here = self.held.at[spot.b, spot.a, spot.t]
        tile = min(64, self.rows)

        def step(i, carry):
            rows = pl.ds(pl.multiple_of(i * tile, tile), tile)
            out[rows] = here[rows].astype(F32)
            return carry

        lax.fori_loop(0, self.rows // tile, step, 0)
        self.line.finish(lambda ref: add_tiled(out, ref, tile))


def k3_body(geo, ga_ref, g_ref, gaf, out, *rest):
    *bufs, send, recv, local, loads = rest
    spot = geo.bind()
    wire = Wire(send, recv)
    rows = ga_ref.shape[0]

    def slot(t):
        return gaf.at[pl.ds(pl.multiple_of(t * rows, rows), rows)]

    own = pltpu.make_async_copy(ga_ref, slot(spot.t), local.at[0])
    own.start()
    greet(spot)
    gather = LineGather(spot, wire, ga_ref, slot)
    scatters = [WeightScatter(spot, wire, g_ref.at[k], *(buf.at[k] for buf in bufs), loads.at[k]) for k in range(2)]
    scatters[1].start()
    scatters[0].start()
    gather.start()
    scatters[1].first()
    scatters[0].first()
    gather.forward()
    scatters[1].second()
    scatters[0].second()
    scatters[1].third()
    scatters[0].third()
    gather.finish()
    scatters[1].fourth(out.at[1])
    scatters[0].fourth(out.at[0])
    wire.drain()
    own.wait()


def k3(geo, ga, grads):
    rows = grads.shape[2] // geo.dp
    width = grads.shape[3]
    t, a, b = geo.tensor, geo.a_size, geo.b_size
    ab = a * b
    half = t // 2
    sems = 12 + 2 * t + 2 * (ab + 2 * a + 2 * b + 6)
    return pl.pallas_call(
        functools.partial(k3_body, geo),
        out_shape=(
            jax.ShapeDtypeStruct((t * ga.shape[0], ga.shape[1]), BF),
            jax.ShapeDtypeStruct((2, rows, width), F32),
        ),
        in_specs=[ANY, ANY],
        out_specs=(ANY, VM),
        scratch_shapes=[
            pltpu.VMEM((2, b, a, t, rows, width), BF),
            pltpu.VMEM((2, b, a, t, rows, width), BF),
            pltpu.VMEM((2, a - 1, b, half, rows, width), BF),
            pltpu.VMEM((2, b - 1, a, half, rows, width), BF),
            pltpu.VMEM((2, b - 1, half, rows, width), BF),
            pltpu.VMEM((2, a - 1, half, rows, width), BF),
            pltpu.VMEM((2, max(5, t - 1), rows, width), BF),
            pltpu.SemaphoreType.DMA((sems,)), pltpu.SemaphoreType.DMA((sems,)),
            pltpu.SemaphoreType.DMA((1,)), pltpu.SemaphoreType.DMA((2, ab))],
        compiler_params=pltpu.CompilerParams(collective_id=3, has_side_effects=True, vmem_limit_bytes=56 * 2**20),
        name="k3",
    )(ga, grads)


def k4_body(geo, part, w_ref, s_ref, total, wout, sout, land, wland, sland, stot, tland, send, recv):
    spot = geo.bind()
    wire = Wire(send, recv)
    rows = total.shape[0]
    wrows = wout.shape[1]
    greet(spot)

    def block(t):
        return part.at[pl.ds(pl.multiple_of(t * rows, rows), rows)]

    def wblock(d):
        return w_ref.at[:, pl.ds(pl.multiple_of(d * wrows, wrows), wrows)]

    small = wire.take(geo.dp - 1)
    big = wire.take(geo.dp - 1)
    last = wire.take(geo.tensor - 1)
    scatter = LineScatter(spot, wire, block, lambda k: land.at[k], lambda dst, src: add_tiled(dst, src, 64))
    scatter.start()
    for step in range(1, geo.dp):
        to = ring_next(spot.d, step, geo.dp)
        wire.start(small + step - 1, s_ref.at[to], sland.at[step - 1], spot.at_d(to))
    for step in range(1, geo.dp):
        to = ring_next(spot.d, step, geo.dp)
        wire.start(big + step - 1, wblock(to), wland.at[step - 1], spot.at_d(to))
    stot[...] = s_ref[spot.d]
    for step in range(1, geo.dp):
        wire.landed(small + step - 1, sland.at[step - 1], spot.at_d(ring_prev(spot.d, step, geo.dp)))
        stot[...] += sland[step - 1]
    for step in range(1, geo.tensor):
        wire.start(last + step - 1, stot, tland.at[step - 1], spot.at_t(ring_next(spot.t, step, geo.tensor)))
    scatter.forward()
    own = wblock(spot.d)
    for k in range(w_ref.shape[0]):
        wout[k] = own[k].astype(F32)
    for step in range(1, geo.dp):
        wire.landed(big + step - 1, wland.at[step - 1], spot.at_d(ring_prev(spot.d, step, geo.dp)))

        def add(k, carry):
            wout[k] += wland[step - 1, k].astype(F32)
            return carry

        lax.fori_loop(0, w_ref.shape[0], add, 0)
    sout[...] = stot[...]
    for step in range(1, geo.tensor):
        wire.landed(last + step - 1, tland.at[step - 1], spot.at_t(ring_prev(spot.t, step, geo.tensor)))
        sout[...] += tland[step - 1]
    mine = block(spot.t)

    def set_total(i, carry):
        span = pl.ds(pl.multiple_of(i * 64, 64), 64)
        total[span] = mine[span].astype(F32)
        return carry

    lax.fori_loop(0, rows // 64, set_total, 0)
    scatter.finish(lambda ref: add_tiled(total, ref, 64))
    wire.drain()


def k4(geo, part, wgrad, small):
    rows = part.shape[0] // geo.tensor
    width = part.shape[1]
    wshape = (wgrad.shape[0], wgrad.shape[1] // geo.dp, wgrad.shape[2])
    sshape = small.shape[1:]
    sems = 6 + 2 * geo.tensor + 2 * geo.dp
    return pl.pallas_call(
        functools.partial(k4_body, geo),
        out_shape=(
            jax.ShapeDtypeStruct((rows, width), F32),
            jax.ShapeDtypeStruct(wshape, F32),
            jax.ShapeDtypeStruct(sshape, F32),
        ),
        in_specs=[VM, VM, VM],
        out_specs=(VM, VM, VM),
        scratch_shapes=[
            pltpu.VMEM((max(5, geo.tensor - 1), rows, width), BF),
            pltpu.VMEM((geo.dp - 1,) + wshape, BF),
            pltpu.VMEM((geo.dp - 1,) + sshape, F32),
            pltpu.VMEM(sshape, F32),
            pltpu.VMEM((geo.tensor - 1,) + sshape, F32),
            pltpu.SemaphoreType.DMA((sems,)), pltpu.SemaphoreType.DMA((sems,))],
        compiler_params=pltpu.CompilerParams(collective_id=4, has_side_effects=True, vmem_limit_bytes=48 * 2**20),
        name="k4",
    )(part, wgrad, small)


PAIR = 2 * HD


def nt(x, w):
    return lax.dot_general(x, w, (((1,), (1,)), ((), ())), preferred_element_type=F32)


def nn(x, w):
    return lax.dot_general(x, w, (((1,), (0,)), ((), ())), preferred_element_type=F32)


def tn(x, w):
    return lax.dot_general(x, w, (((0,), (0,)), ((), ())), preferred_element_type=F32)


def block_bias(seg_col, seg_row, bias, start, rows, keys):
    query = seg_col[start:start + rows, :]
    for first in range(0, keys, rows):
        key = seg_row[:, first:first + rows]
        seen = query == key
        if first + rows > start:
            q_pos = start + lax.broadcasted_iota(jnp.int32, (rows, rows), 0)
            k_pos = first + lax.broadcasted_iota(jnp.int32, (rows, rows), 1)
            seen = seen & (k_pos <= q_pos)
        bias[:, first:first + rows] = jnp.where(seen, 0.0, MASKED).astype(F32)


def one_head(pair, head):
    lane = lax.broadcasted_iota(jnp.int32, pair.shape, 1)
    return jnp.where((lane < HD) if head == 0 else (lane >= HD), pair, jnp.zeros_like(pair))


def attend_block(qkv, bias, att, lse, start, rows):
    keys = start + rows
    width = qkv.shape[2]
    stat_lane = lax.broadcasted_iota(jnp.int32, (rows, 128), 1)
    stats = jnp.zeros((rows, 128), F32)
    for p in range(width // PAIR):
        lanes = slice(p * PAIR, (p + 1) * PAIR)
        query = qkv[0, start:keys, lanes]
        outs = []
        for head in range(2):
            s = nt(one_head(query, head), qkv[1, 0:keys, lanes]) + bias[:, 0:keys]
            top = jnp.max(s, axis=1, keepdims=True)
            e = jnp.exp(s - top)
            total = jnp.sum(e, axis=1, keepdims=True)
            prob = (e * (1.0 / total)).astype(BF)
            outs.append(nn(prob, qkv[2, 0:keys, lanes]))
            stats = jnp.where(stat_lane == 2 * p + head, top + jnp.log(total), stats)
        lane = lax.broadcasted_iota(jnp.int32, outs[0].shape, 1)
        att[start:keys, lanes] = jnp.where(lane < HD, outs[0], outs[1]).astype(BF)
    lse[start:keys, :] = stats


def attend_block_back(qkv, bias, lse, do, dq, dk, dv, start, rows):
    keys = start + rows
    width = qkv.shape[2]
    stat_lane = lax.broadcasted_iota(jnp.int32, (rows, 128), 1)
    stats = lse[start:keys, :]
    for p in range(width // PAIR):
        lanes = slice(p * PAIR, (p + 1) * PAIR)
        query = qkv[0, start:keys, lanes]
        grad = do[start:keys, lanes]
        dqs, dks, dvs = [], [], []
        for head in range(2):
            level = jnp.sum(jnp.where(stat_lane == 2 * p + head, stats, 0.0), axis=1, keepdims=True)
            s = nt(one_head(query, head), qkv[1, 0:keys, lanes]) + bias[:, 0:keys]
            prob = jnp.exp(s - level)
            d_prob = nt(one_head(grad, head), qkv[2, 0:keys, lanes])
            mixed = prob * d_prob
            ds = (mixed - prob * jnp.sum(mixed, axis=1, keepdims=True)).astype(BF)
            dqs.append(nn(ds, qkv[1, 0:keys, lanes]))
            dks.append(tn(ds, query))
            dvs.append(tn(prob.astype(BF), grad))
        lane = lax.broadcasted_iota(jnp.int32, dqs[0].shape, 1)
        dq[start:keys, lanes] = (jnp.where(lane < HD, dqs[0], dqs[1]) * (HD ** -0.5)).astype(dq.dtype)
        lane = lax.broadcasted_iota(jnp.int32, dks[0].shape, 1)
        dk[0:keys, lanes] += jnp.where(lane < HD, dks[0], dks[1])
        dv[0:keys, lanes] += jnp.where(lane < HD, dvs[0], dvs[1])


def attend_body(qkv, seg_col, seg_row, att, lse, bias):
    rows = 256
    for start in range(0, SEQ, rows):
        block_bias(seg_col, seg_row, bias, start, rows, start + rows)
        attend_block(qkv, bias, att, lse, start, rows)


def attend(qkv, seg_col, seg_row):
    return pl.pallas_call(
        attend_body,
        out_shape=(jax.ShapeDtypeStruct(qkv.shape[1:], BF), jax.ShapeDtypeStruct((qkv.shape[1], 128), F32)),
        in_specs=[VM] * 3, out_specs=(VM, VM),
        scratch_shapes=[pltpu.VMEM((256, SEQ), F32)],
        compiler_params=pltpu.CompilerParams(vmem_limit_bytes=40 * 2**20),
        name="attend",
    )(qkv, seg_col, seg_row)


def attend_back_body(qkv, seg_col, seg_row, lse, do, dqkv, bias, dk, dv):
    rows = 256
    dk[...] = jnp.zeros_like(dk)
    dv[...] = jnp.zeros_like(dv)
    for start in range(SEQ - rows, -1, -rows):
        block_bias(seg_col, seg_row, bias, start, rows, start + rows)
        attend_block_back(qkv, bias, lse, do, dqkv.at[0], dk, dv, start, rows)
        dqkv[1, start:start + rows, :] = dk[start:start + rows, :].astype(BF)
        dqkv[2, start:start + rows, :] = dv[start:start + rows, :].astype(BF)


def attend_back(qkv, seg_col, seg_row, lse, do):
    return pl.pallas_call(
        attend_back_body,
        out_shape=jax.ShapeDtypeStruct(qkv.shape, BF),
        in_specs=[VM] * 5, out_specs=VM,
        scratch_shapes=[pltpu.VMEM((256, SEQ), F32), pltpu.VMEM(qkv.shape[1:], F32), pltpu.VMEM(qkv.shape[1:], F32)],
        compiler_params=pltpu.CompilerParams(vmem_limit_bytes=40 * 2**20),
        name="attend_back",
    )(qkv, seg_col, seg_row, lse, do)


def loop_rows(count, tile, body):
    def step(i, carry):
        body(pl.ds(pl.multiple_of(i * tile, tile), tile))
        return carry

    lax.fori_loop(0, count // tile, step, 0)


def sub_rows(start, count, tile, body):
    def step(i, carry):
        body(pl.ds(pl.multiple_of(start + i * tile, tile), tile))
        return carry

    lax.fori_loop(0, count // tile, step, 0)


def mk1_body(geo, x_ref, aw_ref, ow_ref, up_ref, down_ref, gain_ref, bias_ref, seg_col, seg_row,
             n1, qkv, att, lse, wf, sf, total, xf, full,
             rows12, part, land, bias, wsend, dsend, ssend, send, recv, local):
    spot = geo.bind()
    wire = Wire(send, recv)
    size = geo.tensor
    rows = x_ref.shape[0]
    wrows = aw_ref.shape[1]
    mrows = up_ref.shape[0]
    heads = aw_ref.shape[2]

    def xslot(t):
        return xf.at[pl.ds(pl.multiple_of(t * rows, rows), rows)]

    def wslot(d):
        return wf.at[:, pl.ds(pl.multiple_of(d * wrows, wrows), wrows)]

    def block(i):
        return part.at[pl.ds(pl.multiple_of(i * rows, rows), rows)]

    gain_copy = pltpu.make_async_copy(x_ref, xslot(spot.t), local.at[0])
    gain_copy.start()
    span = pl.ds(pl.multiple_of(spot.d * mrows, mrows), mrows)
    up_copy = pltpu.make_async_copy(up_ref, full.at[0, spot.t, span], local.at[1])
    up_copy.start()
    ssend[0:2, :] = gain_ref[...].astype(F32)
    ssend[2:12, :] = bias_ref[...].astype(F32)
    wsend[0:3] = aw_ref[...]
    wsend[3] = ow_ref[...].T
    greet(spot)
    ups = WeightGather(spot, wire, up_ref, full.at[0])
    downs = WeightGather(spot, wire, dsend, full.at[1])
    xs = LineGather(spot, wire, x_ref, xslot)
    ups.line.start()
    small = wire.take(geo.dp - 1)
    big = wire.take(geo.dp - 1)
    for step in range(1, geo.dp):
        wire.start(small + step - 1, ssend, sf.at[spot.d], spot.at_d(ring_next(spot.d, step, geo.dp)))
    for step in range(1, geo.dp):
        wire.start(big + step - 1, wsend, wslot(spot.d), spot.at_d(ring_next(spot.d, step, geo.dp)))
    sf[spot.d] = ssend[...]
    wf[:, pl.ds(pl.multiple_of(spot.d * wrows, wrows), wrows)] = wsend[...]
    dsend[...] = down_ref[...].T
    down_copy = pltpu.make_async_copy(dsend, full.at[1, spot.t, span], local.at[2])
    down_copy.start()
    ups.line.forward()
    xs.start()
    up_copy.wait()
    ups.line.finish()
    ups.first()
    for step in range(1, geo.dp):
        source = ring_prev(spot.d, step, geo.dp)
        wire.landed(small + step - 1, sf.at[source], spot.at_d(source))
    piece = ssend.shape[1]
    for d in range(geo.dp):
        rows12[:, d * piece:(d + 1) * piece] = sf[d]
    for step in range(1, geo.dp):
        source = ring_prev(spot.d, step, geo.dp)
        wire.landed(big + step - 1, wslot(source), spot.at_d(source))
    gain_copy.wait()
    column = pl.ds(pl.multiple_of(spot.t * heads, 128), heads)

    def project(t):
        def norm(r):
            n1[r] = layer_norm(xf[r].astype(F32), rows12[0:1, :], rows12[2:3, :]).astype(BF)

        sub_rows(pl.multiple_of(t * rows, rows), rows, min(64, rows), norm)
        r = pl.ds(pl.multiple_of(t * rows, rows), rows)
        normed = n1[r]
        qkv[0, r] = ((nn(normed, wf[0]) + rows12[3:4, column]).astype(BF).astype(F32) * HD ** -0.5).astype(BF)
        qkv[1, r] = nn(normed, wf[1]).astype(BF)
        qkv[2, r] = (nn(normed, wf[2]) + rows12[4:5, column]).astype(BF)

    project(spot.t)
    ups.second()
    xs.forward()
    xs.finish()
    downs.line.start()

    def other(step, carry):
        project(ring_next(spot.t, step, size))
        return carry

    lax.fori_loop(1, size, other, 0)
    ups.third()
    scatter = LineScatter(spot, wire, block, lambda k: land.at[k], lambda dst, src: add_tiled(dst, src, 64))
    qrows = min(256, SEQ)
    for start in range(0, SEQ, qrows):
        block_bias(seg_col, seg_row, bias, start, qrows, start + qrows)
        attend_block(qkv, bias, att, lse, start, qrows)
        part[start:start + qrows, :] = nt(att[start:start + qrows, :], wf[3]).astype(BF)
        if scatter.line:
            scatter.start_block(start // rows)
        if start == 0:
            downs.line.forward()
    if not scatter.line:
        scatter.start()
    down_copy.wait()
    downs.line.finish()
    downs.first()
    scatter.forward()
    downs.second()
    mine = block(spot.t)

    def set_total(r):
        total[r] = mine[r].astype(F32)

    loop_rows(rows, min(64, rows), set_total)
    scatter.finish(lambda ref: add_tiled(total, ref, 64))
    ups.fourth()
    downs.third()
    downs.fourth()
    wire.drain()


def mk1(geo, x, aw, ow, up, down, gains, biases, seg_col, seg_row):
    rows, width = x.shape
    wrows, heads = aw.shape[1:]
    size = geo.tensor
    sems = 12 + 2 * size + 2 * geo.dp + 2 * gather_sems(geo)
    seq = size * rows
    return pl.pallas_call(
        functools.partial(mk1_body, geo),
        out_shape=(
            jax.ShapeDtypeStruct((seq, width), BF),
            jax.ShapeDtypeStruct((3, seq, heads), BF),
            jax.ShapeDtypeStruct((seq, heads), BF),
            jax.ShapeDtypeStruct((seq, 128), F32),
            jax.ShapeDtypeStruct((4, width, heads), BF),
            jax.ShapeDtypeStruct((geo.dp, 12, wrows), F32),
            jax.ShapeDtypeStruct((rows, width), F32),
            jax.ShapeDtypeStruct((seq, width), BF),
            jax.ShapeDtypeStruct((2, size, width, up.shape[1]), BF),
        ),
        in_specs=[ANY, VM, VM, ANY, VM, VM, VM, VM, VM],
        out_specs=(VM,) * 8 + (ANY,),
        scratch_shapes=[
            pltpu.VMEM((12, width), F32),
            pltpu.VMEM((seq, width), BF),
            pltpu.VMEM((max(5, size - 1), rows, width), BF),
            pltpu.VMEM((min(256, SEQ), SEQ), F32),
            pltpu.VMEM((4, wrows, heads), BF),
            pltpu.VMEM(up.shape, BF),
            pltpu.VMEM((12, wrows), F32),
            pltpu.SemaphoreType.DMA((sems,)), pltpu.SemaphoreType.DMA((sems,)), pltpu.SemaphoreType.DMA((3,))],
        compiler_params=pltpu.CompilerParams(collective_id=1, has_side_effects=True, vmem_limit_bytes=50 * 2**20),
        name="mk1",
    )(x, aw, ow, up, down, gains, biases, seg_col, seg_row)


def dot_nt(x, w):
    return lax.dot_general(x, w, (((1,), (1,)), ((), ())), preferred_element_type=F32)


def dot_tn(x, w):
    return lax.dot_general(x, w, (((0,), (0,)), ((), ())), preferred_element_type=F32)


def per_device(geo, activations, segments, attn_weight, out_weight, up_weight, down_weight, norm_gains, bias_rows, cotangent):
    tensor_rank = lax.axis_index("tensor")
    width = activations.shape[1]
    head_width = attn_weight.shape[3]
    seg_col, seg_row = segments[:, None], segments[None, :]
    normed_full, project, attended, log_total, w_full, small_full, attn_sum, x_full, m_full = mk1(
        geo, activations, attn_weight[0], out_weight[0], up_weight[0], down_weight[0], norm_gains[0], bias_rows[0], seg_col, seg_row)
    rows12 = small_full.transpose(1, 0, 2).reshape(12, width)
    gains, biases = rows12[:2], rows12[2:]
    column = tensor_rank * head_width

    residual = activations.astype(F32)
    middle = residual + (attn_sum + biases[3])
    unit_two, scale_two = norm_stats(middle)
    normed_two = (unit_two * gains[1] + biases[4]).astype(BF)
    up_full, down_full = m_full[0], m_full[1]
    tensor = up_full.shape[0]
    unit_width = up_full.shape[2]
    up_bias = biases[6:10].reshape(1, -1)
    hidden = jnp.concatenate([jnp.dot(normed_two, up_full[s], preferred_element_type=F32) for s in range(tensor)], axis=1) + up_bias
    active = gelu_tanh(hidden).astype(BF)
    branch = cotangent.astype(BF)
    ff = sum(dot_nt(active[:, s * unit_width:(s + 1) * unit_width], down_full[s]) for s in range(tensor))
    output = middle + (ff + biases[5])
    active_grad = jnp.concatenate([jnp.dot(branch, down_full[s], preferred_element_type=F32) for s in range(tensor)], axis=1)
    hidden_grad = jax.vjp(gelu_tanh, hidden)[1](active_grad)[0].astype(BF)
    up_bias_grad = jnp.sum(hidden_grad.astype(F32), axis=0).reshape(4, width)
    grads = jnp.stack([
        jnp.stack([dot_tn(normed_two, hidden_grad[:, s * unit_width:(s + 1) * unit_width]).astype(BF) for s in range(tensor)]),
        jnp.stack([dot_tn(branch, active[:, s * unit_width:(s + 1) * unit_width]).astype(BF) for s in range(tensor)]),
    ])
    normed_two_grad = sum(dot_nt(hidden_grad[:, s * unit_width:(s + 1) * unit_width], up_full[s]) for s in range(tensor))
    middle_grad = cotangent + norm_back(normed_two_grad, unit_two, scale_two, gains[1])
    attn_branch = middle_grad.astype(BF)
    ga_full, mlp_grads = k3(geo, attn_branch, grads)

    attended_grad = jnp.dot(ga_full, w_full[3], preferred_element_type=F32).astype(BF)
    project_grad = attend_back(project, seg_col, seg_row, log_total, attended_grad)
    dn_part = sum(dot_nt(project_grad[j], w_full[j]) for j in range(3))
    w_grads = jnp.stack([dot_tn(normed_full, project_grad[j]).astype(BF) for j in range(3)] + [dot_tn(ga_full, attended).astype(BF)])

    query_bias_grad = jnp.sum(project_grad[0].astype(F32), axis=0)
    value_bias_grad = jnp.sum(project_grad[2].astype(F32), axis=0)
    zeros = jnp.zeros((width,), F32)
    dn_total, w_out, small_one = k4(geo, dn_part.astype(BF), w_grads, split_dp(geo, jnp.stack([
        jnp.sum(dn_part * norm_stats(x_full.astype(F32))[0], axis=0),
        jnp.sum(normed_two_grad * unit_two, axis=0),
        jnp.sum(dn_part, axis=0),
        lax.dynamic_update_slice_in_dim(zeros, query_bias_grad, column, 0),
        lax.dynamic_update_slice_in_dim(zeros, value_bias_grad, column, 0),
        jnp.sum(attn_branch.astype(F32), axis=0),
        jnp.sum(normed_two_grad, axis=0),
        jnp.sum(branch.astype(F32), axis=0),
        up_bias_grad[0], up_bias_grad[1], up_bias_grad[2], up_bias_grad[3],
    ])))
    unit_one, scale_one = norm_stats(residual)
    input_grad = middle_grad + norm_back(dn_total, unit_one, scale_one, gains[0])
    return (
        output, input_grad, w_out[None, :3], w_out[3].T[None], mlp_grads[0][None], mlp_grads[1].T[None],
        small_one[None, :2], small_one[None, 2:12])


def split_dp(geo, rows):
    n, width = rows.shape
    pad = -n % 8
    rows = jnp.pad(rows, ((0, pad), (0, 0)))
    return rows.reshape(n + pad, geo.dp, width // geo.dp).transpose(1, 0, 2)


def solution(mesh):
    geo = Geometry(mesh.shape["dp"], mesh.shape["tensor"])
    return jax.shard_map(
        functools.partial(per_device, geo),
        mesh=mesh,
        in_specs=(
            P(("dp", "tensor"), None),
            P("dp"),
            P(None, None, "dp", "tensor"),
            P(None, "tensor", "dp"),
            P(None, "dp", "tensor"),
            P(None, "tensor", "dp"),
            P(None, None, "dp"),
            P(None, None, "dp"),
            P(("dp", "tensor"), None),
        ),
        out_specs=(
            P(("dp", "tensor"), None),
            P(("dp", "tensor"), None),
            P(None, None, "dp", "tensor"),
            P(None, "tensor", "dp"),
            P(None, "dp", "tensor"),
            P(None, "tensor", "dp"),
            P(None, None, "dp"),
            P(None, None, "dp"),
        ),
        check_vma=False,
    )
```

profile of v0, /device:TPU:0, one launch (start us, length us, event | category | flops | bytes accessed | tf_op | source)
XLA Modules:
  0.0 378.3 jit_solution(6435081401034705163)
XLA Ops:
  8.3 133.6 %mk1.1 = (bf16[1024,1024]{1,0:T(8,128)(2,1)}, bf16[3,1024,256]{2,1,0:T(8,128)(2,1)}, bf16[1024,256]{1,0:T(8,128)(2,1)S(1)}, f32[1024,128]{1,0:T(8,128)S(1)}, bf1...) custom-call(bf16[256,1024]{1,0:T(8,128)(2,1)S(1)} %copy-done, ...), custom_call_target="tpu_custom_call" | custom-call | tf_op jit(solution)/shard_map/mk1/pallas_call | solution.py:869
  143.1 2.7 fusion.30
  145.8 3.0 fusion.34
  148.8 2.3 fusion.38
  155.3 4.0 %convert_reduce_fusion.1 = (f32[4096]{0:T(1024)S(1)}, bf16[256,4096]{1,0:T(8,128)(2,1)S(1)}, bf16[256,4096]{1,0:T(8,128)(2,1)S(1)}) fusion(f32[4096]{0:T(1024)S(1)} %bitcast.229, f32[256,1024]{1,0:T(8,128)S(1)} %fusion.30, f32[256,1024]{1,0:T(8,128)S(1)} %fusion.34, f32[256,1024]{1,0:T(8,128)S(1)} %fusion.38, f32[256,1024]{1,0:T(8,128)S(1)} %fusion.42, ...), kind=kLoop, calls=%fused_computation.21 | loop fusion | flops 32501760 | bytes 12615680 | tf_op jit(solution)/shard_map/reduce_sum | solution.py:932
  159.2 2.3 fusion.14
  161.6 2.3 fusion.18
  163.9 2.3 fusion.22
  166.3 3.5 fusion.93
  169.8 2.4 fusion.28
  172.2 2.4 fusion.32
  174.6 2.4 fusion.36
  177.0 2.9 multiply_reduce_fusion
  179.8 1.2 convert_reduce_fusion.4
  185.7 1.3 maximum_bitcast_fusion.1
  190.1 1.1 maximum_bitcast_fusion
  191.2 6.8 %pad_maximum_fusion.g_ref = bf16[2,4,1024,1024]{3,2,1,0:T(8,128)(2,1)} fusion(bf16[1,4,1024,1024]{3,2,1,0:T(8,128)(2,1)S(1)} %maximum_bitcast_fusion.1, bf16[1,4,1024,1024]{3,2,1,0:T(8,128)(2,1)S(1)} %maximum_bitcast_fusion), kind=kLoop, calls=%fused_computation | loop fusion | flops 8388608 | bytes 33554432 | tf_op jit(solution)/shard_map/stack | solution.py:933
  198.0 109.7 %k3.1 = (bf16[1024,1024]{1,0:T(8,128)(2,1)}, f32[2,128,1024]{2,1,0:T(8,128)}) custom-call(bf16[256,1024]{1,0:T(8,128)(2,1)} %get-tuple-element.67.ga_ref, bf16[2,4,1024,1024]{3,2,1,0:T(8,128)(2,1)} %pad_maximum_fusion.g_ref), custom_call_target="tpu_custom_call" | custom-call | tf_op jit(solution)/shard_map/k3/pallas_call | solution.py:503
  307.8 2.5 convolution_convert_fusion.4.do
  310.3 11.2 %attend_back.1 = bf16[3,1024,256]{2,1,0:T(8,128)(2,1)S(1)} custom-call(bf16[3,1024,256]{2,1,0:T(8,128)(2,1)S(1)} %copy-done.3, s32[1024,1]{1,0:T(8,128)S(1)} %copy.28.seg_col, s32[1,1024]{1,0:T(1,128)S(1)} %bitcast.224, f32[1024,128]{1,0:T(8,128)S(1)} %get-tuple-element.26.lse, bf16[1024,256]{1,0:T(8,128)(2,1)S(1)} %convolution_convert_fusion.4.do), custom_call_target="tpu_custom_call" | custom-call | tf_op jit(solution)/shard_map/attend_back/pallas_call | solution.py:722
  323.2 2.8 fusion.135
  330.6 1.6 copy-done.2
  332.2 39.5 %k4.1 = (f32[256,1024]{1,0:T(8,128)S(1)}, f32[4,128,256]{2,1,0:T(8,128)S(1)}, f32[16,128]{1,0:T(8,128)S(1)}) custom-call(bf16[1024,1024]{1,0:T(8,128)(2,1)S(1)} %copy-done.2, bf16[4,1024,256]{2,1,0:T(8,128)(2,1)S(1)} %pad_maximum_fusion.2.w_ref, f32[8,16,128]{2,1,0:T(8,128)S(1)} %bitcast_bitcast_fusion.s_ref), custom_call_target="tpu_custom_call" | custom-call | tf_op jit(solution)/shard_map/k4/pallas_call | solution.py:590
  372.1 1.4 fusion.107
  (94 shorter events, 31.7 us)
Async XLA Ops:
  1.5 1.0 copy-start
  2.6 0.9 copy-start.4
  3.5 0.9 copy-start.5
  4.5 0.9 copy-start.6
  5.4 0.8 copy-start.7
  6.3 0.7 copy-start.8
  6.9 0.7 copy-start.10
  7.6 0.7 copy-start.11
  142.1 9.0 %copy-start.15 = (bf16[2,4,1024,1024]{3,2,1,0:T(8,128)(2,1)S(1)}, bf16[2,4,1024,1024]{3,2,1,0:T(8,128)(2,1)}, u32[]{:S(2)}) copy-start(bf16[2,4,1024,1024]{3,2,1,0:T(8,128)(2,1)} %get-tuple-element.24) | copy-start | bytes 50331652
  151.1 1.2 copy-start.13
  179.8 1.8 copy-start.12
  307.7 2.5 copy-start.3
  307.7 2.5 copy-start.9
  310.3 11.2 %copy-start.14 = (bf16[4,1024,256]{2,1,0:T(8,128)(2,1)S(1)}, bf16[4,1024,256]{2,1,0:T(8,128)(2,1)}, u32[]{:S(2)}) copy-start(bf16[4,1024,256]{2,1,0:T(8,128)(2,1)} %get-tuple-element.28) | copy-start | bytes 6291460
  323.2 2.8 copy-start.18
  326.0 1.6 copy-start.17
  330.6 1.6 copy-start.2
  332.2 39.5 %copy-start.1 = (bf16[256,1024]{1,0:T(8,128)(2,1)S(1)}, bf16[256,1024]{1,0:T(8,128)(2,1)}, u32[]{:S(2)}) copy-start(bf16[256,1024]{1,0:T(8,128)(2,1)} %x_ref.1) | copy-start | bytes 1572868
  372.1 2.9 copy-start.16
where the time goes:
time: 386 us; the launch traced here: 378 us
  Pallas kernels  294 us (76%)
  matrix products  48.2 us (12%)
  other arithmetic  18.9 us (5%)
  local copies, waits for them, and re-layouts  15.9 us (4%)
    pallas_call x1, Pallas kernels, mk1(): pl.pallas_call(functools.partial(mk1_body, geo), out_shape=(jax.ShapeDtyp...  134 us
    pallas_call x1, Pallas kernels, k3(): pl.pallas_call(functools.partial(k3_body, geo), out_shape=(jax.ShapeDtype...  110 us
    pallas_call x1, Pallas kernels, k4(): pl.pallas_call(functools.partial(k4_body, geo), out_shape=(jax.ShapeDtype...  39.5 us
    dot_general x11, matrix products, dot_nt(): lax.dot_general(x, w, (((1,), (1,)), ((), ())), preferred_element_type=F32)  25 us
    unnamed x41, local copies, waits for them, and re-layouts  12.6 us
    pallas_call x1, Pallas kernels, attend_back(): pl.pallas_call(attend_back_body, out_shape=jax.ShapeDtypeStruct(qkv.shape...  11.2 us
    another operation x3, other arithmetic, per_device(): jnp.stack([jnp.stack([dot_tn(normed_two, hidden_grad[:, s * unit_width:(s...  9.22 us
    dot_general x12, matrix products, dot_tn(): lax.dot_general(x, w, (((0,), (0,)), ((), ())), preferred_element_type=F32)  9.12 us

commit v1 on v0

v1 whole, which is shorter than its diff:
```python
import functools

import jax
import jax.numpy as jnp
from jax import lax
from jax.experimental import pallas as pl
from jax.experimental.pallas import tpu as pltpu
from jax.sharding import PartitionSpec as P

HD = 64
SEQ = 1024
EPSILON = 1e-05
MASKED = -1e30
MESH_ID = pl.DeviceIdType.MESH
BF = jnp.bfloat16
F32 = jnp.float32
ANY = pl.BlockSpec(memory_space=pl.ANY)
VM = pl.BlockSpec(memory_space=pltpu.VMEM)


def layer_norm(values, gain_row, shift_row):
    center = values - jnp.mean(values, axis=-1, keepdims=True)
    spread = jnp.mean(center * center, axis=-1, keepdims=True)
    return center * lax.rsqrt(spread + EPSILON) * gain_row + shift_row


def norm_stats(values):
    center = values - jnp.mean(values, axis=-1, keepdims=True)
    spread = jnp.mean(center * center, axis=-1, keepdims=True)
    scale = lax.rsqrt(spread + EPSILON)
    return center * scale, scale


def norm_back(grad, unit, scale, gain_row):
    u = grad * gain_row
    mean_u = jnp.mean(u, axis=-1, keepdims=True)
    mean_ux = jnp.mean(u * unit, axis=-1, keepdims=True)
    return scale * (u - mean_u - unit * mean_ux)


def gelu_tanh(values):
    return jax.nn.gelu(values, approximate=True)


class Geometry:
    def __init__(self, dp, tensor):
        self.dp, self.tensor = dp, tensor
        self.c_size = 2
        rest = dp // 2
        self.a_size = 1
        while self.a_size * self.a_size < rest:
            self.a_size *= 2
        self.b_size = rest // self.a_size
        assert self.a_size * self.b_size * 2 == dp

    def bind(self):
        spot = Spot()
        spot.geo = self
        spot.d = lax.axis_index("dp")
        spot.t = lax.axis_index("tensor")
        spot.c = lax.rem(spot.d, 2)
        half = lax.div(spot.d, 2)
        spot.a = lax.rem(half, self.a_size)
        spot.b = lax.div(half, self.a_size)
        return spot


class Spot:
    def rank(self, b, a, c):
        return (b * self.geo.a_size + a) * 2 + c

    def at_t(self, t):
        return (self.d, t)

    def at_d(self, d):
        return (d, self.t)


def ring_next(rank, step, size):
    return lax.rem(rank + step, size)


def ring_prev(rank, step, size):
    return lax.rem(rank + size - step, size)


class Wire:
    def __init__(self, send, recv):
        self.send_sems, self.recv_sems = send, recv
        self.count = 0
        self.pending = []

    def take(self, n):
        first = self.count
        self.count += n
        return first

    def copy(self, i, src, dst, device):
        return pltpu.make_async_remote_copy(
            src_ref=src, dst_ref=dst, send_sem=self.send_sems.at[i], recv_sem=self.recv_sems.at[i],
            device_id=device, device_id_type=MESH_ID)

    def plan(self, i, src, dst, device, when=None):
        return self.copy(i, src, dst, device), when

    def go(self, planned):
        copy, when = planned
        if when is None:
            copy.start()
        else:
            pl.when(when)(copy.start)
        self.pending.append(planned)

    def start(self, i, src, dst, device, when=None):
        self.go(self.plan(i, src, dst, device, when))

    def landed(self, i, dst, device, when=None):
        copy = self.copy(i, dst, dst, device)
        if when is None:
            copy.wait_recv()
        else:
            pl.when(when)(copy.wait_recv)

    def drain(self):
        for copy, when in self.pending:
            if when is None:
                copy.wait_send()
            else:
                pl.when(when)(copy.wait_send)
        self.pending = []


def greet(spot, with_dp=True):
    geo = spot.geo
    barrier = pltpu.get_barrier_semaphore()
    total = 0
    for step in range(1, geo.tensor):
        pl.semaphore_signal(barrier, inc=1, device_id=spot.at_t(ring_next(spot.t, step, geo.tensor)), device_id_type=MESH_ID)
        total += 1
    for step in range(1, geo.dp):
        pl.semaphore_signal(barrier, inc=1, device_id=spot.at_d(ring_next(spot.d, step, geo.dp)), device_id_type=MESH_ID)
        total += 1
    pl.semaphore_wait(barrier, total)


class LineGather:
    def __init__(self, spot, wire, src, slot):
        self.spot, self.wire, self.slot = spot, wire, slot
        self.size = spot.geo.tensor
        self.line = self.size == 4
        self.first = wire.take(6 if self.line else self.size - 1)
        t = spot.t
        self.sends, self.passes = [], []
        if not self.line:
            for step in range(1, self.size):
                self.sends.append(wire.plan(self.first + step - 1, src, slot(t), spot.at_t(ring_next(t, step, self.size))))
            return
        for k, delta in enumerate((2, -2, 1, -1)):
            to = t + delta
            self.sends.append(wire.plan(self.first + k, src, slot(t), spot.at_t(to), when=(to >= 0) & (to < self.size)))
        for k, delta in enumerate((-2, 2)):
            at_work = t == (2, 1)[k]
            piece = slot(t + delta)
            self.passes.append((at_work, t + delta, wire.plan(self.first + 4 + k, piece, piece, spot.at_t(t + (1, -1)[k]), when=at_work)))

    def start(self):
        for planned in self.sends:
            self.wire.go(planned)

    def forward(self):
        for k, (at_work, source, planned) in enumerate(self.passes):
            self.wire.landed(self.first + k, self.slot(source), self.spot.at_t(source), when=at_work)
            self.wire.go(planned)

    def finish(self):
        spot, t = self.spot, self.spot.t
        if not self.line:
            for step in range(1, self.size):
                source = ring_prev(t, step, self.size)
                self.wire.landed(self.first + step - 1, self.slot(source), spot.at_t(source))
            return
        self.wire.landed(self.first + 0, self.slot(t - 2), spot.at_t(t - 2), when=t == 3)
        self.wire.landed(self.first + 1, self.slot(t + 2), spot.at_t(t + 2), when=t == 0)
        self.wire.landed(self.first + 2, self.slot(t - 1), spot.at_t(t - 1), when=t >= 1)
        self.wire.landed(self.first + 3, self.slot(t + 1), spot.at_t(t + 1), when=t <= 2)
        self.wire.landed(self.first + 4, self.slot(t - 3), spot.at_t(t - 1), when=t == 3)
        self.wire.landed(self.first + 5, self.slot(t + 3), spot.at_t(t + 1), when=t == 0)


class LineScatter:
    def __init__(self, spot, wire, part, land, add):
        self.spot, self.wire, self.part, self.land, self.add = spot, wire, part, land, add
        self.size = spot.geo.tensor
        self.line = self.size == 4
        self.first = wire.take(6 if self.line else self.size - 1)

    def start(self):
        spot, t = self.spot, self.spot.t
        if not self.line:
            for step in range(1, self.size):
                to = ring_next(t, step, self.size)
                self.wire.start(self.first + step - 1, self.part(to), self.land(step - 1), spot.at_t(to))
            return
        self.wire.start(self.first + 4, self.part(3), self.land(4), spot.at_t(1), when=t == 0)
        self.wire.start(self.first + 5, self.part(0), self.land(4), spot.at_t(2), when=t == 3)
        self.wire.start(self.first + 0, self.part(2), self.land(0), spot.at_t(2), when=t == 0)
        self.wire.start(self.first + 1, self.part(1), self.land(1), spot.at_t(1), when=t == 3)
        self.wire.start(self.first + 2, self.part(jnp.minimum(t + 1, 3)), self.land(2), spot.at_t(t + 1), when=t <= 2)
        self.wire.start(self.first + 3, self.part(jnp.maximum(t - 1, 0)), self.land(3), spot.at_t(t - 1), when=t >= 1)

    def start_block(self, i):
        spot, t = self.spot, self.spot.t
        if i == 3:
            self.wire.start(self.first + 4, self.part(3), self.land(4), spot.at_t(1), when=t == 0)
        if i == 0:
            self.wire.start(self.first + 5, self.part(0), self.land(4), spot.at_t(2), when=t == 3)
        if i == 2:
            self.wire.start(self.first + 0, self.part(2), self.land(0), spot.at_t(2), when=t == 0)
        if i == 1:
            self.wire.start(self.first + 1, self.part(1), self.land(1), spot.at_t(1), when=t == 3)
        if i >= 1:
            self.wire.start(self.first + 2, self.part(i), self.land(2), spot.at_t(i), when=t == i - 1)
        if i <= 2:
            self.wire.start(self.first + 3, self.part(i), self.land(3), spot.at_t(i), when=t == i + 1)

    def forward(self):
        if not self.line:
            return
        spot, t = self.spot, self.spot.t

        @pl.when(t == 1)
        def _():
            self.wire.landed(self.first + 4, self.land(4), spot.at_t(0))
            self.add(self.part(3), self.land(4))

        @pl.when(t == 2)
        def _():
            self.wire.landed(self.first + 5, self.land(4), spot.at_t(3))
            self.add(self.part(0), self.land(4))

        self.wire.start(self.first + 0, self.part(3), self.land(0), spot.at_t(3), when=t == 1)
        self.wire.start(self.first + 1, self.part(0), self.land(1), spot.at_t(0), when=t == 2)

    def finish(self, total):
        spot, t = self.spot, self.spot.t
        if not self.line:
            for step in range(1, self.size):
                self.wire.landed(self.first + step - 1, self.land(step - 1), spot.at_t(ring_prev(t, step, self.size)))
                total(self.land(step - 1))
            return
        for k, delta in enumerate((2, -2, 1, -1)):
            source = t - delta

            @pl.when((source >= 0) & (source < self.size))
            def _():
                self.wire.landed(self.first + k, self.land(k), spot.at_t(source))
                total(self.land(k))


def add_tiled(dst, src, tile):
    count = dst.shape[0] // tile

    def step(i, carry):
        rows = pl.ds(pl.multiple_of(i * tile, tile), tile)
        dst[rows] = (dst[rows].astype(F32) + src[rows].astype(F32)).astype(dst.dtype)
        return carry

    lax.fori_loop(0, count, step, 0)


class WeightGather:
    def __init__(self, spot, wire, rows, full):
        geo = spot.geo
        self.spot, self.wire, self.full, self.rows = spot, wire, full, rows
        self.slots = full.shape[0]
        self.half = self.slots // 2
        self.one_a = wire.take(geo.a_size - 1)
        self.one_b = wire.take(geo.b_size - 1)
        self.two_a = wire.take((geo.b_size - 1) * geo.a_size)
        self.two_b = wire.take((geo.a_size - 1) * geo.b_size)
        self.last = wire.take(geo.a_size * geo.b_size)

    def span(self, d):
        return pl.ds(pl.multiple_of(d * self.rows, self.rows), self.rows)

    def low(self, d):
        return self.full.at[pl.ds(0, self.half), self.span(d)]

    def high(self, d):
        return self.full.at[pl.ds(self.half, self.slots - self.half), self.span(d)]

    def both(self, d):
        return self.full.at[:, self.span(d)]

    def first(self):
        spot, geo = self.spot, self.spot.geo
        mine = spot.d
        for j in range(1, geo.a_size):
            to = spot.rank(spot.b, ring_next(spot.a, j, geo.a_size), spot.c)
            self.wire.start(self.one_a + j - 1, self.low(mine), self.low(mine), spot.at_d(to))
        for j in range(1, geo.b_size):
            to = spot.rank(ring_next(spot.b, j, geo.b_size), spot.a, spot.c)
            self.wire.start(self.one_b + j - 1, self.high(mine), self.high(mine), spot.at_d(to))
        sibling = spot.rank(spot.b, spot.a, 1 - spot.c)
        self.wire.start(self.last, self.both(mine), self.both(mine), spot.at_d(sibling))

    def second(self):
        spot, geo = self.spot, self.spot.geo
        for i in range(geo.a_size):
            held = spot.rank(spot.b, ring_prev(spot.a, i, geo.a_size), spot.c)
            if i:
                self.wire.landed(self.one_a + i - 1, self.low(held), spot.at_d(held))
            for j in range(1, geo.b_size):
                to = spot.rank(ring_next(spot.b, j, geo.b_size), spot.a, spot.c)
                self.wire.start(self.two_a + (j - 1) * geo.a_size + i, self.low(held), self.low(held), spot.at_d(to))
        for i in range(geo.b_size):
            held = spot.rank(ring_prev(spot.b, i, geo.b_size), spot.a, spot.c)
            if i:
                self.wire.landed(self.one_b + i - 1, self.high(held), spot.at_d(held))
            for j in range(1, geo.a_size):
                to = spot.rank(spot.b, ring_next(spot.a, j, geo.a_size), spot.c)
                self.wire.start(self.two_b + (j - 1) * geo.b_size + i, self.high(held), self.high(held), spot.at_d(to))

    def third(self):
        spot, geo = self.spot, self.spot.geo
        for j in range(1, geo.b_size):
            for i in range(geo.a_size):
                held = spot.rank(ring_prev(spot.b, j, geo.b_size), ring_prev(spot.a, i, geo.a_size), spot.c)
                source = spot.rank(ring_prev(spot.b, j, geo.b_size), spot.a, spot.c)
                self.wire.landed(self.two_a + (j - 1) * geo.a_size + i, self.low(held), spot.at_d(source))
        for j in range(1, geo.a_size):
            for i in range(geo.b_size):
                held = spot.rank(ring_prev(spot.b, i, geo.b_size), ring_prev(spot.a, j, geo.a_size), spot.c)
                source = spot.rank(spot.b, ring_prev(spot.a, j, geo.a_size), spot.c)
                self.wire.landed(self.two_b + (j - 1) * geo.b_size + i, self.high(held), spot.at_d(source))
        sibling = spot.rank(spot.b, spot.a, 1 - spot.c)
        for j in range(geo.b_size):
            for i in range(geo.a_size):
                if i or j:
                    held = spot.rank(ring_prev(spot.b, j, geo.b_size), ring_prev(spot.a, i, geo.a_size), spot.c)
                    self.wire.start(self.last + j * geo.a_size + i, self.both(held), self.both(held), spot.at_d(sibling))

    def fourth(self):
        spot, geo = self.spot, self.spot.geo
        sibling = spot.rank(spot.b, spot.a, 1 - spot.c)
        for j in range(geo.b_size):
            for i in range(geo.a_size):
                held = spot.rank(ring_prev(spot.b, j, geo.b_size), ring_prev(spot.a, i, geo.a_size), 1 - spot.c)
                self.wire.landed(self.last + j * geo.a_size + i, self.both(held), spot.at_d(sibling))


def gather_sems(geo):
    return geo.a_size + geo.b_size + 3 * geo.a_size * geo.b_size


class WeightScatter:
    def __init__(self, spot, wire, held, one_a, one_b, two_a, two_b):
        geo = spot.geo
        self.spot, self.wire, self.held = spot, wire, held
        self.one_a_buf, self.one_b_buf, self.two_a_buf, self.two_b_buf = one_a, one_b, two_a, two_b
        self.slots, self.rows = held.shape[2], held.shape[3]
        self.half = self.slots // 2
        self.one_a = wire.take(geo.a_size - 1)
        self.one_b = wire.take(geo.b_size - 1)
        self.two_a = wire.take(geo.b_size - 1)
        self.two_b = wire.take(geo.a_size - 1)
        low, high = pl.ds(0, self.half), pl.ds(self.half, self.half)
        self.sends = []
        for j in range(1, geo.a_size):
            a = ring_next(spot.a, j, geo.a_size)
            self.sends.append(wire.plan(self.one_a + j - 1, held.at[:, a, low], one_a.at[j - 1], spot.at_d(spot.rank(spot.b, a, spot.c))))
        for j in range(1, geo.b_size):
            b = ring_next(spot.b, j, geo.b_size)
            self.sends.append(wire.plan(self.one_b + j - 1, held.at[b, :, high], one_b.at[j - 1], spot.at_d(spot.rank(b, spot.a, spot.c))))

    def add(self, dst, src):
        tile = min(64, self.rows)
        per = self.rows // tile

        def step(i, carry):
            rows = pl.ds(pl.multiple_of(lax.rem(i, per) * tile, tile), tile)
            j = lax.div(i, per)
            dst[j, rows] = (dst[j, rows].astype(F32) + src[j, rows].astype(F32)).astype(dst.dtype)
            return carry

        lax.fori_loop(0, dst.shape[0] * per, step, 0)

    def first(self):
        for planned in self.sends:
            self.wire.go(planned)

    def second(self):
        spot, geo = self.spot, self.spot.geo
        low, high = pl.ds(0, self.half), pl.ds(self.half, self.half)
        for j in range(1, geo.a_size):
            self.wire.landed(self.one_a + j - 1, self.one_a_buf.at[j - 1], spot.at_d(spot.rank(spot.b, ring_prev(spot.a, j, geo.a_size), spot.c)))
            for b in range(geo.b_size):
                self.add(self.held.at[b, spot.a, low], self.one_a_buf.at[j - 1, b])
        for j in range(1, geo.b_size):
            b = ring_next(spot.b, j, geo.b_size)
            self.wire.start(self.two_a + j - 1, self.held.at[b, spot.a, low], self.two_a_buf.at[j - 1], spot.at_d(spot.rank(b, spot.a, spot.c)))
        for j in range(1, geo.b_size):
            self.wire.landed(self.one_b + j - 1, self.one_b_buf.at[j - 1], spot.at_d(spot.rank(ring_prev(spot.b, j, geo.b_size), spot.a, spot.c)))
            for a in range(geo.a_size):
                self.add(self.held.at[spot.b, a, high], self.one_b_buf.at[j - 1, a])
        for j in range(1, geo.a_size):
            a = ring_next(spot.a, j, geo.a_size)
            self.wire.start(self.two_b + j - 1, self.held.at[spot.b, a, high], self.two_b_buf.at[j - 1], spot.at_d(spot.rank(spot.b, a, spot.c)))

    def third(self):
        spot, geo = self.spot, self.spot.geo
        low, high = pl.ds(0, self.half), pl.ds(self.half, self.half)
        for j in range(1, geo.b_size):
            self.wire.landed(self.two_a + j - 1, self.two_a_buf.at[j - 1], spot.at_d(spot.rank(ring_prev(spot.b, j, geo.b_size), spot.a, spot.c)))
            self.add(self.held.at[spot.b, spot.a, low], self.two_a_buf.at[j - 1])
        for j in range(1, geo.a_size):
            self.wire.landed(self.two_b + j - 1, self.two_b_buf.at[j - 1], spot.at_d(spot.rank(spot.b, ring_prev(spot.a, j, geo.a_size), spot.c)))
            self.add(self.held.at[spot.b, spot.a, high], self.two_b_buf.at[j - 1])


def scatter_sems(geo):
    return 2 * geo.a_size + 2 * geo.b_size


def scatter_bufs(geo, n, slots, rows, width):
    a, b, half = geo.a_size, geo.b_size, slots // 2
    return [
        pltpu.VMEM((n, b, a, slots, rows, width), BF),
        pltpu.VMEM((n, a - 1, b, half, rows, width), BF),
        pltpu.VMEM((n, b - 1, a, half, rows, width), BF),
        pltpu.VMEM((n, b - 1, half, rows, width), BF),
        pltpu.VMEM((n, a - 1, half, rows, width), BF),
    ]


def loop_rows(count, tile, body, start=0):
    def step(i, carry):
        body(pl.ds(pl.multiple_of(start + i * tile, tile), tile))
        return carry

    lax.fori_loop(0, count // tile, step, 0)


def fetch(copies):
    for copy in copies:
        copy.start()
    return copies


def settle(copies):
    for copy in copies:
        copy.wait()


PAIR = 2 * HD


def nt(x, w):
    return lax.dot_general(x, w, (((1,), (1,)), ((), ())), preferred_element_type=F32)


def nn(x, w):
    return lax.dot_general(x, w, (((1,), (0,)), ((), ())), preferred_element_type=F32)


def tn(x, w):
    return lax.dot_general(x, w, (((0,), (0,)), ((), ())), preferred_element_type=F32)


def block_bias(seg_col, seg_row, bias, start, rows, keys):
    query = seg_col[start:start + rows, 0:1]
    for first in range(0, keys, rows):
        key = seg_row[:, first:first + rows]
        seen = query == key
        if first + rows > start:
            q_pos = start + lax.broadcasted_iota(jnp.int32, (rows, rows), 0)
            k_pos = first + lax.broadcasted_iota(jnp.int32, (rows, rows), 1)
            seen = seen & (k_pos <= q_pos)
        bias[:, first:first + rows] = jnp.where(seen, 0.0, MASKED).astype(F32)


def one_head(pair, head):
    lane = lax.broadcasted_iota(jnp.int32, pair.shape, 1)
    return jnp.where((lane < HD) if head == 0 else (lane >= HD), pair, jnp.zeros_like(pair))


def attend_block(qkv, bias, att, lse, start, rows):
    keys = start + rows
    width = qkv.shape[2]
    stat_lane = lax.broadcasted_iota(jnp.int32, (rows, 128), 1)
    stats = jnp.zeros((rows, 128), F32)
    for p in range(width // PAIR):
        lanes = slice(p * PAIR, (p + 1) * PAIR)
        query = qkv[0, start:keys, lanes]
        outs = []
        for head in range(2):
            s = nt(one_head(query, head), qkv[1, 0:keys, lanes]) + bias[:, 0:keys]
            top = jnp.max(s, axis=1, keepdims=True)
            e = jnp.exp(s - top)
            total = jnp.sum(e, axis=1, keepdims=True)
            prob = (e * (1.0 / total)).astype(BF)
            outs.append(nn(prob, qkv[2, 0:keys, lanes]))
            stats = jnp.where(stat_lane == 2 * p + head, top + jnp.log(total), stats)
        lane = lax.broadcasted_iota(jnp.int32, outs[0].shape, 1)
        att[start:keys, lanes] = jnp.where(lane < HD, outs[0], outs[1]).astype(BF)
    lse[start:keys, :] = stats


def attend_block_back(qkv, bias, lse, do, dq, dk, dv, start, rows):
    keys = start + rows
    width = qkv.shape[2]
    stat_lane = lax.broadcasted_iota(jnp.int32, (rows, 128), 1)
    stats = lse[start:keys, :]
    for p in range(width // PAIR):
        lanes = slice(p * PAIR, (p + 1) * PAIR)
        query = qkv[0, start:keys, lanes]
        grad = do[start:keys, lanes]
        dqs, dks, dvs = [], [], []
        for head in range(2):
            level = jnp.sum(jnp.where(stat_lane == 2 * p + head, stats, 0.0), axis=1, keepdims=True)
            s = nt(one_head(query, head), qkv[1, 0:keys, lanes]) + bias[:, 0:keys]
            prob = jnp.exp(s - level)
            d_prob = nt(one_head(grad, head), qkv[2, 0:keys, lanes])
            mixed = prob * d_prob
            ds = (mixed - prob * jnp.sum(mixed, axis=1, keepdims=True)).astype(BF)
            dqs.append(nn(ds, qkv[1, 0:keys, lanes]))
            dks.append(tn(ds, query))
            dvs.append(tn(prob.astype(BF), grad))
        lane = lax.broadcasted_iota(jnp.int32, dqs[0].shape, 1)
        dq[start:keys, lanes] = (jnp.where(lane < HD, dqs[0], dqs[1]) * (HD ** -0.5)).astype(dq.dtype)
        lane = lax.broadcasted_iota(jnp.int32, dks[0].shape, 1)
        dk[0:keys, lanes] += jnp.where(lane < HD, dks[0], dks[1])
        dv[0:keys, lanes] += jnp.where(lane < HD, dvs[0], dvs[1])


def mk1_body(geo, x_ref, aw_ref, ow_ref, up_ref, down_ref, gain_ref, bias_ref, seg_ref,
             n1t, qkv, att, lse, wf, rows12, total, xf, seg_col, full,
             sf, n1, part, land, bias, wsend, ow_in, down_in, dsend, gain_in, bias_in, seg_row, ssend, send, recv, local):
    spot = geo.bind()
    wire = Wire(send, recv)
    size = geo.tensor
    rows = x_ref.shape[0]
    wrows = aw_ref.shape[1]
    mrows = up_ref.shape[0]
    heads = aw_ref.shape[2]

    def xslot(t):
        return xf.at[pl.ds(pl.multiple_of(t * rows, rows), rows)]

    def block(i):
        return part.at[pl.ds(pl.multiple_of(i * rows, rows), rows)]

    wspan = pl.ds(pl.multiple_of(spot.d * wrows, wrows), wrows)
    span = pl.ds(pl.multiple_of(spot.d * mrows, mrows), mrows)
    pairs = [
        (gain_ref, gain_in), (bias_ref, bias_in), (aw_ref, wsend.at[pl.ds(0, 3)]), (ow_ref, ow_in), (up_ref, full.at[0, spot.t, span]),
        (x_ref, xslot(spot.t)), (down_ref, down_in), (seg_ref, seg_row)]
    loads = fetch([pltpu.make_async_copy(src, dst, local.at[i]) for i, (src, dst) in enumerate(pairs)])
    greet(spot)
    weights = WeightGather(spot, wire, wrows, wf)
    lines = [LineGather(spot, wire, src, lambda t, k=k: full.at[k, t, span]) for k, src in enumerate((up_ref, dsend))]
    ups, downs = [WeightGather(spot, wire, mrows, full.at[k]) for k in range(2)]
    xs = LineGather(spot, wire, x_ref, xslot)
    small = wire.take(geo.dp - 1)
    lines[0].start()
    settle(loads[0:4])
    ssend[0:2, :] = gain_in[...].astype(F32)
    ssend[2:12, :] = bias_in[...].astype(F32)
    for step in range(1, geo.dp):
        wire.start(small + step - 1, ssend, sf.at[spot.d], spot.at_d(ring_next(spot.d, step, geo.dp)))
    wsend[3] = ow_in[...].T
    wf[:, wspan] = wsend[...]
    weights.first()
    sf[spot.d] = ssend[...]
    loads[6].wait()
    dsend[...] = down_in[...].T
    down_copy = pltpu.make_async_copy(dsend, full.at[1, spot.t, span], local.at[8])
    down_copy.start()
    weights.second()
    lines[0].forward()
    xs.start()
    weights.third()
    loads[4].wait()
    lines[0].finish()
    ups.first()
    for step in range(1, geo.dp):
        source = ring_prev(spot.d, step, geo.dp)
        wire.landed(small + step - 1, sf.at[source], spot.at_d(source))
    piece = ssend.shape[1]
    for d in range(geo.dp):
        rows12[:, d * piece:(d + 1) * piece] = sf[d]
    loads[7].wait()
    seg_col[...] = jnp.broadcast_to(seg_row[...], (128, seg_row.shape[1])).T
    weights.fourth()
    loads[5].wait()
    column = pl.ds(pl.multiple_of(spot.t * heads, 128), heads)

    def project(t):
        def norm(r):
            n1[r] = layer_norm(xf[r].astype(F32), rows12[0:1, :], rows12[2:3, :]).astype(BF)

        first = pl.multiple_of(t * rows, rows)
        loop_rows(rows, min(64, rows), norm, first)
        r = pl.ds(first, rows)
        normed = n1[r]
        qkv[0, r] = ((nn(normed, wf[0]) + rows12[3:4, column]).astype(BF).astype(F32) * HD ** -0.5).astype(BF)
        qkv[1, r] = nn(normed, wf[1]).astype(BF)
        qkv[2, r] = (nn(normed, wf[2]) + rows12[4:5, column]).astype(BF)

    project(spot.t)
    ups.second()
    xs.forward()
    xs.finish()
    lines[1].start()

    def other(step, carry):
        project(ring_next(spot.t, step, size))
        return carry

    lax.fori_loop(1, size, other, 0)
    ups.third()
    scatter = LineScatter(spot, wire, block, lambda k: land.at[k], lambda dst, src: add_tiled(dst, src, 64))
    qrows = min(256, SEQ)
    for start in range(0, SEQ, qrows):
        block_bias(seg_col, seg_row, bias, start, qrows, start + qrows)
        attend_block(qkv, bias, att, lse, start, qrows)
        part[start:start + qrows, :] = nt(att[start:start + qrows, :], wf[3]).astype(BF)
        if scatter.line:
            scatter.start_block(start // rows)
        if start == 0:
            lines[1].forward()
    if not scatter.line:
        scatter.start()
    down_copy.wait()
    lines[1].finish()
    downs.first()
    for start in range(0, SEQ, qrows):
        n1t[:, start:start + qrows] = n1[start:start + qrows, :].T
    scatter.forward()
    downs.second()
    mine = block(spot.t)

    def set_total(r):
        total[r] = mine[r].astype(F32)

    loop_rows(rows, min(64, rows), set_total)
    scatter.finish(lambda ref: add_tiled(total, ref, 64))
    ups.fourth()
    downs.third()
    downs.fourth()
    wire.drain()


def mk1(geo, x, aw, ow, up, down, gains, biases, seg_row):
    rows, width = x.shape
    wrows, heads = aw.shape[1:]
    size = geo.tensor
    sems = 24 + 4 * size + geo.dp + 3 * gather_sems(geo)
    seq = size * rows
    return pl.pallas_call(
        functools.partial(mk1_body, geo),
        out_shape=(
            jax.ShapeDtypeStruct((width, seq), BF),
            jax.ShapeDtypeStruct((3, seq, heads), BF),
            jax.ShapeDtypeStruct((seq, heads), BF),
            jax.ShapeDtypeStruct((seq, 128), F32),
            jax.ShapeDtypeStruct((4, width, heads), BF),
            jax.ShapeDtypeStruct((12, width), F32),
            jax.ShapeDtypeStruct((rows, width), F32),
            jax.ShapeDtypeStruct((seq, width), BF),
            jax.ShapeDtypeStruct((seq, 128), jnp.int32),
            jax.ShapeDtypeStruct((2, size, width, up.shape[1]), BF),
        ),
        in_specs=[ANY] * 8,
        out_specs=(VM,) * 9 + (ANY,),
        scratch_shapes=[
            pltpu.VMEM((geo.dp, 12, wrows), F32),
            pltpu.VMEM((seq, width), BF),
            pltpu.VMEM((seq, width), BF),
            pltpu.VMEM((max(5, size - 1), rows, width), BF),
            pltpu.VMEM((min(256, SEQ), SEQ), F32),
            pltpu.VMEM((4, wrows, heads), BF),
            pltpu.VMEM(ow.shape, BF),
            pltpu.VMEM(down.shape, BF),
            pltpu.VMEM(up.shape, BF),
            pltpu.VMEM(gains.shape, BF),
            pltpu.VMEM(biases.shape, BF),
            pltpu.VMEM(seg_row.shape, jnp.int32),
            pltpu.VMEM((12, wrows), F32),
            pltpu.SemaphoreType.DMA((sems,)), pltpu.SemaphoreType.DMA((sems,)), pltpu.SemaphoreType.DMA((9,))],
        compiler_params=pltpu.CompilerParams(collective_id=1, has_side_effects=True, vmem_limit_bytes=56 * 2**20),
        name="mk1",
    )(x, aw, ow, up, down, gains, biases, seg_row)


GELU_C = 0.7978845608028654


def gelu_parts(a):
    square = a * a
    tanh = jnp.tanh(GELU_C * a * (1.0 + 0.044715 * square))
    half = 0.5 * (1.0 + tanh)
    slope = half + 0.5 * a * (1.0 - tanh * tanh) * (GELU_C * (1.0 + 3 * 0.044715 * square))
    return a * half, slope


def column_sum(values):
    return jnp.sum(values, axis=0, keepdims=True)


def mk2_body(geo, m_ref, cot_ref, n1t_ref, qkv_ref, att_ref, lse_ref, wf_ref, rows_ref, sum_ref, xf_ref, segc_ref, segr_ref,
             out, igrad, awg, owg, upg, downg, gaing, biasg,
             mid, cot, rows12, n1t, qkv, att, lse, wf, xf, seg_col, seg_row, gaf, sums, spart, sland, stot, tland,
             held, one_a, one_b, two_a, two_b, wheld, wone_a, wone_b, wtwo_a, wtwo_b, mland, land, gtot,
             send, recv, local, msem):
    spot = geo.bind()
    wire = Wire(send, recv)
    size = geo.tensor
    rows, width = out.shape
    seq = size * rows
    heads = att.shape[1]
    unit = m_ref.shape[3]
    mrows = upg.shape[0]
    wrows = awg.shape[1]
    a_size, b_size = geo.a_size, geo.b_size
    ab = a_size * b_size
    chunk = min(512, unit)
    per = unit // chunk
    count = size * per
    tail = min(64, rows)
    tile = min(64, mrows)
    sibling = spot.at_d(spot.rank(spot.b, spot.a, 1 - spot.c))
    pairs = [
        (sum_ref, mid), (xf_ref, xf), (rows_ref, rows12), (cot_ref, cot), (wf_ref, wf), (qkv_ref, qkv), (att_ref, att), (lse_ref, lse),
        (n1t_ref, n1t), (segc_ref, seg_col), (segr_ref, seg_row)]
    loads = fetch([pltpu.make_async_copy(src, dst, local.at[i]) for i, (src, dst) in enumerate(pairs)])
    greet(spot)

    def slot(t):
        return gaf.at[pl.ds(pl.multiple_of(t * rows, rows), rows)]

    def own_rows(r, n):
        return pl.ds(pl.multiple_of(spot.t * rows + r.start, n), n)

    gather = LineGather(spot, wire, slot(spot.t), slot)
    zero = [wire.take(size) for _ in range(2)]
    wzero = wire.take(ab)
    scatters = [WeightScatter(spot, wire, *(buf.at[k] for buf in (held, one_a, one_b, two_a, two_b))) for k in range(2)]
    wscatter = WeightScatter(spot, wire, *(buf.at[0] for buf in (wheld, wone_a, wone_b, wtwo_a, wtwo_b)))

    def line_of(k):
        here = held.at[k, spot.b, spot.a]
        return LineScatter(spot, wire, lambda t: here.at[t], lambda j: mland.at[k, j], lambda dst, src: add_tiled(dst, src, tile))

    lines = [line_of(k) for k in range(2)]
    small = wire.take(geo.dp - 1)
    last = wire.take(size - 1)
    sums[...] = jnp.zeros_like(sums)

    def mlp(mbuf, hmid, da, n2, gm, turned, n2t, gmt, snd, dn2):
        def mload(j, s):
            return pltpu.make_async_copy(
                m_ref.at[:, lax.div(j, per), :, pl.ds(pl.multiple_of(lax.rem(j, per) * chunk, chunk), chunk)], mbuf.at[s], msem.at[s])

        mload(0, 0).start()
        settle(loads[0:4])

        def norm(r):
            value = xf[own_rows(r, tail)].astype(F32) + (mid[r] + rows12[5:6, :])
            mid[r] = value
            n2[r] = layer_norm(value, rows12[1:2, :], rows12[6:7, :]).astype(BF)
            branch = cot[r].astype(BF)
            gm[r] = branch
            sums[7:8, :] += column_sum(branch.astype(F32))

        loop_rows(rows, tail, norm)

        def turn(value, dst):
            turned[...] = value[...].T
            for i in range(ab):
                for other in range(2):
                    core = lax.rem(spot.c + other, 2)
                    dst[other, i * mrows:(i + 1) * mrows, :] = turned[pl.ds(pl.multiple_of((i * 2 + core) * mrows, mrows), mrows), :]

        turn(gm, gmt)
        dn2[...] = jnp.zeros_like(dn2)
        out[...] = jnp.zeros_like(out)

        def cols_of(j):
            return pl.ds(pl.multiple_of(j * chunk, chunk), chunk)

        def sub_of(j):
            return pl.ds(pl.multiple_of(lax.rem(j, per) * chunk, chunk), chunk)

        def sending(k, t):
            return wire.copy(zero[k] + t, snd.at[:, :, t], held.at[k, :, :, t], sibling)

        def give(k, j, left, right):
            product = nn(left[1], right).astype(BF)
            t = lax.div(j, per)
            for i in range(ab):
                snd[i // a_size, i % a_size, t, :, sub_of(j)] = product[i * mrows:(i + 1) * mrows, :]

            @pl.when(lax.rem(j, per) == per - 1)
            def _():
                sending(k, t).start()

        def keep(k, j, left, right):
            t = lax.div(j, per)

            @pl.when(lax.rem(j, per) == 0)
            def _():
                sending(k, t).wait_recv()

            product = nn(left[0], right)
            for i in range(ab):
                b, a = i // a_size, i % a_size
                held[k, b, a, t, :, sub_of(j)] = (
                    held[k, b, a, t, :, sub_of(j)].astype(F32) + product[i * mrows:(i + 1) * mrows, :]).astype(BF)

        def one(j, carry):
            s = lax.rem(j, 2)
            mload(j, s).wait()

            @pl.when(j + 1 < count)
            def _():
                mload(j + 1, 1 - s).start()

            cols = cols_of(j)
            row = pl.ds(8 + lax.div(j * chunk, width), 1)
            bcols = pl.ds(pl.multiple_of(lax.rem(j * chunk, width), chunk), chunk)
            a = nn(n2[...], mbuf[s, 0]) + rows12[row, bcols]
            value, slope = gelu_parts(a)
            active = value.astype(BF)
            hmid[:, cols] = active
            grad = (nn(gm[...], mbuf[s, 1]) * slope).astype(BF)
            da[:, cols] = grad
            sums[row, bcols] = column_sum(grad.astype(F32))
            give(1, j, gmt, active)
            dn2[...] += nt(grad, mbuf[s, 0])
            out[...] += nt(active, mbuf[s, 1])
            return carry

        lax.fori_loop(0, count, one, 0)

        def back(r):
            value = mid[r]
            unit_two, scale_two = norm_stats(value)
            grad = dn2[r]
            total = cot[r] + norm_back(grad, unit_two, scale_two, rows12[1:2, :])
            cot[r] = total
            branch = total.astype(BF)
            gaf[own_rows(r, tail)] = branch
            sums[1:2, :] += column_sum(grad * unit_two)
            sums[6:7, :] += column_sum(grad)
            sums[5:6, :] += column_sum(branch.astype(F32))
            out[r] = value + (out[r] + rows12[7:8, :])

        loop_rows(rows, tail, back)
        gather.start()

        def keep_down(j, carry):
            keep(1, j, gmt, hmid[:, cols_of(j)])
            return carry

        lax.fori_loop(0, count, keep_down, 0)
        scatters[1].first()
        turn(n2, n2t)
        for t in range(size):
            sending(1, t).wait_send()

        def give_up(j, carry):
            give(0, j, n2t, da[:, cols_of(j)])
            return carry

        lax.fori_loop(0, count, give_up, 0)
        gather.forward()

        def keep_up(j, carry):
            keep(0, j, n2t, da[:, cols_of(j)])
            return carry

        lax.fori_loop(0, count, keep_up, 0)
        scatters[0].first()
        for t in range(size):
            sending(0, t).wait_send()

    ff = size * unit
    pl.run_scoped(
        mlp,
        pltpu.VMEM((2, 2, width, chunk), BF),
        pltpu.VMEM((rows, ff), BF),
        pltpu.VMEM((rows, ff), BF),
        pltpu.VMEM((rows, width), BF),
        pltpu.VMEM((rows, width), BF),
        pltpu.VMEM((width, rows), BF),
        pltpu.VMEM((2, ab * mrows, rows), BF),
        pltpu.VMEM((2, ab * mrows, rows), BF),
        pltpu.VMEM((b_size, a_size, size, mrows, unit), BF),
        pltpu.VMEM((rows, width), F32),
    )
    settle(loads[4:])
    scatters[1].second()
    gather.finish()

    def attention(gat, do, dqkv, dk, dv, bias, wg, part):
        def block(i):
            return part.at[pl.ds(pl.multiple_of(i * rows, rows), rows)]

        scatter = LineScatter(spot, wire, block, lambda k: land.at[k], lambda dst, src: add_tiled(dst, src, tail))
        column = pl.ds(pl.multiple_of(spot.t * heads, 128), heads)
        dk[...] = jnp.zeros_like(dk)
        dv[...] = jnp.zeros_like(dv)
        qrows = min(256, SEQ)
        half = width // 2
        for start in range(SEQ - qrows, -1, -qrows):
            end = start + qrows
            do[start:end, :] = nn(gaf[start:end, :], wf[3]).astype(BF)
            block_bias(seg_col, seg_row, bias, start, qrows, end)
            attend_block_back(qkv, bias, lse, do, dqkv.at[0], dk, dv, start, qrows)
            dqkv[1, start:end, :] = dk[start:end, :].astype(BF)
            dqkv[2, start:end, :] = dv[start:end, :].astype(BF)
            for j in (0, 2):
                sums[3 + j // 2:4 + j // 2, column] += column_sum(dqkv[j, start:end, :].astype(F32))
            x = xf[start:end, :].astype(F32)
            center = x - jnp.mean(x, axis=-1, keepdims=True)
            unit_one = center * lax.rsqrt(jnp.mean(center * center, axis=-1, keepdims=True) + EPSILON)
            for first in range(0, width, half):
                cols = slice(first, first + half)
                term = sum(nt(dqkv[j, start:end, :], wf[j, cols, :]) for j in range(3))
                sums[0:1, cols] += column_sum(term * unit_one[:, cols])
                sums[2:3, cols] += column_sum(term)
                part[start:end, cols] = term.astype(BF)
            if scatter.line:
                scatter.start_block(start // rows)
            gat[:, start:end] = gaf[start:end, :].T
            if start == SEQ - 2 * qrows:
                scatters[1].third()
                lines[1].start()
        if not scatter.line:
            scatter.start()
        piece = spart.shape[2]
        for d in range(geo.dp):
            spart[d] = sums[:, d * piece:(d + 1) * piece]
        for step in range(1, geo.dp):
            to = ring_next(spot.d, step, geo.dp)
            wire.start(small + step - 1, spart.at[to], sland.at[step - 1], spot.at_d(to))
        stot[...] = spart[spot.d]
        scatter.forward()

        def wgrad(r):
            for j in range(3):
                wg[j, r] = nn(n1t[r], dqkv[j]).astype(BF)
            wg[3, r] = nn(gat[r], att[...]).astype(BF)

        loop_rows(width, min(256, width), wgrad)

        def wspan(i, core):
            return pl.ds(pl.multiple_of((i * 2 + core) * wrows, wrows), wrows)

        for i in range(ab):
            wire.start(wzero + i, wg.at[:, wspan(i, 1 - spot.c)], wheld.at[0, i // a_size, i % a_size], sibling)
        scatters[0].second()
        for i in range(ab):
            here = wheld.at[0, i // a_size, i % a_size]
            wire.landed(wzero + i, here, sibling)
            wscatter.add(here, wg.at[:, wspan(i, spot.c)])
        wscatter.first()
        lines[1].forward()
        for step in range(1, geo.dp):
            wire.landed(small + step - 1, sland.at[step - 1], spot.at_d(ring_prev(spot.d, step, geo.dp)))
            stot[...] += sland[step - 1]
        for step in range(1, size):
            wire.start(last + step - 1, stot, tland.at[step - 1], spot.at_t(ring_next(spot.t, step, size)))
        scatters[0].third()
        lines[0].start()
        wscatter.second()
        mine = block(spot.t)

        def set_total(r):
            igrad[r] = mine[r].astype(F32)

        loop_rows(rows, tail, set_total)
        scatter.finish(lambda ref: add_tiled(igrad, ref, tail))

        def back(r):
            unit_one, scale_one = norm_stats(xf[own_rows(r, tail)].astype(F32))
            igrad[r] = cot[r] + norm_back(igrad[r], unit_one, scale_one, rows12[0:1, :])

        loop_rows(rows, tail, back)

        def line_end(k, total):
            here = held.at[k, spot.b, spot.a, spot.t]

            def set_row(r):
                total[r] = here[r].astype(F32)

            loop_rows(mrows, tile, set_row)
            lines[k].finish(lambda ref: add_tiled(total, ref, tile))

        line_end(1, gtot)
        downg[...] = gtot[...].T
        lines[0].forward()
        wscatter.third()
        sums_w = wheld.at[0, spot.b, spot.a]
        for j in range(3):
            awg[j] = sums_w[j].astype(F32)
        owg[...] = sums_w[3].astype(F32).T
        for step in range(1, size):
            wire.landed(last + step - 1, tland.at[step - 1], spot.at_t(ring_prev(spot.t, step, size)))
        total = stot[...]
        for step in range(1, size):
            total = total + tland[step - 1]
        gaing[...] = total[0:2, :]
        biasg[...] = total[2:12, :]
        line_end(0, upg)
        wire.drain()

    pl.run_scoped(
        attention,
        pltpu.VMEM((width, seq), BF),
        pltpu.VMEM((seq, heads), BF),
        pltpu.VMEM((3, seq, heads), BF),
        pltpu.VMEM((seq, heads), F32),
        pltpu.VMEM((seq, heads), F32),
        pltpu.VMEM((min(256, SEQ), SEQ), F32),
        pltpu.VMEM((4, width, heads), BF),
        pltpu.VMEM((seq, width), BF),
    )


def mk2(geo, m_full, cot, n1t, qkv, att, lse, wf, rows12, attn_sum, xf, seg_col, seg_row):
    rows, width = cot.shape
    seq, heads = att.shape
    size = geo.tensor
    unit = m_full.shape[3]
    mrows = width // geo.dp
    wrows = width // geo.dp
    sems = 30 + 8 * size + geo.a_size * geo.b_size + 3 * scatter_sems(geo) + geo.dp
    like = lambda x: pltpu.VMEM(x.shape, x.dtype)
    return pl.pallas_call(
        functools.partial(mk2_body, geo),
        out_shape=(
            jax.ShapeDtypeStruct((rows, width), F32),
            jax.ShapeDtypeStruct((rows, width), F32),
            jax.ShapeDtypeStruct((3, wrows, heads), F32),
            jax.ShapeDtypeStruct((heads, wrows), F32),
            jax.ShapeDtypeStruct((mrows, unit), F32),
            jax.ShapeDtypeStruct((unit, mrows), F32),
            jax.ShapeDtypeStruct((2, wrows), F32),
            jax.ShapeDtypeStruct((10, wrows), F32),
        ),
        in_specs=[ANY] * 12,
        out_specs=(VM,) * 8,
        scratch_shapes=[
            like(attn_sum), like(cot), like(rows12), like(n1t), like(qkv), like(att), like(lse), like(wf), like(xf), like(seg_col),
            like(seg_row),
            pltpu.VMEM((seq, width), BF),
            pltpu.VMEM((12, width), F32),
            pltpu.VMEM((geo.dp, 12, wrows), F32),
            pltpu.VMEM((geo.dp - 1, 12, wrows), F32),
            pltpu.VMEM((12, wrows), F32),
            pltpu.VMEM((size - 1, 12, wrows), F32),
            *scatter_bufs(geo, 2, size, mrows, unit),
            *scatter_bufs(geo, 1, 4, wrows, heads),
            pltpu.VMEM((2, max(5, size - 1), mrows, unit), BF),
            pltpu.VMEM((max(5, size - 1), rows, width), BF),
            pltpu.VMEM((mrows, unit), F32),
            pltpu.SemaphoreType.DMA((sems,)), pltpu.SemaphoreType.DMA((sems,)), pltpu.SemaphoreType.DMA((11,)),
            pltpu.SemaphoreType.DMA((2,))],
        compiler_params=pltpu.CompilerParams(collective_id=2, has_side_effects=True, vmem_limit_bytes=60 * 2**20),
        name="mk2",
    )(m_full, cot, n1t, qkv, att, lse, wf, rows12, attn_sum, xf, seg_col, seg_row)


def per_device(geo, activations, segments, attn_weight, out_weight, up_weight, down_weight, norm_gains, bias_rows, cotangent):
    normed_t, project, attended, log_total, w_full, rows12, attn_sum, x_full, seg_col, m_full = mk1(
        geo, activations, attn_weight[0], out_weight[0], up_weight[0], down_weight[0], norm_gains[0], bias_rows[0], segments[None, :])
    outs = mk2(
        geo, m_full, cotangent, normed_t, project, attended, log_total, w_full, rows12, attn_sum, x_full, seg_col, segments[None, :])
    return outs[:2] + tuple(part[None] for part in outs[2:])


def solution(mesh):
    geo = Geometry(mesh.shape["dp"], mesh.shape["tensor"])
    return jax.shard_map(
        functools.partial(per_device, geo),
        mesh=mesh,
        in_specs=(
            P(("dp", "tensor"), None),
            P("dp"),
            P(None, None, "dp", "tensor"),
            P(None, "tensor", "dp"),
            P(None, "dp", "tensor"),
            P(None, "tensor", "dp"),
            P(None, None, "dp"),
            P(None, None, "dp"),
            P(("dp", "tensor"), None),
        ),
        out_specs=(
            P(("dp", "tensor"), None),
            P(("dp", "tensor"), None),
            P(None, None, "dp", "tensor"),
            P(None, "tensor", "dp"),
            P(None, "dp", "tensor"),
            P(None, "tensor", "dp"),
            P(None, None, "dp"),
            P(None, None, "dp"),
        ),
        check_vma=False,
    )
```

time: 386 us -> 305 us (0.79); the launches traced: 378 us -> 305 us
  matrix products: 48.2 us -> 0 us
  other arithmetic: 18.9 us -> 0 us
  local copies, waits for them, and re-layouts: 15.9 us -> 8.29 us
    dot_general x32 -> x0, matrix products: 48.2 us -> none  [the longest x11 25 us: dot_nt(): lax.dot_general(x, w, (((1,), (1,)), ((), ())), preferred_element_type=F32)]
    another operation x4 -> x0, other arithmetic: 9.48 us -> none  [the longest x3 9.22 us: per_device(): jnp.stack([jnp.stack([dot_tn(normed_two, hidden_grad[:, s * unit_width:(s...]
    reduce_sum x10 -> x0, other arithmetic: 7.7 us -> none  [the longest x1 3.97 us: per_device(): up_bias_grad = jnp.sum(hidden_grad.astype(F32), axis=0).reshape(4, width)]
    unnamed x41 -> x20, local copies, waits for them, and re-layouts: 12.6 us -> 8.29 us
    pallas_call x3 -> x1, Pallas kernels: 160 us -> 161 us  [mk2(): pl.pallas_call(functools.partial(mk2_body, geo), out_shape=(jax.ShapeDtyp...]
where the time goes in v1:
time: 305 us
  Pallas kernels  296 us (97%)
  local copies, waits for them, and re-layouts  8.29 us (3%)
    pallas_call x1, Pallas kernels, mk2(): pl.pallas_call(functools.partial(mk2_body, geo), out_shape=(jax.ShapeDtyp...  161 us
    pallas_call x1, Pallas kernels, mk1(): pl.pallas_call(functools.partial(mk1_body, geo), out_shape=(jax.ShapeDtyp...  135 us
    unnamed x20, local copies, waits for them, and re-layouts  8.29 us

profile of v1, /device:TPU:0, one launch (start us, length us, event | category | flops | bytes accessed | tf_op | source)
XLA Modules:
  0.0 305.0 jit_solution(9992455836692067375)
XLA Ops:
  0.6 134.8 %mk1.1 = (bf16[1024,1024]{1,0:T(8,128)(2,1)}, bf16[3,1024,256]{2,1,0:T(8,128)(2,1)}, bf16[1024,256]{1,0:T(8,128)(2,1)}, f32[1024,128]{1,0:T(8,128)}, bf16[4,1024...) custom-call(bf16[256,1024]{1,0:T(8,128)(2,1)} %x_ref.1, ...), custom_call_target="tpu_custom_call" | custom-call | tf_op jit(solution)/shard_map/mk1/pallas_call | solution.py:660
  135.4 161.2 %mk2.1 = (f32[256,1024]{1,0:T(8,128)}, f32[256,1024]{1,0:T(8,128)}, f32[3,128,256]{2,1,0:T(8,128)}, f32[256,128]{1,0:T(8,128)}, f32[128,1024]{1,0:T(8,128)}, /*i...) custom-call(bf16[2,4,1024,1024]{3,2,1,0:T(8,128)(2,1)} %get-tuple-element.26.m_ref, f32[256,1024]{1,0:T(8,128)} %cot_ref.1, ...), custom_call_target="tpu_custom_call" | custom-call | tf_op jit(solution)/shard_map/mk2/pallas_call | solution.py:1041
  296.7 0.0 copy-start
  296.7 1.4 copy.17
  298.1 0.0 copy-start.3
  298.1 0.0 copy-start.4
  298.1 2.4 copy.25
  300.4 0.0 copy-done
  300.4 0.0 copy-start.2
  300.4 0.0 copy-start.1
  300.4 1.0 copy.26
  301.4 0.0 copy-done.3
  301.4 0.0 copy-start.5
  301.4 0.7 copy.27
  302.2 0.0 copy-done.4
  302.2 0.7 copy.28
  302.8 0.0 copy-done.2
  302.8 0.8 copy.29
  303.6 0.0 copy-done.1
  303.6 0.8 copy.30
  304.4 0.0 copy-done.5
  304.4 0.6 copy.31
Async XLA Ops:
  296.7 3.8 %copy-start = (f32[256,1024]{1,0:T(8,128)S(1)}, f32[256,1024]{1,0:T(8,128)}, u32[]{:S(2)}) copy-start(f32[256,1024]{1,0:T(8,128)} %get-tuple-element.61) | copy-start | bytes 3145732
  298.1 3.3 %copy-start.3 = (f32[3,128,256]{2,1,0:T(8,128)S(1)}, f32[3,128,256]{2,1,0:T(8,128)}, u32[]{:S(2)}) copy-start(f32[3,128,256]{2,1,0:T(8,128)} %get-tuple-element.38) | copy-start | bytes 1179652
  298.1 4.1 %copy-start.4 = (f32[256,128]{1,0:T(8,128)S(1)}, f32[256,128]{1,0:T(8,128)}, u32[]{:S(2)}) copy-start(f32[256,128]{1,0:T(8,128)} %get-tuple-element.39) | copy-start | bytes 393220
  300.4 2.4 copy-start.2
  300.4 3.2 %copy-start.1 = (f32[1024,128]{1,0:T(8,128)S(1)}, f32[1024,128]{1,0:T(8,128)}, u32[]{:S(2)}) copy-start(f32[1024,128]{1,0:T(8,128)} %get-tuple-element.41) | copy-start | bytes 1572868
  301.4 3.0 copy-start.5

commit v2 on v1

v2 whole, which is shorter than its diff:
```python
import functools

import jax
import jax.numpy as jnp
from jax import lax
from jax.experimental import pallas as pl
from jax.experimental.pallas import tpu as pltpu
from jax.sharding import PartitionSpec as P

HD = 64
EPSILON = 1e-05
MASKED = -1e30
MESH_ID = pl.DeviceIdType.MESH
BF = jnp.bfloat16
F32 = jnp.float32
ANY = pl.BlockSpec(memory_space=pl.ANY)
VM = pl.BlockSpec(memory_space=pltpu.VMEM)


def layer_norm(values, gain_row, shift_row):
    center = values - jnp.mean(values, axis=-1, keepdims=True)
    spread = jnp.mean(center * center, axis=-1, keepdims=True)
    return center * lax.rsqrt(spread + EPSILON) * gain_row + shift_row


def norm_stats(values):
    center = values - jnp.mean(values, axis=-1, keepdims=True)
    spread = jnp.mean(center * center, axis=-1, keepdims=True)
    scale = lax.rsqrt(spread + EPSILON)
    return center * scale, scale


def norm_back(grad, unit, scale, gain_row):
    u = grad * gain_row
    mean_u = jnp.mean(u, axis=-1, keepdims=True)
    mean_ux = jnp.mean(u * unit, axis=-1, keepdims=True)
    return scale * (u - mean_u - unit * mean_ux)


def gelu_tanh(values):
    return jax.nn.gelu(values, approximate=True)


class Geometry:
    def __init__(self, dp, tensor):
        self.dp, self.tensor = dp, tensor
        self.c_size = 2
        rest = dp // 2
        self.a_size = 1
        while self.a_size * self.a_size < rest:
            self.a_size *= 2
        self.b_size = rest // self.a_size
        assert self.a_size * self.b_size * 2 == dp

    def bind(self):
        spot = Spot()
        spot.geo = self
        spot.d = lax.axis_index("dp")
        spot.t = lax.axis_index("tensor")
        spot.c = lax.rem(spot.d, 2)
        half = lax.div(spot.d, 2)
        spot.a = lax.rem(half, self.a_size)
        spot.b = lax.div(half, self.a_size)
        return spot


class Spot:
    def rank(self, b, a, c):
        return (b * self.geo.a_size + a) * 2 + c

    def at_t(self, t):
        return (self.d, t)

    def at_d(self, d):
        return (d, self.t)


def ring_next(rank, step, size):
    return lax.rem(rank + step, size)


def ring_prev(rank, step, size):
    return lax.rem(rank + size - step, size)


class Wire:
    def __init__(self, send, recv):
        self.send_sems, self.recv_sems = send, recv
        self.count = 0
        self.pending = []

    def take(self, n):
        first = self.count
        self.count += n
        return first

    def copy(self, i, src, dst, device):
        return pltpu.make_async_remote_copy(
            src_ref=src, dst_ref=dst, send_sem=self.send_sems.at[i], recv_sem=self.recv_sems.at[i],
            device_id=device, device_id_type=MESH_ID)

    def plan(self, i, src, dst, device, when=None):
        return self.copy(i, src, dst, device), when

    def go(self, planned):
        copy, when = planned
        if when is None:
            copy.start()
        else:
            pl.when(when)(copy.start)
        if not any(other is planned for other in self.pending):
            self.pending.append(planned)

    def start(self, i, src, dst, device, when=None):
        self.go(self.plan(i, src, dst, device, when))

    def landed(self, i, dst, device, when=None):
        copy = self.copy(i, dst, dst, device)
        if when is None:
            copy.wait_recv()
        else:
            pl.when(when)(copy.wait_recv)

    def sent(self, plans):
        for planned in plans:
            copy, when = planned
            self.pending = [other for other in self.pending if other is not planned]
            if when is None:
                copy.wait_send()
            else:
                pl.when(when)(copy.wait_send)

    def drain(self):
        for copy, when in self.pending:
            if when is None:
                copy.wait_send()
            else:
                pl.when(when)(copy.wait_send)
        self.pending = []


def greet(spot):
    geo = spot.geo
    barrier = pltpu.get_barrier_semaphore()
    total = 0
    for step in range(1, geo.tensor):
        pl.semaphore_signal(barrier, inc=1, device_id=spot.at_t(ring_next(spot.t, step, geo.tensor)), device_id_type=MESH_ID)
        total += 1
    for step in range(1, geo.dp):
        pl.semaphore_signal(barrier, inc=1, device_id=spot.at_d(ring_next(spot.d, step, geo.dp)), device_id_type=MESH_ID)
        total += 1
    return lambda: pl.semaphore_wait(barrier, total)


def halves(ref, count, part):
    rows = ref.shape[-2] // count
    return ref.at[(slice(None),) * (len(ref.shape) - 2) + (pl.ds(part * rows, rows),)]


class LineGather:
    def __init__(self, spot, wire, src, slot, parts=2):
        self.spot, self.wire, self.src, self.slot, self.parts = spot, wire, src, slot, parts
        self.size = size = spot.geo.tensor
        self.base = [wire.take((size - 1) * parts) for _ in range(2)]
        t = spot.t
        self.sends = {}
        for k in range(size - 1):
            for part in range(parts):
                for side in range(2):
                    self.sends[k, part, side] = self.plan(k, part, side)

    def place(self, k, side):
        t = self.spot.t
        origin = t - k if side == 0 else t + k
        there = (origin >= 0) & (origin < self.size)
        onward = t + 1 if side == 0 else t - 1
        return origin, there, t - 1 if side == 0 else t + 1, onward, there & (onward >= 0) & (onward < self.size)

    def plan(self, k, part, side):
        origin, _, _, onward, going = self.place(k, side)
        piece = halves(self.slot(origin), self.parts, part)
        first = isinstance(k, int) and k == 0
        src = halves(self.src, self.parts, part) if first else piece
        return self.wire.plan(self.base[side] + k * self.parts + part, src, piece, self.spot.at_t(onward), when=going)

    def start(self):
        for part in range(self.parts):
            for side in range(2):
                self.wire.go(self.sends[0, part, side])

    def step(self, k):
        for part in range(self.parts):
            for side in range(2):
                origin, there, near, _, _ = self.place(k, side)
                piece = halves(self.slot(origin), self.parts, part)
                self.wire.landed(self.base[side] + (k - 1) * self.parts + part, piece, self.spot.at_t(near), when=there)
                if not isinstance(k, int):
                    copy, going = self.plan(k, part, side)
                    pl.when(going & (k < self.size - 1))(copy.start)
                elif k < self.size - 1:
                    self.wire.go(self.sends[k, part, side])

    def owe(self):
        for (k, part, side), planned in self.sends.items():
            if k > 0:
                self.wire.pending.append(planned)


class LineScatter:
    def __init__(self, spot, wire, part, land, add, rising=False, parts=2):
        self.spot, self.wire, self.part, self.land, self.add, self.parts = spot, wire, part, land, add, parts
        self.size = spot.geo.tensor
        base = [wire.take(self.size * parts) for _ in range(2)]
        t, end = spot.t, self.size - 1
        self.starts, self.hops = {}, {}
        for h in range(parts):
            for j in range(self.size):
                if j > 0:
                    self.starts[0, j, h] = wire.plan(
                        base[0] + j * parts + h, halves(part(j), parts, h), halves(land(0, j), parts, h), spot.at_t(1), when=t == 0)
                if j < end:
                    self.starts[1, j, h] = wire.plan(
                        base[1] + j * parts + h, halves(part(j), parts, h), halves(land(1, j), parts, h), spot.at_t(end - 1), when=t == end)
        self.events = []
        if rising:
            for e in range(1, 2 * end):
                self.events.append((10 * e, 0, e + 1 - t, (t >= 1) & (e + 1 - t >= t) & (e + 1 - t <= end)))
        for s in range(1, self.size):
            if not rising:
                self.events.append((10 * s, 0, end - s + t, (t >= 1) & (s >= t)))
            self.events.append((10 * s + (15 if rising else 0), 1, s - (end - t), (end - t >= 1) & (s >= end - t)))
        self.events.sort(key=lambda event: event[0])
        self.hops = []
        for _, side, j, here in self.events:
            near = spot.at_t(t - 1 if side == 0 else t + 1)
            away = spot.at_t(t + 1 if side == 0 else t - 1)
            for h in range(parts):
                held = halves(land(side, j), parts, h)
                i = base[side] + j * parts + h
                self.hops.append((here & (j == t), here & (j != t), j, h, held, wire.copy(i, held, held, near),
                                  wire.plan(i, held, held, away, when=here & (j != t))))

    def start_block(self, j):
        for side in range(2):
            for h in range(self.parts):
                if (side, j, h) in self.starts:
                    self.wire.go(self.starts[side, j, h])

    def start(self):
        for n in range(self.size):
            for side, j in ((0, self.size - 1 - n), (1, n)):
                for h in range(self.parts):
                    if (side, j, h) in self.starts:
                        self.wire.go(self.starts[side, j, h])

    def count(self):
        return len(self.hops)

    def step(self, first, last, total):
        for final, passing, j, h, held, landing, onward in self.hops[first:last]:
            @pl.when(final)
            def _():
                landing.wait_recv()
                total(held, h)

            @pl.when(passing)
            def _():
                landing.wait_recv()
                self.add(held, halves(self.part(j), self.parts, h))

            self.wire.go(onward)

    def plans(self):
        return list(self.starts.values()) + [hop[-1] for hop in self.hops]


def add_tiled(dst, src, tile):
    def step(i, carry):
        rows = pl.ds(pl.multiple_of(i * tile, tile), tile)
        dst[rows] = (dst[rows].astype(F32) + src[rows].astype(F32)).astype(dst.dtype)
        return carry

    lax.fori_loop(0, dst.shape[0] // tile, step, 0)


class WeightGather:
    def __init__(self, spot, wire, rows, full):
        geo = spot.geo
        self.spot, self.wire, self.full, self.rows = spot, wire, full, rows
        self.slots = full.shape[0]
        self.half = self.slots // 2
        self.one_a = wire.take(geo.a_size - 1)
        self.one_b = wire.take(geo.b_size - 1)
        self.two_a = wire.take((geo.b_size - 1) * geo.a_size)
        self.two_b = wire.take((geo.a_size - 1) * geo.b_size)
        self.last = wire.take(2 * geo.a_size * geo.b_size)
        self.plan_shares()
        self.plan_hops()

    def span(self, d):
        return pl.ds(pl.multiple_of(d * self.rows, self.rows), self.rows)

    def low(self, d):
        return self.full.at[pl.ds(0, self.half), self.span(d)]

    def high(self, d):
        return self.full.at[pl.ds(self.half, self.slots - self.half), self.span(d)]

    def plan_shares(self):
        spot, geo = self.spot, self.spot.geo
        self.shares = {}
        for j in range(geo.b_size):
            for i in range(geo.a_size):
                held = spot.rank(ring_prev(spot.b, j, geo.b_size), ring_prev(spot.a, i, geo.a_size), spot.c)
                sibling = spot.rank(spot.b, spot.a, 1 - spot.c)
                for part in range(2):
                    half = (self.low, self.high)[part](held)
                    self.shares[part, j, i] = self.wire.plan(
                        self.last + 2 * (j * geo.a_size + i) + part, half, half, spot.at_d(sibling))

    def share(self, part, j, i):
        self.wire.go(self.shares[part, j, i])

    def plan_hops(self):
        spot, geo, wire = self.spot, self.spot.geo, self.wire
        self.ones, self.twos_a, self.twos_b = [], {}, {}
        mine = spot.d
        for j in range(1, geo.a_size):
            to = spot.rank(spot.b, ring_next(spot.a, j, geo.a_size), spot.c)
            self.ones.append(wire.plan(self.one_a + j - 1, self.low(mine), self.low(mine), spot.at_d(to)))
        for j in range(1, geo.b_size):
            to = spot.rank(ring_next(spot.b, j, geo.b_size), spot.a, spot.c)
            self.ones.append(wire.plan(self.one_b + j - 1, self.high(mine), self.high(mine), spot.at_d(to)))
        for i in range(geo.a_size):
            held = spot.rank(spot.b, ring_prev(spot.a, i, geo.a_size), spot.c)
            for j in range(1, geo.b_size):
                to = spot.rank(ring_next(spot.b, j, geo.b_size), spot.a, spot.c)
                self.twos_a[i, j] = wire.plan(self.two_a + (j - 1) * geo.a_size + i, self.low(held), self.low(held), spot.at_d(to))
        for i in range(geo.b_size):
            held = spot.rank(ring_prev(spot.b, i, geo.b_size), spot.a, spot.c)
            for j in range(1, geo.a_size):
                to = spot.rank(spot.b, ring_next(spot.a, j, geo.a_size), spot.c)
                self.twos_b[i, j] = wire.plan(self.two_b + (j - 1) * geo.b_size + i, self.high(held), self.high(held), spot.at_d(to))

    def first(self):
        for planned in self.ones:
            self.wire.go(planned)
        self.share(0, 0, 0)
        self.share(1, 0, 0)

    def second(self):
        spot, geo = self.spot, self.spot.geo
        for i in range(geo.a_size):
            held = spot.rank(spot.b, ring_prev(spot.a, i, geo.a_size), spot.c)
            if i:
                self.wire.landed(self.one_a + i - 1, self.low(held), spot.at_d(held))
                self.share(0, 0, i)
            for j in range(1, geo.b_size):
                self.wire.go(self.twos_a[i, j])
        for i in range(geo.b_size):
            held = spot.rank(ring_prev(spot.b, i, geo.b_size), spot.a, spot.c)
            if i:
                self.wire.landed(self.one_b + i - 1, self.high(held), spot.at_d(held))
                self.share(1, i, 0)
            for j in range(1, geo.a_size):
                self.wire.go(self.twos_b[i, j])

    def third(self):
        spot, geo = self.spot, self.spot.geo
        for j in range(1, geo.b_size):
            for i in range(geo.a_size):
                held = spot.rank(ring_prev(spot.b, j, geo.b_size), ring_prev(spot.a, i, geo.a_size), spot.c)
                source = spot.rank(ring_prev(spot.b, j, geo.b_size), spot.a, spot.c)
                self.wire.landed(self.two_a + (j - 1) * geo.a_size + i, self.low(held), spot.at_d(source))
                self.share(0, j, i)
        for j in range(1, geo.a_size):
            for i in range(geo.b_size):
                held = spot.rank(ring_prev(spot.b, i, geo.b_size), ring_prev(spot.a, j, geo.a_size), spot.c)
                source = spot.rank(spot.b, ring_prev(spot.a, j, geo.a_size), spot.c)
                self.wire.landed(self.two_b + (j - 1) * geo.b_size + i, self.high(held), spot.at_d(source))
                self.share(1, i, j)

    def fourth(self):
        spot, geo = self.spot, self.spot.geo
        sibling = spot.rank(spot.b, spot.a, 1 - spot.c)
        for j in range(geo.b_size):
            for i in range(geo.a_size):
                held = spot.rank(ring_prev(spot.b, j, geo.b_size), ring_prev(spot.a, i, geo.a_size), 1 - spot.c)
                for part in range(2):
                    half = (self.low, self.high)[part](held)
                    self.wire.landed(self.last + 2 * (j * geo.a_size + i) + part, half, spot.at_d(sibling))


def gather_sems(geo):
    return geo.a_size + geo.b_size + 4 * geo.a_size * geo.b_size


class WeightScatter:
    def __init__(self, spot, wire, held, one_a, one_b, two_a, two_b):
        geo = spot.geo
        self.spot, self.wire, self.held = spot, wire, held
        self.one_a_buf, self.one_b_buf, self.two_a_buf, self.two_b_buf = one_a, one_b, two_a, two_b
        self.slots, self.rows = held.shape[2], held.shape[3]
        self.half = self.slots // 2
        self.one_a = wire.take(geo.a_size - 1)
        self.one_b = wire.take(geo.b_size - 1)
        self.two_a = wire.take(geo.b_size - 1)
        self.two_b = wire.take(geo.a_size - 1)
        low, high = pl.ds(0, self.half), pl.ds(self.half, self.half)
        self.sends = []
        for j in range(1, geo.a_size):
            a = ring_next(spot.a, j, geo.a_size)
            self.sends.append(wire.plan(self.one_a + j - 1, held.at[:, a, low], one_a.at[j - 1], spot.at_d(spot.rank(spot.b, a, spot.c))))
        for j in range(1, geo.b_size):
            b = ring_next(spot.b, j, geo.b_size)
            self.sends.append(wire.plan(self.one_b + j - 1, held.at[b, :, high], one_b.at[j - 1], spot.at_d(spot.rank(b, spot.a, spot.c))))
        self.later = []
        for j in range(1, geo.b_size):
            b = ring_next(spot.b, j, geo.b_size)
            self.later.append(wire.plan(self.two_a + j - 1, held.at[b, spot.a, low], two_a.at[j - 1], spot.at_d(spot.rank(b, spot.a, spot.c))))
        for j in range(1, geo.a_size):
            a = ring_next(spot.a, j, geo.a_size)
            self.later.append(wire.plan(self.two_b + j - 1, held.at[spot.b, a, high], two_b.at[j - 1], spot.at_d(spot.rank(spot.b, a, spot.c))))

    def add(self, dst, src):
        tile = min(64, self.rows)
        per = self.rows // tile

        def step(i, carry):
            rows = pl.ds(pl.multiple_of(lax.rem(i, per) * tile, tile), tile)
            j = lax.div(i, per)
            dst[j, rows] = (dst[j, rows].astype(F32) + src[j, rows].astype(F32)).astype(dst.dtype)
            return carry

        lax.fori_loop(0, dst.shape[0] * per, step, 0)

    def first(self):
        for planned in self.sends:
            self.wire.go(planned)

    def second(self):
        spot, geo = self.spot, self.spot.geo
        low, high = pl.ds(0, self.half), pl.ds(self.half, self.half)
        for j in range(1, geo.a_size):
            self.wire.landed(self.one_a + j - 1, self.one_a_buf.at[j - 1], spot.at_d(spot.rank(spot.b, ring_prev(spot.a, j, geo.a_size), spot.c)))
            for b in range(geo.b_size):
                self.add(self.held.at[b, spot.a, low], self.one_a_buf.at[j - 1, b])
        for j in range(1, geo.b_size):
            self.wire.landed(self.one_b + j - 1, self.one_b_buf.at[j - 1], spot.at_d(spot.rank(ring_prev(spot.b, j, geo.b_size), spot.a, spot.c)))
            for a in range(geo.a_size):
                self.add(self.held.at[spot.b, a, high], self.one_b_buf.at[j - 1, a])
        for planned in self.later:
            self.wire.go(planned)

    def third(self):
        spot, geo = self.spot, self.spot.geo
        low, high = pl.ds(0, self.half), pl.ds(self.half, self.half)
        for j in range(1, geo.b_size):
            self.wire.landed(self.two_a + j - 1, self.two_a_buf.at[j - 1], spot.at_d(spot.rank(ring_prev(spot.b, j, geo.b_size), spot.a, spot.c)))
            self.add(self.held.at[spot.b, spot.a, low], self.two_a_buf.at[j - 1])
        for j in range(1, geo.a_size):
            self.wire.landed(self.two_b + j - 1, self.two_b_buf.at[j - 1], spot.at_d(spot.rank(spot.b, ring_prev(spot.a, j, geo.a_size), spot.c)))
            self.add(self.held.at[spot.b, spot.a, high], self.two_b_buf.at[j - 1])


def scatter_sems(geo):
    return 2 * geo.a_size + 2 * geo.b_size


def scatter_bufs(geo, n, slots, rows, width):
    a, b, half = geo.a_size, geo.b_size, slots // 2
    return [
        pltpu.VMEM((n, b, a, slots, rows, width), BF),
        pltpu.VMEM((a - 1, b, half, rows, width), BF),
        pltpu.VMEM((b - 1, a, half, rows, width), BF),
        pltpu.VMEM((b - 1, half, rows, width), BF),
        pltpu.VMEM((a - 1, half, rows, width), BF),
    ]


def loop_rows(count, tile, body, start=0):
    def step(i, carry):
        body(pl.ds(pl.multiple_of(start + i * tile, tile), tile))
        return carry

    lax.fori_loop(0, count // tile, step, 0)


def fetch(copies):
    for copy in copies:
        copy.start()
    return copies


def settle(copies):
    for copy in copies:
        copy.wait()


PAIR = 2 * HD


def nt(x, w):
    return lax.dot_general(x, w, (((1,), (1,)), ((), ())), preferred_element_type=F32)


def nn(x, w):
    return lax.dot_general(x, w, (((1,), (0,)), ((), ())), preferred_element_type=F32)


def tn(x, w):
    return lax.dot_general(x, w, (((0,), (0,)), ((), ())), preferred_element_type=F32)


def block_bias(seg_col, seg_row, bias, start, rows, keys):
    query = seg_col[start:start + rows, 0:1]
    for first in range(0, keys, rows):
        key = seg_row[:, first:first + rows]
        seen = query == key
        if first + rows > start:
            q_pos = start + lax.broadcasted_iota(jnp.int32, (rows, rows), 0)
            k_pos = first + lax.broadcasted_iota(jnp.int32, (rows, rows), 1)
            seen = seen & (k_pos <= q_pos)
        bias[:, first:first + rows] = jnp.where(seen, 0.0, MASKED).astype(F32)


def one_head(pair, head):
    lane = lax.broadcasted_iota(jnp.int32, pair.shape, 1)
    return jnp.where((lane < HD) if head == 0 else (lane >= HD), pair, jnp.zeros_like(pair))


def attend_block(qkv, bias, att, lse, start, rows):
    keys = start + rows
    width = qkv.shape[2]
    stat_lane = lax.broadcasted_iota(jnp.int32, (rows, 128), 1)
    stats = jnp.zeros((rows, 128), F32)
    for p in range(width // PAIR):
        lanes = slice(p * PAIR, (p + 1) * PAIR)
        query = qkv[0, start:keys, lanes]
        outs = []
        for head in range(2):
            s = nt(one_head(query, head), qkv[1, 0:keys, lanes]) + bias[:, 0:keys]
            top = jnp.max(s, axis=1, keepdims=True)
            e = jnp.exp(s - top)
            total = jnp.sum(e, axis=1, keepdims=True)
            prob = (e * (1.0 / total)).astype(BF)
            outs.append(nn(prob, qkv[2, 0:keys, lanes]))
            stats = jnp.where(stat_lane == 2 * p + head, top + jnp.log(total), stats)
        lane = lax.broadcasted_iota(jnp.int32, outs[0].shape, 1)
        att[start:keys, lanes] = jnp.where(lane < HD, outs[0], outs[1]).astype(BF)
    lse[start:keys, :] = stats


def attend_block_back(qkv, bias, lse, do, dq, dk, dv, start, rows):
    keys = start + rows
    width = qkv.shape[2]
    stat_lane = lax.broadcasted_iota(jnp.int32, (rows, 128), 1)
    stats = lse[start:keys, :]
    for p in range(width // PAIR):
        lanes = slice(p * PAIR, (p + 1) * PAIR)
        query = qkv[0, start:keys, lanes]
        grad = do[start:keys, lanes]
        dqs, dks, dvs = [], [], []
        for head in range(2):
            level = jnp.sum(jnp.where(stat_lane == 2 * p + head, stats, 0.0), axis=1, keepdims=True)
            s = nt(one_head(query, head), qkv[1, 0:keys, lanes]) + bias[:, 0:keys]
            prob = jnp.exp(s - level)
            d_prob = nt(one_head(grad, head), qkv[2, 0:keys, lanes])
            mixed = prob * d_prob
            ds = (mixed - prob * jnp.sum(mixed, axis=1, keepdims=True)).astype(BF)
            dqs.append(nn(ds, qkv[1, 0:keys, lanes]))
            dks.append(tn(ds, query))
            dvs.append(tn(prob.astype(BF), grad))
        lane = lax.broadcasted_iota(jnp.int32, dqs[0].shape, 1)
        dq[start:keys, lanes] = (jnp.where(lane < HD, dqs[0], dqs[1]) * (HD ** -0.5)).astype(dq.dtype)
        lane = lax.broadcasted_iota(jnp.int32, dks[0].shape, 1)
        dk[0:keys, lanes] += jnp.where(lane < HD, dks[0], dks[1])
        dv[0:keys, lanes] += jnp.where(lane < HD, dvs[0], dvs[1])


GELU_C = 0.7978845608028654


def gelu_parts(a):
    square = a * a
    tanh = jnp.tanh(GELU_C * a * (1.0 + 0.044715 * square))
    half = 0.5 * (1.0 + tanh)
    slope = half + 0.5 * a * (1.0 - tanh * tanh) * (GELU_C * (1.0 + 3 * 0.044715 * square))
    return a * half, slope


def column_sum(values):
    return jnp.sum(values, axis=0, keepdims=True)


def block_body(geo, x_ref, aw_ref, ow_ref, up_ref, down_ref, gain_ref, bias_ref, seg_ref, cot_ref,
               full, out_ref, igrad_ref, awg_ref, owg_ref, upg_ref, downg_ref, gaing_ref, biasg_ref,
               xf, n1, n1t, qkv, att, lse, wf, part, land, bias, mid, cot, gaf, rows12, seg_col, seg_row,
               sf, wsend, ow_in, down_in, msend, gain_in, bias_in, ssend,
               sums, spart, sland, stot, tland,
               held, one_a, one_b, two_a, two_b, wheld, wone_a, wone_b, wtwo_a, wtwo_b, mland,
               gtot, downg, awg, owg, gaing, biasg,
               send, recv, local, msem, osem):
    spot = geo.bind()
    wire = Wire(send, recv)
    size = geo.tensor
    rows, width = x_ref.shape
    seq = size * rows
    wrows, heads = aw_ref.shape[1:]
    mrows, unit = up_ref.shape
    a_size, b_size = geo.a_size, geo.b_size
    ab = a_size * b_size
    chunk = min(512, unit)
    per = unit // chunk
    pieces = msem.shape[1]
    count = size * per
    tail = min(64, rows)
    tile = min(64, mrows)
    end = size - 1
    sibling = spot.at_d(spot.rank(spot.b, spot.a, 1 - spot.c))
    wspan = pl.ds(pl.multiple_of(spot.d * wrows, wrows), wrows)
    mspan = pl.ds(pl.multiple_of(spot.d * mrows, mrows), mrows)
    column = pl.ds(pl.multiple_of(spot.t * heads, 128), heads)

    def block_of(ref, t):
        return ref.at[pl.ds(pl.multiple_of(t * rows, rows), rows)]

    def own_rows(r, n):
        return pl.ds(pl.multiple_of(spot.t * rows + r.start, n), n)

    weights = WeightGather(spot, wire, wrows, wf)
    wlines = [LineGather(spot, wire, msend.at[k], lambda t, k=k: full.at[k, pl.ds(t * per, per), mspan]) for k in range(2)]
    ups, downs = [WeightGather(spot, wire, mrows, full.at[k]) for k in range(2)]
    xs = LineGather(spot, wire, x_ref, lambda t: block_of(xf, t))
    gas = LineGather(spot, wire, block_of(gaf, spot.t), lambda t: block_of(gaf, t))
    blocks = [
        LineScatter(spot, wire, lambda t: block_of(part, t), lambda side, j: land.at[side, j - 1 + side],
                    lambda dst, src: add_tiled(dst, src, tail), rising=k == 0) for k in range(2)]
    scatters = [WeightScatter(spot, wire, held.at[k], one_a, one_b, two_a, two_b) for k in range(2)]
    wscatter = WeightScatter(spot, wire, wheld.at[0], wone_a, wone_b, wtwo_a, wtwo_b)

    def line_of(k):
        here = held.at[k, spot.b, spot.a]
        return LineScatter(spot, wire, lambda t: here.at[t], lambda side, j: mland.at[k, side, j - 1 + side],
                           lambda dst, src: add_tiled(dst, src, min(64, mrows // 2)))

    lines = [line_of(k) for k in range(2)]
    zero = [wire.take(size) for _ in range(2)]
    wzero = wire.take(ab)
    gains_in = wire.take(geo.dp - 1)
    small = wire.take(geo.dp - 1)
    last = wire.take(size - 1)

    pairs = [
        (gain_ref, gain_in), (bias_ref, bias_in), (aw_ref, wsend.at[pl.ds(0, 3)]), (ow_ref, ow_in),
        (x_ref, block_of(xf, spot.t)), (down_ref, down_in), (seg_ref, seg_row), (cot_ref, cot)]
    pairs += [(up_ref.at[:, pl.ds(i * chunk, chunk)], msend.at[0, i]) for i in range(per)]
    loads = fetch([pltpu.make_async_copy(src, dst, local.at[i]) for i, (src, dst) in enumerate(pairs)])
    met = greet(spot)
    sums[...] = jnp.zeros_like(sums)
    settle(loads[0:4])
    ssend[0:2, :] = gain_in[...].astype(F32)
    ssend[2:12, :] = bias_in[...].astype(F32)
    sf[spot.d] = ssend[...]
    wsend[3] = ow_in[...].T
    wf[:, wspan] = wsend[...]
    settle(loads[8:])

    def store(k):
        return pltpu.make_async_copy(msend.at[k], full.at[k, pl.ds(spot.t * per, per), mspan], osem.at[k])

    store(0).start()
    met()
    wlines[0].start()
    for step in range(1, geo.dp):
        wire.start(gains_in + step - 1, ssend, sf.at[spot.d], spot.at_d(ring_next(spot.d, step, geo.dp)))
    weights.first()
    loads[5].wait()
    for i in range(per):
        msend[1, i] = down_in[i * chunk:(i + 1) * chunk, :].T
    store(1).start()
    wlines[0].step(1)
    weights.second()
    for k in range(2, size - 1):
        wlines[0].step(k)
    xs.start()
    weights.third()
    store(0).wait()
    wlines[0].step(end)
    ups.first()
    for step in range(1, geo.dp):
        source = ring_prev(spot.d, step, geo.dp)
        wire.landed(gains_in + step - 1, sf.at[source], spot.at_d(source))
    piece = ssend.shape[1]
    for d in range(geo.dp):
        rows12[:, d * piece:(d + 1) * piece] = sf[d]
    loads[6].wait()
    seg_col[...] = jnp.broadcast_to(seg_row[...], (128, seq)).T
    weights.fourth()
    loads[4].wait()

    def project(t):
        def norm(r):
            n1[r] = layer_norm(xf[r].astype(F32), rows12[0:1, :], rows12[2:3, :]).astype(BF)

        first = pl.multiple_of(t * rows, rows)
        loop_rows(rows, tail, norm, first)
        r = pl.ds(first, rows)
        normed = n1[r]
        qkv[0, r] = ((nn(normed, wf[0]) + rows12[3:4, column]).astype(BF).astype(F32) * HD ** -0.5).astype(BF)
        qkv[1, r] = nn(normed, wf[1]).astype(BF)
        qkv[2, r] = (nn(normed, wf[2]) + rows12[4:5, column]).astype(BF)

    def arrive(k, carry):
        @pl.when(k >= 1)
        def _():
            xs.step(k)

        @pl.when(k == end - 1)
        def _():
            wlines[1].start()

        def side(i, inner):
            t = spot.t + (2 * i - 1) * k

            @pl.when((t >= 0) & (t < size) & ((i == 0) | (k >= 1)))
            def _():
                project(t)

            return inner

        lax.fori_loop(0, 2, side, 0)

        @pl.when(k == 1)
        def _():
            ups.second()

        @pl.when(k == end)
        def _():
            wlines[1].step(1)
            ups.third()

        for i in range(size):
            start = i * rows

            @pl.when(jnp.maximum(spot.t, i - spot.t) == k)
            def _():
                block_bias(seg_col, seg_row, bias, start, rows, start + rows)
                attend_block(qkv, bias, att, lse, start, rows)
                part[start:start + rows, :] = nt(att[start:start + rows, :], wf[3]).astype(BF)
                blocks[0].start_block(i)

            if i == 1:
                @pl.when(k == end)
                def _():
                    wlines[1].step(2)

        return carry

    lax.fori_loop(0, size, arrive, 0)
    xs.owe()
    for k in range(3, size):
        wlines[1].step(k)
    store(1).wait()
    downs.first()
    for i in range(size):
        n1t[:, i * rows:(i + 1) * rows] = n1[i * rows:(i + 1) * rows, :].T

    def set_total(r):
        mid[r] = part[own_rows(r, tail)].astype(F32)

    loop_rows(rows, tail, set_total)

    def mid_total(ref, h):
        n = ref.shape[0]
        add_tiled(mid.at[pl.ds(h * n, n)], ref, tail)

    events = blocks[0].count()
    blocks[0].step(0, events // 2, mid_total)
    ups.fourth()
    downs.second()
    blocks[0].step(events // 2, events, mid_total)

    def mlp(mbuf, hmid, da, n2, gm, turned, n2t, gmt, snd, dn2, outv):
        def cols_of(j):
            return pl.ds(pl.multiple_of(j * chunk, chunk), chunk)

        def sub_of(j):
            return pl.ds(pl.multiple_of(lax.rem(j, per) * chunk, chunk), chunk)

        def mload(k, j, s):
            n = width // pieces
            return [
                pltpu.make_async_copy(
                    full.at[k, j, pl.ds(i * n, n)], mbuf.at[s, pl.ds(i * n, n)], msem.at[s, i])
                for i in range(pieces)]

        def depth(which):
            return mbuf.shape[0] // len(which)

        def ahead(which):
            for j in range(min(depth(which) - 1, count)):
                for n, k in enumerate(which):
                    fetch(mload(k, j, j * len(which) + n))

        def streamed(which, body):
            deep = depth(which)

            def one(j, carry):
                slots = [lax.rem(j, deep) * len(which) + n for n in range(len(which))]
                for n, k in enumerate(which):
                    settle(mload(k, j, slots[n]))

                @pl.when(j + deep - 1 < count)
                def _():
                    for n, k in enumerate(which):
                        fetch(mload(k, j + deep - 1, lax.rem(j + deep - 1, deep) * len(which) + n))

                body(j, *slots)
                return carry

            lax.fori_loop(0, count, one, 0)

        ahead((0,))
        loads[7].wait()

        def norm(r):
            value = xf[own_rows(r, tail)].astype(F32) + (mid[r] + rows12[5:6, :])
            mid[r] = value
            n2[r] = layer_norm(value, rows12[1:2, :], rows12[6:7, :]).astype(BF)
            branch = cot[r].astype(BF)
            gm[r] = branch
            sums[7:8, :] += column_sum(branch.astype(F32))

        loop_rows(rows, tail, norm)

        def turn(value, dst):
            turned[...] = value[...].T
            for i in range(ab):
                for other in range(2):
                    core = lax.rem(spot.c + other, 2)
                    dst[other, i * mrows:(i + 1) * mrows, :] = turned[pl.ds(pl.multiple_of((i * 2 + core) * mrows, mrows), mrows), :]

        downs.third()
        turn(gm, gmt)

        def sending(k, t):
            return wire.copy(zero[k] + t, snd.at[:, :, t], held.at[k, :, :, t], sibling)

        def give(k, j, left, right):
            product = nn(left[1], right).astype(BF)
            t = lax.div(j, per)
            for i in range(ab):
                snd[i // a_size, i % a_size, t, :, sub_of(j)] = product[i * mrows:(i + 1) * mrows, :]

            @pl.when(lax.rem(j, per) == per - 1)
            def _():
                sending(k, t).start()

        def keep(k, j, left, right):
            t = lax.div(j, per)

            @pl.when(lax.rem(j, per) == 0)
            def _():
                sending(k, t).wait_recv()

            product = nn(left[0], right)
            for i in range(ab):
                b, a = i // a_size, i % a_size
                held[k, b, a, t, :, sub_of(j)] = (
                    held[k, b, a, t, :, sub_of(j)].astype(F32) + product[i * mrows:(i + 1) * mrows, :]).astype(BF)

        def hidden(j, s):
            cols = cols_of(j)
            row = pl.ds(8 + lax.div(j * chunk, width), 1)
            bcols = pl.ds(pl.multiple_of(lax.rem(j * chunk, width), chunk), chunk)
            value, slope = gelu_parts(nn(n2[...], mbuf[s]) + rows12[row, bcols])
            active = value.astype(BF)
            hmid[:, cols] = active
            da[:, cols] = slope.astype(BF)
            give(1, j, gmt, active)

        streamed((0,), hidden)
        downs.fourth()
        ahead((0, 1))

        def keep_down(j, carry):
            keep(1, j, gmt, hmid[:, cols_of(j)])
            return carry

        lax.fori_loop(0, count, keep_down, 0)
        scatters[1].first()
        dn2[...] = jnp.zeros_like(dn2)
        outv[...] = jnp.zeros_like(outv)

        def hidden_back(j, s, s_down):
            cols = cols_of(j)
            row = pl.ds(8 + lax.div(j * chunk, width), 1)
            bcols = pl.ds(pl.multiple_of(lax.rem(j * chunk, width), chunk), chunk)
            grad = (nn(gm[...], mbuf[s_down]) * da[:, cols].astype(F32)).astype(BF)
            da[:, cols] = grad
            sums[row, bcols] = column_sum(grad.astype(F32))
            dn2[...] += nt(grad, mbuf[s])

        streamed((0, 1), hidden_back)

        def back(r):
            value = mid[r]
            unit_two, scale_two = norm_stats(value)
            grad = dn2[r]
            total = cot[r] + norm_back(grad, unit_two, scale_two, rows12[1:2, :])
            cot[r] = total
            branch = total.astype(BF)
            gaf[own_rows(r, tail)] = branch
            sums[1:2, :] += column_sum(grad * unit_two)
            sums[6:7, :] += column_sum(grad)
            sums[5:6, :] += column_sum(branch.astype(F32))

        loop_rows(rows, tail, back)
        wire.sent(blocks[0].plans())
        gas.start()
        turn(n2, n2t)
        for t in range(size):
            sending(1, t).wait_send()

        def give_up(j, carry):
            give(0, j, n2t, da[:, cols_of(j)])
            return carry

        lax.fori_loop(0, count, give_up, 0)

        def keep_up(j, carry):
            keep(0, j, n2t, da[:, cols_of(j)])
            return carry

        lax.fori_loop(0, count, keep_up, 0)
        ahead((1,))
        scatters[1].second()

        def output(j, s):
            outv[...] += nt(hmid[:, cols_of(j)], mbuf[s])

        streamed((1,), output)

        def set_out(r):
            outv[r] = mid[r] + (outv[r] + rows12[7:8, :])

        loop_rows(rows, tail, set_out)
        out_copy = pltpu.make_async_copy(outv, out_ref, osem.at[0])
        out_copy.start()
        for t in range(size):
            sending(0, t).wait_send()
        out_copy.wait()

    ff = size * unit
    pl.run_scoped(
        mlp,
        pltpu.VMEM((6, width, chunk), BF),
        pltpu.VMEM((rows, ff), BF),
        pltpu.VMEM((rows, ff), BF),
        pltpu.VMEM((rows, width), BF),
        pltpu.VMEM((rows, width), BF),
        pltpu.VMEM((width, rows), BF),
        pltpu.VMEM((2, ab * mrows, rows), BF),
        pltpu.VMEM((2, ab * mrows, rows), BF),
        pltpu.VMEM((b_size, a_size, size, mrows, unit), BF),
        pltpu.VMEM((rows, width), F32),
        pltpu.VMEM((rows, width), F32),
    )

    def attention(gat, do, dqkv, dk, dv, wg):
        def own_line(k, total):
            here = held.at[k, spot.b, spot.a, spot.t]

            def set_row(r):
                total[r] = here[r].astype(F32)

            loop_rows(mrows, tile, set_row)

        def down_total(ref, h):
            n = ref.shape[0]
            add_tiled(gtot.at[pl.ds(h * n, n)], ref, min(tile, n))

        def arrived(t):
            r = pl.ds(pl.multiple_of(t * rows, rows), rows)
            value = gaf[r]
            do[r] = nn(value, wf[3]).astype(BF)
            gat[:, r] = value.T

        dk[...] = jnp.zeros_like(dk)
        dv[...] = jnp.zeros_like(dv)

        def arrive_back(k, carry):
            @pl.when(k >= 1)
            def _():
                gas.step(k)

            @pl.when(k == 1)
            def _():
                scatters[1].third()
                lines[1].start()
                scatters[0].first()

            def side(i, inner):
                t = spot.t + (2 * i - 1) * k

                @pl.when((t >= 0) & (t < size) & ((i == 0) | (k >= 1)))
                def _():
                    arrived(t)

                return inner

            lax.fori_loop(0, 2, side, 0)
            for i in range(size):
                @pl.when((i == spot.t - k) | (i == spot.t + k))
                def _():
                    start, stop = i * rows, (i + 1) * rows
                    block_bias(seg_col, seg_row, bias, start, rows, stop)
                    attend_block_back(qkv, bias, lse, do, dqkv.at[0], dk, dv, start, rows)

            @pl.when(k == end - 1)
            def _():
                lines[1].step(0, lines[1].count() // 3, down_total)

            return carry

        lax.fori_loop(0, size, arrive_back, 0)
        gas.owe()
        own_line(1, gtot)
        half = width // 2
        dqkv[1] = dk[...].astype(BF)
        dqkv[2] = dv[...].astype(BF)
        order = []
        for i in range(size // 2):
            order += [end - i, i]
        for i in order:
            start, stop = i * rows, (i + 1) * rows
            for first in range(0, width, half):
                cols = slice(first, first + half)
                part[start:stop, cols] = sum(nt(dqkv[j, start:stop, :], wf[j, cols, :]) for j in range(3)).astype(BF)
            blocks[1].start_block(i)
        scatters[0].second()
        third = lines[1].count() // 3
        lines[1].step(third, 2 * third, down_total)
        loop_rows(rows, tail, lambda r: set_total(r))
        third = blocks[1].count() // 3
        blocks[1].step(0, third, mid_total)
        lines[1].step(2 * (lines[1].count() // 3), lines[1].count(), down_total)
        downg[...] = gtot[...].T
        def first_norm(r):
            unit_one, _ = norm_stats(xf[r].astype(F32))
            term = part[r].astype(F32)
            sums[0:1, :] += column_sum(term * unit_one)
            sums[2:3, :] += column_sum(term)

        loop_rows(seq, tail, first_norm)
        sums[3:4, column] = column_sum(dqkv[0].astype(F32))
        sums[4:5, column] = column_sum(dqkv[2].astype(F32))
        for d in range(geo.dp):
            spart[d] = sums[:, d * piece:(d + 1) * piece]
        for step in range(1, geo.dp):
            to = ring_next(spot.d, step, geo.dp)
            wire.start(small + step - 1, spart.at[to], sland.at[step - 1], spot.at_d(to))
        stot[...] = spart[spot.d]
        def wgrad(r):
            for j in range(3):
                wg[j, r] = nn(n1t[r], dqkv[j]).astype(BF)
            wg[3, r] = nn(gat[r], att[...]).astype(BF)

        loop_rows(width, min(256, width), wgrad)

        def wrows_of(i, core):
            return pl.ds(pl.multiple_of((i * 2 + core) * wrows, wrows), wrows)

        for i in range(ab):
            wire.start(wzero + i, wg.at[:, wrows_of(i, 1 - spot.c)], wheld.at[0, i // a_size, i % a_size], sibling)
        for i in range(ab):
            here = wheld.at[0, i // a_size, i % a_size]
            wire.landed(wzero + i, here, sibling)
            wscatter.add(here, wg.at[:, wrows_of(i, spot.c)])
        wscatter.first()
        blocks[1].step(third, 2 * third, mid_total)
        for step in range(1, geo.dp):
            wire.landed(small + step - 1, sland.at[step - 1], spot.at_d(ring_prev(spot.d, step, geo.dp)))
            stot[...] += sland[step - 1]
        for step in range(1, size):
            wire.start(last + step - 1, stot, tland.at[step - 1], spot.at_t(ring_next(spot.t, step, size)))
        scatters[0].third()
        lines[0].start()
        stores = fetch([pltpu.make_async_copy(downg, downg_ref, osem.at[1])])
        own_line(0, gtot)
        wscatter.second()
        blocks[1].step(2 * third, blocks[1].count(), mid_total)

        def back(r):
            unit_one, scale_one = norm_stats(xf[own_rows(r, tail)].astype(F32))
            cot[r] = cot[r] + norm_back(mid[r], unit_one, scale_one, rows12[0:1, :])

        loop_rows(rows, tail, back)
        stores += fetch([pltpu.make_async_copy(cot, igrad_ref, osem.at[0])])
        events = lines[0].count()
        lines[0].step(0, events // 3, down_total)
        wscatter.third()
        lines[0].step(events // 3, 2 * events // 3, down_total)
        sums_w = wheld.at[0, spot.b, spot.a]
        for j in range(3):
            awg[j] = sums_w[j].astype(F32)
        owg[...] = sums_w[3].astype(F32).T
        for step in range(1, size):
            wire.landed(last + step - 1, tland.at[step - 1], spot.at_t(ring_prev(spot.t, step, size)))
        total = stot[...]
        for step in range(1, size):
            total = total + tland[step - 1]
        gaing[...] = total[0:2, :]
        for i in range(biasg.shape[0]):
            biasg[i] = total[2 + i:3 + i, :]
        stores += fetch([
            pltpu.make_async_copy(awg, awg_ref, osem.at[2]),
            pltpu.make_async_copy(owg, owg_ref, osem.at[3]),
            pltpu.make_async_copy(gaing, gaing_ref, osem.at[4]),
            pltpu.make_async_copy(biasg, biasg_ref, osem.at[5])])
        lines[0].step(2 * events // 3, events, down_total)
        stores += fetch([pltpu.make_async_copy(gtot, upg_ref, osem.at[6])])
        wire.drain()
        settle(stores)

    pl.run_scoped(
        attention,
        pltpu.VMEM((width, seq), BF),
        pltpu.VMEM((seq, heads), BF),
        pltpu.VMEM((3, seq, heads), BF),
        pltpu.VMEM((seq, heads), F32),
        pltpu.VMEM((seq, heads), F32),
        pltpu.VMEM((4, width, heads), BF),
    )


def block_kernel(geo, x, aw, ow, up, down, gains, biases, seg_row, cot):
    rows, width = x.shape
    wrows, heads = aw.shape[1:]
    mrows, unit = up.shape
    size = geo.tensor
    seq = size * rows
    chunk = min(512, unit)
    sems = 3 * gather_sems(geo) + 48 * size + 3 * scatter_sems(geo) + geo.a_size * geo.b_size + 2 * geo.dp
    like = lambda x: pltpu.VMEM(x.shape, x.dtype)
    return pl.pallas_call(
        functools.partial(block_body, geo),
        out_shape=(
            jax.ShapeDtypeStruct((2, size * (unit // chunk), width, chunk), BF),
            jax.ShapeDtypeStruct((rows, width), F32),
            jax.ShapeDtypeStruct((rows, width), F32),
            jax.ShapeDtypeStruct((3, wrows, heads), F32),
            jax.ShapeDtypeStruct((heads, wrows), F32),
            jax.ShapeDtypeStruct((mrows, unit), F32),
            jax.ShapeDtypeStruct((unit, mrows), F32),
            jax.ShapeDtypeStruct((2, wrows), F32),
            jax.ShapeDtypeStruct((10, 1, wrows), F32),
        ),
        in_specs=[ANY] * 9,
        out_specs=(ANY,) * 9,
        scratch_shapes=[
            pltpu.VMEM((seq, width), BF),
            pltpu.VMEM((seq, width), BF),
            pltpu.VMEM((width, seq), BF),
            pltpu.VMEM((3, seq, heads), BF),
            pltpu.VMEM((seq, heads), BF),
            pltpu.VMEM((seq, 128), F32),
            pltpu.VMEM((4, width, heads), BF),
            pltpu.VMEM((seq, width), BF),
            pltpu.VMEM((2, size - 1, rows, width), BF),
            pltpu.VMEM((rows, seq), F32),
            pltpu.VMEM((rows, width), F32),
            pltpu.VMEM((rows, width), F32),
            pltpu.VMEM((seq, width), BF),
            pltpu.VMEM((12, width), F32),
            pltpu.VMEM((seq, 128), jnp.int32),
            like(seg_row),
            pltpu.VMEM((geo.dp, 12, wrows), F32),
            pltpu.VMEM((4, wrows, heads), BF),
            like(ow), like(down), pltpu.VMEM((2, unit // chunk, mrows, chunk), BF), like(gains), like(biases),
            pltpu.VMEM((12, wrows), F32),
            pltpu.VMEM((12, width), F32),
            pltpu.VMEM((geo.dp, 12, wrows), F32),
            pltpu.VMEM((geo.dp - 1, 12, wrows), F32),
            pltpu.VMEM((12, wrows), F32),
            pltpu.VMEM((size - 1, 12, wrows), F32),
            *scatter_bufs(geo, 2, size, mrows, unit),
            *scatter_bufs(geo, 1, 4, wrows, heads),
            pltpu.VMEM((2, 2, size - 1, mrows, unit), BF),
            pltpu.VMEM((mrows, unit), F32),
            pltpu.VMEM((unit, mrows), F32),
            pltpu.VMEM((3, wrows, heads), F32),
            pltpu.VMEM((heads, wrows), F32),
            pltpu.VMEM((2, wrows), F32),
            pltpu.VMEM((10, 1, wrows), F32),
            pltpu.SemaphoreType.DMA((sems,)), pltpu.SemaphoreType.DMA((sems,)), pltpu.SemaphoreType.DMA((8 + unit // chunk,)),
            pltpu.SemaphoreType.DMA((6, 2)), pltpu.SemaphoreType.DMA((7,))],
        compiler_params=pltpu.CompilerParams(collective_id=1, has_side_effects=True, vmem_limit_bytes=61 * 2**20),
        name="block",
    )(x, aw, ow, up, down, gains, biases, seg_row, cot)


def hand_over_body(*refs):
    *refs, loads, stores = refs
    count = len(refs) // 3
    ins, outs, bufs = refs[:count], refs[count:2 * count], refs[2 * count:]
    coming = fetch([pltpu.make_async_copy(ins[i], bufs[i], loads.at[i]) for i in range(count)])
    going = []
    for i in range(count):
        coming[i].wait()
        going += fetch([pltpu.make_async_copy(bufs[i], outs[i], stores.at[i])])
    settle(going)


def hand_over(parts):
    return pl.pallas_call(
        hand_over_body,
        out_shape=tuple(jax.ShapeDtypeStruct(part.shape, part.dtype) for part in parts),
        in_specs=[ANY] * len(parts),
        out_specs=(ANY,) * len(parts),
        scratch_shapes=[pltpu.VMEM(part.shape, part.dtype) for part in parts] + [pltpu.SemaphoreType.DMA((len(parts),))] * 2,
        name="hand_over",
    )(*parts)


def per_device(geo, activations, segments, attn_weight, out_weight, up_weight, down_weight, norm_gains, bias_rows, cotangent):
    outs = block_kernel(
        geo, activations, attn_weight[0], out_weight[0], up_weight[0], down_weight[0], norm_gains[0], bias_rows[0], segments[None, :],
        cotangent)
    outs = hand_over(outs[1:])
    return outs[:2] + tuple(part[None] for part in outs[2:7]) + (outs[7].reshape(1, 10, -1),)


def solution(mesh):
    geo = Geometry(mesh.shape["dp"], mesh.shape["tensor"])
    return jax.shard_map(
        functools.partial(per_device, geo),
        mesh=mesh,
        in_specs=(
            P(("dp", "tensor"), None),
            P("dp"),
            P(None, None, "dp", "tensor"),
            P(None, "tensor", "dp"),
            P(None, "dp", "tensor"),
            P(None, "tensor", "dp"),
            P(None, None, "dp"),
            P(None, None, "dp"),
            P(("dp", "tensor"), None),
        ),
        out_specs=(
            P(("dp", "tensor"), None),
            P(("dp", "tensor"), None),
            P(None, None, "dp", "tensor"),
            P(None, "tensor", "dp"),
            P(None, "dp", "tensor"),
            P(None, "tensor", "dp"),
            P(None, None, "dp"),
            P(None, None, "dp"),
        ),
        check_vma=False,
    )
```

time: 305 us -> 246 us (0.81)
  Pallas kernels: 296 us -> 245 us
  local copies, waits for them, and re-layouts: 8.29 us -> 0 us
    pallas_call x2, Pallas kernels: 296 us -> 245 us  [the longest x1 241 us: block_kernel(): pl.pallas_call(functools.partial(block_body, geo), out_shape=(jax.ShapeDt...]
    unnamed x20 -> x0, local copies, waits for them, and re-layouts: 8.29 us -> none
where the time goes in v2:
time: 246 us; the launch traced here: 245 us
  Pallas kernels  245 us (100%)
    pallas_call x1, Pallas kernels, block_kernel(): pl.pallas_call(functools.partial(block_body, geo), out_shape=(jax.ShapeDt...  241 us

profile of v2, /device:TPU:0, one launch (start us, length us, event | category | flops | bytes accessed | tf_op | source)
XLA Modules:
  0.0 245.4 jit_solution(12917382796534352588)
XLA Ops:
  0.6 241.4 %block.1 = (bf16[2,8,1024,512]{3,2,1,0:T(8,128)(2,1)}, f32[256,1024]{1,0:T(8,128)}, f32[256,1024]{1,0:T(8,128)}, f32[3,128,256]{2,1,0:T(8,128)}, f32[256,128]{1,...) custom-call(bf16[256,1024]{1,0:T(8,128)(2,1)} %x_ref.1, ...), custom_call_target="tpu_custom_call" | custom-call | tf_op jit(solution)/shard_map/block/pallas_call | solution.py:1147
  242.0 3.2 %hand_over.1 = (f32[256,1024]{1,0:T(8,128)}, f32[256,1024]{1,0:T(8,128)}, f32[3,128,256]{2,1,0:T(8,128)}, f32[256,128]{1,0:T(8,128)}, f32[128,1024]{1,0:T(8,128)...) custom-call(f32[256,1024]{1,0:T(8,128)} %get-tuple-element.24.refs_0_, ...), custom_call_target="tpu_custom_call" | custom-call | tf_op jit(solution)/shard_map/hand_over/pallas_call | solution.py:1217

commit v3 on v2

--- a/solution.py
+++ b/solution.py
@@ -108,6 +108,9 @@
             copy.start()
         else:
             pl.when(when)(copy.start)
+        self.owe(planned)
+
+    def owe(self, planned):
         if not any(other is planned for other in self.pending):
             self.pending.append(planned)
 
@@ -203,32 +206,36 @@
     def owe(self):
         for (k, part, side), planned in self.sends.items():
             if k > 0:
-                self.wire.pending.append(planned)
+                self.wire.owe(planned)
 
 
 class LineScatter:
-    def __init__(self, spot, wire, part, land, add, rising=False, parts=2):
+    def __init__(self, spot, wire, part, land, add, rising=None, parts=2):
         self.spot, self.wire, self.part, self.land, self.add, self.parts = spot, wire, part, land, add, parts
         self.size = spot.geo.tensor
-        base = [wire.take(self.size * parts) for _ in range(2)]
+        base = self.base = [wire.take((self.size - 1) * parts) for _ in range(2)]
         t, end = spot.t, self.size - 1
         self.starts, self.hops = {}, {}
         for h in range(parts):
             for j in range(self.size):
                 if j > 0:
                     self.starts[0, j, h] = wire.plan(
-                        base[0] + j * parts + h, halves(part(j), parts, h), halves(land(0, j), parts, h), spot.at_t(1), when=t == 0)
+                        base[0] + (j - 1) * parts + h, halves(part(j), parts, h), halves(land(0, j), parts, h), spot.at_t(1), when=t == 0)
                 if j < end:
                     self.starts[1, j, h] = wire.plan(
                         base[1] + j * parts + h, halves(part(j), parts, h), halves(land(1, j), parts, h), spot.at_t(end - 1), when=t == end)
         self.events = []
-        if rising:
-            for e in range(1, 2 * end):
-                self.events.append((10 * e, 0, e + 1 - t, (t >= 1) & (e + 1 - t >= t) & (e + 1 - t <= end)))
-        for s in range(1, self.size):
-            if not rising:
-                self.events.append((10 * s, 0, end - s + t, (t >= 1) & (s >= t)))
-            self.events.append((10 * s + (15 if rising else 0), 1, s - (end - t), (end - t >= 1) & (s >= end - t)))
+        for side in range(2):
+            place = t if side == 0 else end - t
+            if side == rising:
+                for e in range(1, 2 * end):
+                    far = e + 1 - place
+                    self.events.append((10 * e, side, far if side == 0 else end - far, (place >= 1) & (far >= place) & (far <= end)))
+            else:
+                for s in range(1, self.size):
+                    far = end - s + place
+                    at = 10 * s + (0 if rising is None else 15)
+                    self.events.append((at, side, far if side == 0 else end - far, (place >= 1) & (s >= place)))
         self.events.sort(key=lambda event: event[0])
         self.hops = []
         for _, side, j, here in self.events:
@@ -236,7 +243,7 @@
             away = spot.at_t(t + 1 if side == 0 else t - 1)
             for h in range(parts):
                 held = halves(land(side, j), parts, h)
-                i = base[side] + j * parts + h
+                i = base[side] + (j - 1 + side) * parts + h
                 self.hops.append((here & (j == t), here & (j != t), j, h, held, wire.copy(i, held, held, near),
                                   wire.plan(i, held, held, away, when=here & (j != t))))
 
@@ -245,6 +252,20 @@
             for h in range(self.parts):
                 if (side, j, h) in self.starts:
                     self.wire.go(self.starts[side, j, h])
+
+    def start_traced(self, j):
+        spot, t, end = self.spot, self.spot.t, self.size - 1
+        for side in range(2):
+            first, to = (0, 1) if side == 0 else (end, end - 1)
+            for h in range(self.parts):
+                copy, when = self.wire.plan(
+                    self.base[side] + (j - 1 + side) * self.parts + h, halves(self.part(j), self.parts, h),
+                    halves(self.land(side, j), self.parts, h), spot.at_t(to), when=(t == first) & (j != first))
+                pl.when(when)(copy.start)
+
+    def owe_starts(self):
+        for planned in self.starts.values():
+            self.wire.owe(planned)
 
     def start(self):
         for n in range(self.size):
@@ -392,7 +413,7 @@
 
 
 def gather_sems(geo):
-    return geo.a_size + geo.b_size + 4 * geo.a_size * geo.b_size
+    return geo.a_size + geo.b_size - 2 + (geo.b_size - 1) * geo.a_size + (geo.a_size - 1) * geo.b_size + 2 * geo.a_size * geo.b_size
 
 
 class WeightScatter:
@@ -464,17 +485,17 @@
 
 
 def scatter_sems(geo):
-    return 2 * geo.a_size + 2 * geo.b_size
-
-
-def scatter_bufs(geo, n, slots, rows, width):
+    return 2 * (geo.a_size + geo.b_size - 2)
+
+
+def scatter_bufs(geo, n, sets, slots, rows, width):
     a, b, half = geo.a_size, geo.b_size, slots // 2
     return [
         pltpu.VMEM((n, b, a, slots, rows, width), BF),
-        pltpu.VMEM((a - 1, b, half, rows, width), BF),
-        pltpu.VMEM((b - 1, a, half, rows, width), BF),
-        pltpu.VMEM((b - 1, half, rows, width), BF),
-        pltpu.VMEM((a - 1, half, rows, width), BF),
+        pltpu.VMEM((sets, a - 1, b, half, rows, width), BF),
+        pltpu.VMEM((sets, b - 1, a, half, rows, width), BF),
+        pltpu.VMEM((sets, b - 1, half, rows, width), BF),
+        pltpu.VMEM((sets, a - 1, half, rows, width), BF),
     ]
 
 
@@ -629,27 +650,33 @@
         return pl.ds(pl.multiple_of(spot.t * rows + r.start, n), n)
 
     weights = WeightGather(spot, wire, wrows, wf)
-    wlines = [LineGather(spot, wire, msend.at[k], lambda t, k=k: full.at[k, pl.ds(t * per, per), mspan]) for k in range(2)]
-    ups, downs = [WeightGather(spot, wire, mrows, full.at[k]) for k in range(2)]
+    halved = [(k, p) for k in range(2) for p in range(per)]
+    wlines, gathers = {}, {}
+    for k, p in halved:
+        wlines[k, p] = LineGather(spot, wire, msend.at[k, p], lambda t, k=k, p=p: full.at[k, p, t, mspan], parts=1)
+        gathers[k, p] = WeightGather(spot, wire, mrows, full.at[k, p])
     xs = LineGather(spot, wire, x_ref, lambda t: block_of(xf, t))
     gas = LineGather(spot, wire, block_of(gaf, spot.t), lambda t: block_of(gaf, t))
     blocks = [
         LineScatter(spot, wire, lambda t: block_of(part, t), lambda side, j: land.at[side, j - 1 + side],
-                    lambda dst, src: add_tiled(dst, src, tail), rising=k == 0) for k in range(2)]
-    scatters = [WeightScatter(spot, wire, held.at[k], one_a, one_b, two_a, two_b) for k in range(2)]
-    wscatter = WeightScatter(spot, wire, wheld.at[0], wone_a, wone_b, wtwo_a, wtwo_b)
-
-    def line_of(k):
-        here = held.at[k, spot.b, spot.a]
-        return LineScatter(spot, wire, lambda t: here.at[t], lambda side, j: mland.at[k, side, j - 1 + side],
-                           lambda dst, src: add_tiled(dst, src, min(64, mrows // 2)))
-
-    lines = [line_of(k) for k in range(2)]
-    zero = [wire.take(size) for _ in range(2)]
+                    lambda dst, src: add_tiled(dst, src, tail), rising=k) for k in range(2)]
+    scatters, lines = {}, {}
+
+    def line_of(k, p):
+        here = held.at[k * per + p, spot.b, spot.a]
+        return LineScatter(spot, wire, lambda t: here.at[t], lambda side, j: mland.at[k * per + p, side, j - 1 + side],
+                           lambda dst, src: add_tiled(dst, src, tile), parts=1)
+
+    for k, p in halved:
+        scatters[k, p] = WeightScatter(spot, wire, held.at[k * per + p], *(buf.at[k * per + p] for buf in (one_a, one_b, two_a, two_b)))
+        lines[k, p] = line_of(k, p)
+    wscatter = WeightScatter(spot, wire, wheld.at[0], wone_a.at[0], wone_b.at[0], wtwo_a.at[0], wtwo_b.at[0])
+    zero = [wire.take(count) for _ in range(2)]
     wzero = wire.take(ab)
     gains_in = wire.take(geo.dp - 1)
     small = wire.take(geo.dp - 1)
     last = wire.take(size - 1)
+    assert wire.count == send.shape[0]
 
     pairs = [
         (gain_ref, gain_in), (bias_ref, bias_in), (aw_ref, wsend.at[pl.ds(0, 3)]), (ow_ref, ow_in),
@@ -667,11 +694,12 @@
     settle(loads[8:])
 
     def store(k):
-        return pltpu.make_async_copy(msend.at[k], full.at[k, pl.ds(spot.t * per, per), mspan], osem.at[k])
+        return pltpu.make_async_copy(msend.at[k], full.at[k, :, spot.t, mspan], osem.at[k])
 
     store(0).start()
     met()
-    wlines[0].start()
+    for p in range(per):
+        wlines[0, p].start()
     for step in range(1, geo.dp):
         wire.start(gains_in + step - 1, ssend, sf.at[spot.d], spot.at_d(ring_next(spot.d, step, geo.dp)))
     weights.first()
@@ -679,15 +707,17 @@
     for i in range(per):
         msend[1, i] = down_in[i * chunk:(i + 1) * chunk, :].T
     store(1).start()
-    wlines[0].step(1)
-    weights.second()
-    for k in range(2, size - 1):
-        wlines[0].step(k)
+    for k in range(1, end):
+        for p in range(per):
+            wlines[0, p].step(k)
+        if k == 1:
+            weights.second()
     xs.start()
     weights.third()
     store(0).wait()
-    wlines[0].step(end)
-    ups.first()
+    for p in range(per):
+        wlines[0, p].step(end)
+        gathers[0, p].first()
     for step in range(1, geo.dp):
         source = ring_prev(spot.d, step, geo.dp)
         wire.landed(gains_in + step - 1, sf.at[source], spot.at_d(source))
@@ -701,12 +731,13 @@
 
     def project(t):
         def norm(r):
-            n1[r] = layer_norm(xf[r].astype(F32), rows12[0:1, :], rows12[2:3, :]).astype(BF)
-
-        first = pl.multiple_of(t * rows, rows)
-        loop_rows(rows, tail, norm, first)
-        r = pl.ds(first, rows)
-        normed = n1[r]
+            source = pl.ds(pl.multiple_of(t * rows + r.start, tail), tail)
+            n1[r] = layer_norm(xf[source].astype(F32), rows12[0:1, :], rows12[2:3, :]).astype(BF)
+
+        loop_rows(rows, tail, norm)
+        r = pl.ds(pl.multiple_of(t * rows, rows), rows)
+        normed = n1[...]
+        n1t[:, r] = normed.T
         qkv[0, r] = ((nn(normed, wf[0]) + rows12[3:4, column]).astype(BF).astype(F32) * HD ** -0.5).astype(BF)
         qkv[1, r] = nn(normed, wf[1]).astype(BF)
         qkv[2, r] = (nn(normed, wf[2]) + rows12[4:5, column]).astype(BF)
@@ -718,7 +749,8 @@
 
         @pl.when(k == end - 1)
         def _():
-            wlines[1].start()
+            for p in range(per):
+                wlines[1, p].start()
 
         def side(i, inner):
             t = spot.t + (2 * i - 1) * k
@@ -733,12 +765,8 @@
 
         @pl.when(k == 1)
         def _():
-            ups.second()
-
-        @pl.when(k == end)
-        def _():
-            wlines[1].step(1)
-            ups.third()
+            for p in range(per):
+                gathers[0, p].second()
 
         for i in range(size):
             start = i * rows
@@ -750,22 +778,20 @@
                 part[start:start + rows, :] = nt(att[start:start + rows, :], wf[3]).astype(BF)
                 blocks[0].start_block(i)
 
-            if i == 1:
-                @pl.when(k == end)
-                def _():
-                    wlines[1].step(2)
-
         return carry
 
     lax.fori_loop(0, size, arrive, 0)
     xs.owe()
-    for k in range(3, size):
-        wlines[1].step(k)
+    for k in range(1, end):
+        for p in range(per):
+            wlines[1, p].step(k)
+        if k == 1:
+            for p in range(per):
+                gathers[0, p].third()
     store(1).wait()
-    downs.first()
-    for i in range(size):
-        n1t[:, i * rows:(i + 1) * rows] = n1[i * rows:(i + 1) * rows, :].T
-
+    for p in range(per):
+        wlines[1, p].step(end)
+        gathers[1, p].first()
     def set_total(r):
         mid[r] = part[own_rows(r, tail)].astype(F32)
 
@@ -776,23 +802,27 @@
         add_tiled(mid.at[pl.ds(h * n, n)], ref, tail)
 
     events = blocks[0].count()
-    blocks[0].step(0, events // 2, mid_total)
-    ups.fourth()
-    downs.second()
-    blocks[0].step(events // 2, events, mid_total)
-
-    def mlp(mbuf, hmid, da, n2, gm, turned, n2t, gmt, snd, dn2, outv):
+    blocks[0].step(0, 3 * events // 8, mid_total)
+    gathers[1, 0].second()
+    blocks[0].step(3 * events // 8, 5 * events // 8, mid_total)
+    for p in range(per):
+        gathers[0, p].fourth()
+    for p in range(1, per):
+        gathers[1, p].second()
+    blocks[0].step(5 * events // 8, events, mid_total)
+
+    def mlp(mbuf, hmid, da, n2, gm, turned, left, snd, dn2):
         def cols_of(j):
-            return pl.ds(pl.multiple_of(j * chunk, chunk), chunk)
-
-        def sub_of(j):
-            return pl.ds(pl.multiple_of(lax.rem(j, per) * chunk, chunk), chunk)
+            return pl.ds(pl.multiple_of(unit_of(j) * chunk, chunk), chunk)
+
+        def unit_of(j):
+            return lax.rem(j, size) * per + lax.div(j, size)
 
         def mload(k, j, s):
             n = width // pieces
             return [
                 pltpu.make_async_copy(
-                    full.at[k, j, pl.ds(i * n, n)], mbuf.at[s, pl.ds(i * n, n)], msem.at[s, i])
+                    full.at[k, lax.div(j, size), lax.rem(j, size), pl.ds(i * n, n)], mbuf.at[s, pl.ds(i * n, n)], msem.at[s, i])
                 for i in range(pieces)]
 
         def depth(which):
@@ -803,7 +833,7 @@
                 for n, k in enumerate(which):
                     fetch(mload(k, j, j * len(which) + n))
 
-        def streamed(which, body):
+        def streamed(which, body, first=0, stop=count):
             deep = depth(which)
 
             def one(j, carry):
@@ -819,7 +849,7 @@
                 body(j, *slots)
                 return carry
 
-            lax.fori_loop(0, count, one, 0)
+            lax.fori_loop(first, stop, one, 0)
 
         ahead((0,))
         loads[7].wait()
@@ -834,69 +864,63 @@
 
         loop_rows(rows, tail, norm)
 
-        def turn(value, dst):
+        def turn(value):
             turned[...] = value[...].T
             for i in range(ab):
                 for other in range(2):
                     core = lax.rem(spot.c + other, 2)
-                    dst[other, i * mrows:(i + 1) * mrows, :] = turned[pl.ds(pl.multiple_of((i * 2 + core) * mrows, mrows), mrows), :]
-
-        downs.third()
-        turn(gm, gmt)
-
-        def sending(k, t):
-            return wire.copy(zero[k] + t, snd.at[:, :, t], held.at[k, :, :, t], sibling)
-
-        def give(k, j, left, right):
+                    left[other, i * mrows:(i + 1) * mrows, :] = turned[pl.ds(pl.multiple_of((i * 2 + core) * mrows, mrows), mrows), :]
+
+        turn(gm)
+
+        def sending(k, j):
+            p, t = lax.div(j, size), lax.rem(j, size)
+            return wire.copy(zero[k] + j, snd.at[p, :, :, t], held.at[k * per + p, :, :, t], sibling)
+
+        def give(k, j, right):
             product = nn(left[1], right).astype(BF)
-            t = lax.div(j, per)
+            p, t = lax.div(j, size), lax.rem(j, size)
             for i in range(ab):
-                snd[i // a_size, i % a_size, t, :, sub_of(j)] = product[i * mrows:(i + 1) * mrows, :]
-
-            @pl.when(lax.rem(j, per) == per - 1)
-            def _():
-                sending(k, t).start()
-
-        def keep(k, j, left, right):
-            t = lax.div(j, per)
-
-            @pl.when(lax.rem(j, per) == 0)
-            def _():
-                sending(k, t).wait_recv()
-
+                snd[p, i // a_size, i % a_size, t] = product[i * mrows:(i + 1) * mrows, :]
+            sending(k, j).start()
+
+        def keep(k, j, right):
+            p, t = lax.div(j, size), lax.rem(j, size)
             product = nn(left[0], right)
+            sending(k, j).wait_recv()
             for i in range(ab):
                 b, a = i // a_size, i % a_size
-                held[k, b, a, t, :, sub_of(j)] = (
-                    held[k, b, a, t, :, sub_of(j)].astype(F32) + product[i * mrows:(i + 1) * mrows, :]).astype(BF)
+                held[k * per + p, b, a, t] = (
+                    held[k * per + p, b, a, t].astype(F32) + product[i * mrows:(i + 1) * mrows, :]).astype(BF)
 
         def hidden(j, s):
             cols = cols_of(j)
-            row = pl.ds(8 + lax.div(j * chunk, width), 1)
-            bcols = pl.ds(pl.multiple_of(lax.rem(j * chunk, width), chunk), chunk)
+            row = pl.ds(8 + lax.div(unit_of(j) * chunk, width), 1)
+            bcols = pl.ds(pl.multiple_of(lax.rem(unit_of(j) * chunk, width), chunk), chunk)
             value, slope = gelu_parts(nn(n2[...], mbuf[s]) + rows12[row, bcols])
             active = value.astype(BF)
             hmid[:, cols] = active
             da[:, cols] = slope.astype(BF)
-            give(1, j, gmt, active)
-
-        streamed((0,), hidden)
-        downs.fourth()
+            give(1, j, active)
+
+        def keep_down(j, carry):
+            keep(1, j, hmid[:, cols_of(j)])
+            return carry
+
+        for p in range(per):
+            streamed((0,), hidden, p * size, (p + 1) * size)
+            gathers[1, p].third()
+            lax.fori_loop(p * size, (p + 1) * size, keep_down, 0)
+            scatters[1, p].first()
+        for p in range(per):
+            gathers[1, p].fourth()
         ahead((0, 1))
-
-        def keep_down(j, carry):
-            keep(1, j, gmt, hmid[:, cols_of(j)])
-            return carry
-
-        lax.fori_loop(0, count, keep_down, 0)
-        scatters[1].first()
         dn2[...] = jnp.zeros_like(dn2)
-        outv[...] = jnp.zeros_like(outv)
 
         def hidden_back(j, s, s_down):
             cols = cols_of(j)
-            row = pl.ds(8 + lax.div(j * chunk, width), 1)
-            bcols = pl.ds(pl.multiple_of(lax.rem(j * chunk, width), chunk), chunk)
+            row = pl.ds(8 + lax.div(unit_of(j) * chunk, width), 1)
+            bcols = pl.ds(pl.multiple_of(lax.rem(unit_of(j) * chunk, width), chunk), chunk)
             grad = (nn(gm[...], mbuf[s_down]) * da[:, cols].astype(F32)).astype(BF)
             da[:, cols] = grad
             sums[row, bcols] = column_sum(grad.astype(F32))
@@ -919,37 +943,46 @@
         loop_rows(rows, tail, back)
         wire.sent(blocks[0].plans())
         gas.start()
-        turn(n2, n2t)
-        for t in range(size):
-            sending(1, t).wait_send()
-
+        turn(n2)
         def give_up(j, carry):
-            give(0, j, n2t, da[:, cols_of(j)])
+            sending(1, j).wait_send()
+            give(0, j, da[:, cols_of(j)])
             return carry
 
         lax.fori_loop(0, count, give_up, 0)
+        scatters[1, 0].second()
 
         def keep_up(j, carry):
-            keep(0, j, n2t, da[:, cols_of(j)])
+            keep(0, j, da[:, cols_of(j)])
             return carry
 
-        lax.fori_loop(0, count, keep_up, 0)
+        for p in range(per):
+            lax.fori_loop(p * size, (p + 1) * size, keep_up, 0)
+            if p:
+                scatters[1, p].second()
         ahead((1,))
-        scatters[1].second()
+        gas.step(1)
+        scatters[1, 0].third()
+        lines[1, 0].start()
+        scatters[0, 0].first()
+        dn2[...] = jnp.zeros_like(dn2)
 
         def output(j, s):
-            outv[...] += nt(hmid[:, cols_of(j)], mbuf[s])
+            dn2[...] += nt(hmid[:, cols_of(j)], mbuf[s])
 
         streamed((1,), output)
 
         def set_out(r):
-            outv[r] = mid[r] + (outv[r] + rows12[7:8, :])
+            dn2[r] = mid[r] + (dn2[r] + rows12[7:8, :])
 
         loop_rows(rows, tail, set_out)
-        out_copy = pltpu.make_async_copy(outv, out_ref, osem.at[0])
+        out_copy = pltpu.make_async_copy(dn2, out_ref, osem.at[0])
         out_copy.start()
-        for t in range(size):
-            sending(0, t).wait_send()
+        for p in range(1, per):
+            scatters[1, p].third()
+            lines[1, p].start()
+        for j in range(count):
+            sending(0, j).wait_send()
         out_copy.wait()
 
     ff = size * unit
@@ -962,24 +995,26 @@
         pltpu.VMEM((rows, width), BF),
         pltpu.VMEM((width, rows), BF),
         pltpu.VMEM((2, ab * mrows, rows), BF),
-        pltpu.VMEM((2, ab * mrows, rows), BF),
-        pltpu.VMEM((b_size, a_size, size, mrows, unit), BF),
-        pltpu.VMEM((rows, width), F32),
+        pltpu.VMEM((per, b_size, a_size, size, mrows, chunk), BF),
         pltpu.VMEM((rows, width), F32),
     )
 
     def attention(gat, do, dqkv, dk, dv, wg):
-        def own_line(k, total):
-            here = held.at[k, spot.b, spot.a, spot.t]
-
-            def set_row(r):
-                total[r] = here[r].astype(F32)
-
-            loop_rows(mrows, tile, set_row)
-
-        def down_total(ref, h):
-            n = ref.shape[0]
-            add_tiled(gtot.at[pl.ds(h * n, n)], ref, min(tile, n))
+        def own_line(k):
+            for p in range(per):
+                here = held.at[k * per + p, spot.b, spot.a, spot.t]
+
+                def set_row(r):
+                    gtot[r, p * chunk:(p + 1) * chunk] = here[r].astype(F32)
+
+                loop_rows(mrows, tile, set_row)
+
+        def line_total(p):
+            return lambda ref, h: add_tiled(gtot.at[:, pl.ds(p * chunk, chunk)], ref, tile)
+
+        def line_step(k, p, s):
+            third = lines[k, p].count() // 3
+            lines[k, p].step(s * third, (s + 1) * third, line_total(p))
 
         def arrived(t):
             r = pl.ds(pl.multiple_of(t * rows, rows), rows)
@@ -990,16 +1025,37 @@
         dk[...] = jnp.zeros_like(dk)
         dv[...] = jnp.zeros_like(dv)
 
+        half = width // 2
+
+        def norm_grad(i):
+            r = pl.ds(pl.multiple_of(i * rows, rows), rows)
+            dqkv[1, r] = dk[r].astype(BF)
+            dqkv[2, r] = dv[r].astype(BF)
+            for first in range(0, width, half):
+                cols = slice(first, first + half)
+                part[r, cols] = sum(nt(dqkv[j, r], wf[j, cols, :]) for j in range(3)).astype(BF)
+            blocks[1].start_traced(i)
+
+        plan = {(1, p, n): n + 1 + p for p in range(per) for n in range(end - 1)}
+        plan = {key: at for key, at in plan.items() if at < size}
+
         def arrive_back(k, carry):
-            @pl.when(k >= 1)
+            for n in range(1, size):
+                @pl.when(k == n)
+                def _():
+                    if n == 1 and size > 2:
+                        gas.step(2)
+                    for key, at in plan.items():
+                        if at == n:
+                            line_step(*key)
+                    if n == end:
+                        scatters[0, 0].second()
+                        for p in range(1, per):
+                            scatters[0, p].first()
+
+            @pl.when(k >= 3)
             def _():
                 gas.step(k)
-
-            @pl.when(k == 1)
-            def _():
-                scatters[1].third()
-                lines[1].start()
-                scatters[0].first()
 
             def side(i, inner):
                 t = spot.t + (2 * i - 1) * k
@@ -1018,35 +1074,33 @@
                     block_bias(seg_col, seg_row, bias, start, rows, stop)
                     attend_block_back(qkv, bias, lse, do, dqkv.at[0], dk, dv, start, rows)
 
-            @pl.when(k == end - 1)
-            def _():
-                lines[1].step(0, lines[1].count() // 3, down_total)
-
+            def ready(n, inner):
+                i = jnp.where(lax.rem(n, 2) == 0, end - lax.div(n, 2), lax.div(n, 2))
+
+                @pl.when(jnp.maximum(end - spot.t, spot.t - i) == k)
+                def _():
+                    norm_grad(i)
+
+                return inner
+
+            lax.fori_loop(0, size, ready, 0)
             return carry
 
         lax.fori_loop(0, size, arrive_back, 0)
         gas.owe()
-        own_line(1, gtot)
-        half = width // 2
-        dqkv[1] = dk[...].astype(BF)
-        dqkv[2] = dv[...].astype(BF)
-        order = []
-        for i in range(size // 2):
-            order += [end - i, i]
-        for i in order:
-            start, stop = i * rows, (i + 1) * rows
-            for first in range(0, width, half):
-                cols = slice(first, first + half)
-                part[start:stop, cols] = sum(nt(dqkv[j, start:stop, :], wf[j, cols, :]) for j in range(3)).astype(BF)
-            blocks[1].start_block(i)
-        scatters[0].second()
-        third = lines[1].count() // 3
-        lines[1].step(third, 2 * third, down_total)
+        blocks[1].owe_starts()
         loop_rows(rows, tail, lambda r: set_total(r))
-        third = blocks[1].count() // 3
-        blocks[1].step(0, third, mid_total)
-        lines[1].step(2 * (lines[1].count() // 3), lines[1].count(), down_total)
+        own_line(1)
+        for p in range(per):
+            for n in range(end):
+                if (1, p, n) not in plan:
+                    line_step(1, p, n)
         downg[...] = gtot[...].T
+        stores = fetch([pltpu.make_async_copy(downg, downg_ref, osem.at[1])])
+        events = blocks[1].count()
+        scatters[0, 0].third()
+        lines[0, 0].start()
+
         def first_norm(r):
             unit_one, _ = norm_stats(xf[r].astype(F32))
             term = part[r].astype(F32)
@@ -1062,6 +1116,10 @@
             to = ring_next(spot.d, step, geo.dp)
             wire.start(small + step - 1, spart.at[to], sland.at[step - 1], spot.at_d(to))
         stot[...] = spart[spot.d]
+        blocks[1].step(0, 4 * events // 8, mid_total)
+        for p in range(1, per):
+            scatters[0, p].second()
+
         def wgrad(r):
             for j in range(3):
                 wg[j, r] = nn(n1t[r], dqkv[j]).astype(BF)
@@ -1074,23 +1132,22 @@
 
         for i in range(ab):
             wire.start(wzero + i, wg.at[:, wrows_of(i, 1 - spot.c)], wheld.at[0, i // a_size, i % a_size], sibling)
+        blocks[1].step(4 * events // 8, 6 * events // 8, mid_total)
+        for p in range(1, per):
+            scatters[0, p].third()
+            lines[0, p].start()
+        own_line(0)
         for i in range(ab):
             here = wheld.at[0, i // a_size, i % a_size]
             wire.landed(wzero + i, here, sibling)
             wscatter.add(here, wg.at[:, wrows_of(i, spot.c)])
         wscatter.first()
-        blocks[1].step(third, 2 * third, mid_total)
         for step in range(1, geo.dp):
             wire.landed(small + step - 1, sland.at[step - 1], spot.at_d(ring_prev(spot.d, step, geo.dp)))
             stot[...] += sland[step - 1]
         for step in range(1, size):
             wire.start(last + step - 1, stot, tland.at[step - 1], spot.at_t(ring_next(spot.t, step, size)))
-        scatters[0].third()
-        lines[0].start()
-        stores = fetch([pltpu.make_async_copy(downg, downg_ref, osem.at[1])])
-        own_line(0, gtot)
-        wscatter.second()
-        blocks[1].step(2 * third, blocks[1].count(), mid_total)
+        blocks[1].step(6 * events // 8, events, mid_total)
 
         def back(r):
             unit_one, scale_one = norm_stats(xf[own_rows(r, tail)].astype(F32))
@@ -1098,14 +1155,21 @@
 
         loop_rows(rows, tail, back)
         stores += fetch([pltpu.make_async_copy(cot, igrad_ref, osem.at[0])])
-        events = lines[0].count()
-        lines[0].step(0, events // 3, down_total)
+        wscatter.second()
+        ends = sorted((2 * p + n, p, n) for p in range(per) for n in range(end))
+        for _, p, n in ends[:2]:
+            line_step(0, p, n)
         wscatter.third()
-        lines[0].step(events // 3, 2 * events // 3, down_total)
         sums_w = wheld.at[0, spot.b, spot.a]
         for j in range(3):
             awg[j] = sums_w[j].astype(F32)
         owg[...] = sums_w[3].astype(F32).T
+        stores += fetch([
+            pltpu.make_async_copy(awg, awg_ref, osem.at[2]),
+            pltpu.make_async_copy(owg, owg_ref, osem.at[3])])
+        for _, p, n in ends[2:]:
+            line_step(0, p, n)
+        stores += fetch([pltpu.make_async_copy(gtot, upg_ref, osem.at[6])])
         for step in range(1, size):
             wire.landed(last + step - 1, tland.at[step - 1], spot.at_t(ring_prev(spot.t, step, size)))
         total = stot[...]
@@ -1115,12 +1179,8 @@
         for i in range(biasg.shape[0]):
             biasg[i] = total[2 + i:3 + i, :]
         stores += fetch([
-            pltpu.make_async_copy(awg, awg_ref, osem.at[2]),
-            pltpu.make_async_copy(owg, owg_ref, osem.at[3]),
             pltpu.make_async_copy(gaing, gaing_ref, osem.at[4]),
             pltpu.make_async_copy(biasg, biasg_ref, osem.at[5])])
-        lines[0].step(2 * events // 3, events, down_total)
-        stores += fetch([pltpu.make_async_copy(gtot, upg_ref, osem.at[6])])
         wire.drain()
         settle(stores)
 
@@ -1142,12 +1202,14 @@
     size = geo.tensor
     seq = size * rows
     chunk = min(512, unit)
-    sems = 3 * gather_sems(geo) + 48 * size + 3 * scatter_sems(geo) + geo.a_size * geo.b_size + 2 * geo.dp
+    per = unit // chunk
+    sems = ((2 * per + 1) * (gather_sems(geo) + scatter_sems(geo)) + (size - 1) * (2 * 4 + 2 * 4 + 4 * per * 2 + 1) + 2 * per * size
+            + geo.a_size * geo.b_size + 2 * (geo.dp - 1))
     like = lambda x: pltpu.VMEM(x.shape, x.dtype)
     return pl.pallas_call(
         functools.partial(block_body, geo),
         out_shape=(
-            jax.ShapeDtypeStruct((2, size * (unit // chunk), width, chunk), BF),
+            jax.ShapeDtypeStruct((2, unit // chunk, size, width, chunk), BF),
             jax.ShapeDtypeStruct((rows, width), F32),
             jax.ShapeDtypeStruct((rows, width), F32),
             jax.ShapeDtypeStruct((3, wrows, heads), F32),
@@ -1161,7 +1223,7 @@
         out_specs=(ANY,) * 9,
         scratch_shapes=[
             pltpu.VMEM((seq, width), BF),
-            pltpu.VMEM((seq, width), BF),
+            pltpu.VMEM((rows, width), BF),
             pltpu.VMEM((width, seq), BF),
             pltpu.VMEM((3, seq, heads), BF),
             pltpu.VMEM((seq, heads), BF),
@@ -1185,9 +1247,9 @@
             pltpu.VMEM((geo.dp - 1, 12, wrows), F32),
             pltpu.VMEM((12, wrows), F32),
             pltpu.VMEM((size - 1, 12, wrows), F32),
-            *scatter_bufs(geo, 2, size, mrows, unit),
-            *scatter_bufs(geo, 1, 4, wrows, heads),
-            pltpu.VMEM((2, 2, size - 1, mrows, unit), BF),
+            *scatter_bufs(geo, 2 * (unit // chunk), 2 * (unit // chunk), size, mrows, chunk),
+            *scatter_bufs(geo, 1, 1, 4, wrows, heads),
+            pltpu.VMEM((2 * (unit // chunk), 2, size - 1, mrows, chunk), BF),
             pltpu.VMEM((mrows, unit), F32),
             pltpu.VMEM((unit, mrows), F32),
             pltpu.VMEM((3, wrows, heads), F32),
@@ -1196,7 +1258,7 @@
             pltpu.VMEM((10, 1, wrows), F32),
             pltpu.SemaphoreType.DMA((sems,)), pltpu.SemaphoreType.DMA((sems,)), pltpu.SemaphoreType.DMA((8 + unit // chunk,)),
             pltpu.SemaphoreType.DMA((6, 2)), pltpu.SemaphoreType.DMA((7,))],
-        compiler_params=pltpu.CompilerParams(collective_id=1, has_side_effects=True, vmem_limit_bytes=61 * 2**20),
+        compiler_params=pltpu.CompilerParams(collective_id=1, has_side_effects=True, vmem_limit_bytes=62 * 2**20),
         name="block",
     )(x, aw, ow, up, down, gains, biases, seg_row, cot)
 

time: 246 us -> 226 us (0.919)
  Pallas kernels: 245 us -> 224 us
    pallas_call x1, Pallas kernels: 241 us -> 221 us  [block_kernel(): pl.pallas_call(functools.partial(block_body, geo), out_shape=(jax.ShapeDt...]
where the time goes in v3:
time: 226 us; the launch traced here: 225 us
  Pallas kernels  224 us (99%)
    pallas_call x1, Pallas kernels, block_kernel(): pl.pallas_call(functools.partial(block_body, geo), out_shape=(jax.ShapeDt...  221 us

profile of v3, /device:TPU:0, one launch (start us, length us, event | category | flops | bytes accessed | tf_op | source)
XLA Modules:
  0.0 225.3 jit_solution(6265068917738350954)
XLA Ops:
  0.6 221.3 %block.1 = (bf16[2,2,4,1024,512]{4,3,2,1,0:T(8,128)(2,1)}, f32[256,1024]{1,0:T(8,128)}, f32[256,1024]{1,0:T(8,128)}, f32[3,128,256]{2,1,0:T(8,128)}, f32[256,128...) custom-call(bf16[256,1024]{1,0:T(8,128)(2,1)} %x_ref.1, ...), custom_call_target="tpu_custom_call" | custom-call | tf_op jit(solution)/shard_map/block/pallas_call | solution.py:1209
  221.9 3.2 %hand_over.1 = (f32[256,1024]{1,0:T(8,128)}, f32[256,1024]{1,0:T(8,128)}, f32[3,128,256]{2,1,0:T(8,128)}, f32[256,128]{1,0:T(8,128)}, f32[128,1024]{1,0:T(8,128)...) custom-call(f32[256,1024]{1,0:T(8,128)} %get-tuple-element.24.refs_0_, ...), custom_call_target="tpu_custom_call" | custom-call | tf_op jit(solution)/shard_map/hand_over/pallas_call | solution.py:1279

commit v4 on v3

--- a/solution.py
+++ b/solution.py
@@ -260,8 +260,12 @@
             for h in range(self.parts):
                 copy, when = self.wire.plan(
                     self.base[side] + (j - 1 + side) * self.parts + h, halves(self.part(j), self.parts, h),
-                    halves(self.land(side, j), self.parts, h), spot.at_t(to), when=(t == first) & (j != first))
+                    halves(self.land(side, j), self.parts, h), spot.at_t(to), when=(t == first) & (j != first) & (j != 1 if side == 0 else True))
                 pl.when(when)(copy.start)
+
+    def start_near(self):
+        for h in range(self.parts):
+            self.wire.go(self.starts[0, 1, h])
 
     def owe_starts(self):
         for planned in self.starts.values():
@@ -1074,6 +1078,11 @@
                     block_bias(seg_col, seg_row, bias, start, rows, stop)
                     attend_block_back(qkv, bias, lse, do, dqkv.at[0], dk, dv, start, rows)
 
+            @pl.when((k == end) & (spot.t == 0))
+            def _():
+                scatters[0, 0].third()
+                lines[0, 0].start()
+
             def ready(n, inner):
                 i = jnp.where(lax.rem(n, 2) == 0, end - lax.div(n, 2), lax.div(n, 2))
 
@@ -1098,8 +1107,11 @@
         downg[...] = gtot[...].T
         stores = fetch([pltpu.make_async_copy(downg, downg_ref, osem.at[1])])
         events = blocks[1].count()
-        scatters[0, 0].third()
-        lines[0, 0].start()
+
+        @pl.when(spot.t != 0)
+        def _():
+            scatters[0, 0].third()
+            lines[0, 0].start()
 
         def first_norm(r):
             unit_one, _ = norm_stats(xf[r].astype(F32))
@@ -1119,6 +1131,8 @@
         blocks[1].step(0, 4 * events // 8, mid_total)
         for p in range(1, per):
             scatters[0, p].second()
+        if end > 1:
+            line_step(0, 0, 0)
 
         def wgrad(r):
             for j in range(3):
@@ -1132,10 +1146,13 @@
 
         for i in range(ab):
             wire.start(wzero + i, wg.at[:, wrows_of(i, 1 - spot.c)], wheld.at[0, i // a_size, i % a_size], sibling)
+        for n in range(1, end - 1):
+            line_step(0, 0, n)
         blocks[1].step(4 * events // 8, 6 * events // 8, mid_total)
         for p in range(1, per):
             scatters[0, p].third()
             lines[0, p].start()
+        blocks[1].start_near()
         own_line(0)
         for i in range(ab):
             here = wheld.at[0, i // a_size, i % a_size]
@@ -1147,6 +1164,10 @@
             stot[...] += sland[step - 1]
         for step in range(1, size):
             wire.start(last + step - 1, stot, tland.at[step - 1], spot.at_t(ring_next(spot.t, step, size)))
+        for p in range(1, per):
+            for n in range(end - 1):
+                line_step(0, p, n)
+        wscatter.second()
         blocks[1].step(6 * events // 8, events, mid_total)
 
         def back(r):
@@ -1155,10 +1176,6 @@
 
         loop_rows(rows, tail, back)
         stores += fetch([pltpu.make_async_copy(cot, igrad_ref, osem.at[0])])
-        wscatter.second()
-        ends = sorted((2 * p + n, p, n) for p in range(per) for n in range(end))
-        for _, p, n in ends[:2]:
-            line_step(0, p, n)
         wscatter.third()
         sums_w = wheld.at[0, spot.b, spot.a]
         for j in range(3):
@@ -1167,8 +1184,8 @@
         stores += fetch([
             pltpu.make_async_copy(awg, awg_ref, osem.at[2]),
             pltpu.make_async_copy(owg, owg_ref, osem.at[3])])
-        for _, p, n in ends[2:]:
-            line_step(0, p, n)
+        for p in range(per):
+            line_step(0, p, end - 1)
         stores += fetch([pltpu.make_async_copy(gtot, upg_ref, osem.at[6])])
         for step in range(1, size):
             wire.landed(last + step - 1, tland.at[step - 1], spot.at_t(ring_prev(spot.t, step, size)))

time: 226 us -> 223 us (0.987)
  Pallas kernels: 224 us -> 221 us
    pallas_call x1, Pallas kernels: 221 us -> 218 us  [block_kernel(): pl.pallas_call(functools.partial(block_body, geo), out_shape=(jax.ShapeDt...]
where the time goes in v4:
time: 223 us; the launch traced here: 222 us
  Pallas kernels  221 us (99%)
    pallas_call x1, Pallas kernels, block_kernel(): pl.pallas_call(functools.partial(block_body, geo), out_shape=(jax.ShapeDt...  218 us

profile of v4, /device:TPU:0, one launch (start us, length us, event | category | flops | bytes accessed | tf_op | source)
XLA Modules:
  0.0 221.8 jit_solution(3294328429735948984)
XLA Ops:
  0.6 217.8 %block.1 = (bf16[2,2,4,1024,512]{4,3,2,1,0:T(8,128)(2,1)}, f32[256,1024]{1,0:T(8,128)}, f32[256,1024]{1,0:T(8,128)}, f32[3,128,256]{2,1,0:T(8,128)}, f32[256,128...) custom-call(bf16[256,1024]{1,0:T(8,128)(2,1)} %x_ref.1, ...), custom_call_target="tpu_custom_call" | custom-call | tf_op jit(solution)/shard_map/block/pallas_call | solution.py:1226
  218.4 3.2 %hand_over.1 = (f32[256,1024]{1,0:T(8,128)}, f32[256,1024]{1,0:T(8,128)}, f32[3,128,256]{2,1,0:T(8,128)}, f32[256,128]{1,0:T(8,128)}, f32[128,1024]{1,0:T(8,128)...) custom-call(f32[256,1024]{1,0:T(8,128)} %get-tuple-element.24.refs_0_, ...), custom_call_target="tpu_custom_call" | custom-call | tf_op jit(solution)/shard_map/hand_over/pallas_call | solution.py:1296

commit v5 on v4

--- a/solution.py
+++ b/solution.py
@@ -186,21 +186,33 @@
         src = halves(self.src, self.parts, part) if first else piece
         return self.wire.plan(self.base[side] + k * self.parts + part, src, piece, self.spot.at_t(onward), when=going)
 
-    def start(self):
+    def start(self, where=None):
         for part in range(self.parts):
             for side in range(2):
-                self.wire.go(self.sends[0, part, side])
-
-    def step(self, k):
+                planned = self.sends[0, part, side]
+                if where is None:
+                    self.wire.go(planned)
+                else:
+                    copy, when = planned
+                    pl.when(when & self.inner(where))(copy.start)
+                    self.wire.owe(planned)
+
+    def inner(self, where):
+        inner = (self.spot.t >= 1) & (self.spot.t < self.size - 1)
+        return inner if where else jnp.logical_not(inner)
+
+    def step(self, k, where=None):
         for part in range(self.parts):
             for side in range(2):
                 origin, there, near, _, _ = self.place(k, side)
+                if where is not None:
+                    there = there & self.inner(where)
                 piece = halves(self.slot(origin), self.parts, part)
                 self.wire.landed(self.base[side] + (k - 1) * self.parts + part, piece, self.spot.at_t(near), when=there)
                 if not isinstance(k, int):
                     copy, going = self.plan(k, part, side)
                     pl.when(going & (k < self.size - 1))(copy.start)
-                elif k < self.size - 1:
+                elif k < self.size - 1 and where is not False:
                     self.wire.go(self.sends[k, part, side])
 
     def owe(self):
@@ -260,8 +272,13 @@
             for h in range(self.parts):
                 copy, when = self.wire.plan(
                     self.base[side] + (j - 1 + side) * self.parts + h, halves(self.part(j), self.parts, h),
-                    halves(self.land(side, j), self.parts, h), spot.at_t(to), when=(t == first) & (j != first) & (j != 1 if side == 0 else True))
+                    halves(self.land(side, j), self.parts, h), spot.at_t(to), when=(t == first) & (j != first) & (j != 1 if side == 0 else (j == 0) | (j == end - 1)))
                 pl.when(when)(copy.start)
+
+    def start_middle(self):
+        for j in range(1, self.size - 2):
+            for h in range(self.parts):
+                self.wire.go(self.starts[1, j, h])
 
     def start_near(self):
         for h in range(self.parts):
@@ -663,7 +680,7 @@
     gas = LineGather(spot, wire, block_of(gaf, spot.t), lambda t: block_of(gaf, t))
     blocks = [
         LineScatter(spot, wire, lambda t: block_of(part, t), lambda side, j: land.at[side, j - 1 + side],
-                    lambda dst, src: add_tiled(dst, src, tail), rising=k) for k in range(2)]
+                    lambda dst, src: add_tiled(dst, src, tail), rising=(0, None)[k]) for k in range(2)]
     scatters, lines = {}, {}
 
     def line_of(k, p):
@@ -753,8 +770,9 @@
 
         @pl.when(k == end - 1)
         def _():
-            for p in range(per):
-                wlines[1, p].start()
+            wlines[1, 0].start()
+            for p in range(1, per):
+                wlines[1, p].start(False)
 
         def side(i, inner):
             t = spot.t + (2 * i - 1) * k
@@ -787,15 +805,21 @@
     lax.fori_loop(0, size, arrive, 0)
     xs.owe()
     for k in range(1, end):
-        for p in range(per):
-            wlines[1, p].step(k)
+        wlines[1, 0].step(k)
+        if k == max(1, end - 1):
+            for p in range(1, per):
+                wlines[1, p].start(True)
         if k == 1:
             for p in range(per):
                 gathers[0, p].third()
     store(1).wait()
-    for p in range(per):
-        wlines[1, p].step(end)
+    wlines[1, 0].step(end)
+    gathers[1, 0].first()
+    for p in range(1, per):
+        for k in range(1, size):
+            wlines[1, p].step(k)
         gathers[1, p].first()
+
     def set_total(r):
         mid[r] = part[own_rows(r, tail)].astype(F32)
 
@@ -964,11 +988,11 @@
             lax.fori_loop(p * size, (p + 1) * size, keep_up, 0)
             if p:
                 scatters[1, p].second()
+        scatters[0, 0].first()
         ahead((1,))
         gas.step(1)
         scatters[1, 0].third()
         lines[1, 0].start()
-        scatters[0, 0].first()
         dn2[...] = jnp.zeros_like(dn2)
 
         def output(j, s):
@@ -1052,10 +1076,15 @@
                     for key, at in plan.items():
                         if at == n:
                             line_step(*key)
-                    if n == end:
+                    if n == max(1, end - 1):
                         scatters[0, 0].second()
                         for p in range(1, per):
                             scatters[0, p].first()
+
+            @pl.when((k == end) & (spot.t == 0))
+            def _():
+                scatters[0, 0].third()
+                lines[0, 0].start()
 
             @pl.when(k >= 3)
             def _():
@@ -1078,11 +1107,6 @@
                     block_bias(seg_col, seg_row, bias, start, rows, stop)
                     attend_block_back(qkv, bias, lse, do, dqkv.at[0], dk, dv, start, rows)
 
-            @pl.when((k == end) & (spot.t == 0))
-            def _():
-                scatters[0, 0].third()
-                lines[0, 0].start()
-
             def ready(n, inner):
                 i = jnp.where(lax.rem(n, 2) == 0, end - lax.div(n, 2), lax.div(n, 2))
 
@@ -1098,6 +1122,7 @@
         lax.fori_loop(0, size, arrive_back, 0)
         gas.owe()
         blocks[1].owe_starts()
+        blocks[1].start_middle()
         loop_rows(rows, tail, lambda r: set_total(r))
         own_line(1)
         for p in range(per):
@@ -1128,12 +1153,9 @@
             to = ring_next(spot.d, step, geo.dp)
             wire.start(small + step - 1, spart.at[to], sland.at[step - 1], spot.at_d(to))
         stot[...] = spart[spot.d]
-        blocks[1].step(0, 4 * events // 8, mid_total)
+        blocks[1].step(0, events // 3, mid_total)
         for p in range(1, per):
             scatters[0, p].second()
-        if end > 1:
-            line_step(0, 0, 0)
-
         def wgrad(r):
             for j in range(3):
                 wg[j, r] = nn(n1t[r], dqkv[j]).astype(BF)
@@ -1146,14 +1168,12 @@
 
         for i in range(ab):
             wire.start(wzero + i, wg.at[:, wrows_of(i, 1 - spot.c)], wheld.at[0, i // a_size, i % a_size], sibling)
-        for n in range(1, end - 1):
-            line_step(0, 0, n)
-        blocks[1].step(4 * events // 8, 6 * events // 8, mid_total)
         for p in range(1, per):
             scatters[0, p].third()
             lines[0, p].start()
         blocks[1].start_near()
         own_line(0)
+        blocks[1].step(events // 3, 2 * events // 3, mid_total)
         for i in range(ab):
             here = wheld.at[0, i // a_size, i % a_size]
             wire.landed(wzero + i, here, sibling)
@@ -1164,11 +1184,15 @@
             stot[...] += sland[step - 1]
         for step in range(1, size):
             wire.start(last + step - 1, stot, tland.at[step - 1], spot.at_t(ring_next(spot.t, step, size)))
+        if end > 1:
+            line_step(0, 0, 0)
+        wscatter.second()
+        for n in range(1, end - 1):
+            line_step(0, 0, n)
         for p in range(1, per):
             for n in range(end - 1):
                 line_step(0, p, n)
-        wscatter.second()
-        blocks[1].step(6 * events // 8, events, mid_total)
+        blocks[1].step(2 * events // 3, events, mid_total)
 
         def back(r):
             unit_one, scale_one = norm_stats(xf[own_rows(r, tail)].astype(F32))

time: 223 us -> 219 us (0.982)
  Pallas kernels: 221 us -> 218 us
    pallas_call x1, Pallas kernels: 218 us -> 215 us  [block_kernel(): pl.pallas_call(functools.partial(block_body, geo), out_shape=(jax.ShapeDt...]
where the time goes in v5:
time: 219 us
  Pallas kernels  218 us (100%)
    pallas_call x1, Pallas kernels, block_kernel(): pl.pallas_call(functools.partial(block_body, geo), out_shape=(jax.ShapeDt...  215 us

profile of v5, /device:TPU:0, one launch (start us, length us, event | category | flops | bytes accessed | tf_op | source)
XLA Modules:
  0.0 219.3 jit_solution(5081670488843430993)
XLA Ops:
  0.6 215.3 %block.1 = (bf16[2,2,4,1024,512]{4,3,2,1,0:T(8,128)(2,1)}, f32[256,1024]{1,0:T(8,128)}, f32[256,1024]{1,0:T(8,128)}, f32[3,128,256]{2,1,0:T(8,128)}, f32[256,128...) custom-call(bf16[256,1024]{1,0:T(8,128)(2,1)} %x_ref.1, ...), custom_call_target="tpu_custom_call" | custom-call | tf_op jit(solution)/shard_map/block/pallas_call | solution.py:1250
  215.9 3.2 %hand_over.1 = (f32[256,1024]{1,0:T(8,128)}, f32[256,1024]{1,0:T(8,128)}, f32[3,128,256]{2,1,0:T(8,128)}, f32[256,128]{1,0:T(8,128)}, f32[128,1024]{1,0:T(8,128)...) custom-call(f32[256,1024]{1,0:T(8,128)} %get-tuple-element.24.refs_0_, ...), custom_call_target="tpu_custom_call" | custom-call | tf_op jit(solution)/shard_map/hand_over/pallas_call | solution.py:1320

commit v6 on v5

--- a/solution.py
+++ b/solution.py
@@ -84,10 +84,18 @@
 
 
 class Wire:
-    def __init__(self, send, recv):
-        self.send_sems, self.recv_sems = send, recv
-        self.count = 0
-        self.pending = []
+    def __init__(self, send, recv, base):
+        self.send_sems, self.recv_sems, self.base = send, recv, base
+        self.count = self.grouped = 0
+        self.pending, self.quiet, self.totals, self.group_of = [], [], [], {}
+
+    def take_group(self, n, whole, device):
+        first = self.base + self.grouped
+        self.grouped += n
+        group = self.base + len(self.totals)
+        self.group_of.update((i, group) for i in range(first, first + n))
+        self.totals.append((group, whole, device))
+        return first
 
     def take(self, n):
         first = self.count
@@ -96,11 +104,14 @@
 
     def copy(self, i, src, dst, device):
         return pltpu.make_async_remote_copy(
-            src_ref=src, dst_ref=dst, send_sem=self.send_sems.at[i], recv_sem=self.recv_sems.at[i],
+            src_ref=src, dst_ref=dst, send_sem=self.send_sems.at[self.group_of.get(i, i) if isinstance(i, int) else i], recv_sem=self.recv_sems.at[i],
             device_id=device, device_id_type=MESH_ID)
 
     def plan(self, i, src, dst, device, when=None):
-        return self.copy(i, src, dst, device), when
+        planned = self.copy(i, src, dst, device), when
+        if isinstance(i, int) and i in self.group_of:
+            self.quiet.append(planned)
+        return planned
 
     def go(self, planned):
         copy, when = planned
@@ -111,7 +122,7 @@
         self.owe(planned)
 
     def owe(self, planned):
-        if not any(other is planned for other in self.pending):
+        if not any(other is planned for other in self.pending + self.quiet):
             self.pending.append(planned)
 
     def start(self, i, src, dst, device, when=None):
@@ -139,6 +150,10 @@
                 copy.wait_send()
             else:
                 pl.when(when)(copy.wait_send)
+        for group, whole, device in self.totals:
+            pltpu.make_async_remote_copy(
+                src_ref=whole, dst_ref=whole, send_sem=self.send_sems.at[group], recv_sem=self.recv_sems.at[group],
+                device_id=device, device_id_type=MESH_ID).wait_send()
         self.pending = []
 
 
@@ -331,11 +346,13 @@
         self.spot, self.wire, self.full, self.rows = spot, wire, full, rows
         self.slots = full.shape[0]
         self.half = self.slots // 2
-        self.one_a = wire.take(geo.a_size - 1)
-        self.one_b = wire.take(geo.b_size - 1)
-        self.two_a = wire.take((geo.b_size - 1) * geo.a_size)
-        self.two_b = wire.take((geo.a_size - 1) * geo.b_size)
-        self.last = wire.take(2 * geo.a_size * geo.b_size)
+        a, b = geo.a_size, geo.b_size
+        counts = [a - 1, b - 1, (b - 1) * a, (a - 1) * b, 2 * a * b]
+        whole = full.at[:, pl.ds(0, sum(counts) // 2 * rows)]
+        firsts = [wire.take_group(sum(counts), whole, spot.at_d(spot.rank(spot.b, spot.a, 1 - spot.c)))]
+        for n in counts[:-1]:
+            firsts.append(firsts[-1] + n)
+        self.one_a, self.one_b, self.two_a, self.two_b, self.last = firsts
         self.plan_shares()
         self.plan_hops()
 
@@ -644,7 +661,8 @@
                gtot, downg, awg, owg, gaing, biasg,
                send, recv, local, msem, osem):
     spot = geo.bind()
-    wire = Wire(send, recv)
+    groups = 2 * (up_ref.shape[1] // min(512, up_ref.shape[1])) + 1
+    wire = Wire(send, recv, send.shape[0] - groups)
     size = geo.tensor
     rows, width = x_ref.shape
     seq = size * rows
@@ -697,7 +715,7 @@
     gains_in = wire.take(geo.dp - 1)
     small = wire.take(geo.dp - 1)
     last = wire.take(size - 1)
-    assert wire.count == send.shape[0]
+    assert wire.count == wire.base and recv.shape[0] == wire.base + wire.grouped
 
     pairs = [
         (gain_ref, gain_in), (bias_ref, bias_in), (aw_ref, wsend.at[pl.ds(0, 3)]), (ow_ref, ow_in),
@@ -1246,6 +1264,7 @@
     per = unit // chunk
     sems = ((2 * per + 1) * (gather_sems(geo) + scatter_sems(geo)) + (size - 1) * (2 * 4 + 2 * 4 + 4 * per * 2 + 1) + 2 * per * size
             + geo.a_size * geo.b_size + 2 * (geo.dp - 1))
+    shared = (2 * per + 1) * gather_sems(geo)
     like = lambda x: pltpu.VMEM(x.shape, x.dtype)
     return pl.pallas_call(
         functools.partial(block_body, geo),
@@ -1297,7 +1316,7 @@
             pltpu.VMEM((heads, wrows), F32),
             pltpu.VMEM((2, wrows), F32),
             pltpu.VMEM((10, 1, wrows), F32),
-            pltpu.SemaphoreType.DMA((sems,)), pltpu.SemaphoreType.DMA((sems,)), pltpu.SemaphoreType.DMA((8 + unit // chunk,)),
+            pltpu.SemaphoreType.DMA((sems - shared + 2 * per + 1,)), pltpu.SemaphoreType.DMA((sems,)), pltpu.SemaphoreType.DMA((8 + unit // chunk,)),
             pltpu.SemaphoreType.DMA((6, 2)), pltpu.SemaphoreType.DMA((7,))],
         compiler_params=pltpu.CompilerParams(collective_id=1, has_side_effects=True, vmem_limit_bytes=62 * 2**20),
         name="block",

time: 219 us -> 219 us (level)
  no operation moved by 1% of the time
where the time goes in v6:
time: 219 us
  Pallas kernels  218 us (100%)
    pallas_call x1, Pallas kernels, block_kernel(): pl.pallas_call(functools.partial(block_body, geo), out_shape=(jax.ShapeDt...  215 us

profile of v6, /device:TPU:0, one launch (start us, length us, event | category | flops | bytes accessed | tf_op | source)
XLA Modules:
  0.0 218.7 jit_solution(17985237525561405325)
XLA Ops:
  0.6 214.7 %block.1 = (bf16[2,2,4,1024,512]{4,3,2,1,0:T(8,128)(2,1)}, f32[256,1024]{1,0:T(8,128)}, f32[256,1024]{1,0:T(8,128)}, f32[3,128,256]{2,1,0:T(8,128)}, f32[256,128...) custom-call(bf16[256,1024]{1,0:T(8,128)(2,1)} %x_ref.1, ...), custom_call_target="tpu_custom_call" | custom-call | tf_op jit(solution)/shard_map/block/pallas_call | solution.py:1269
  215.3 3.2 %hand_over.1 = (f32[256,1024]{1,0:T(8,128)}, f32[256,1024]{1,0:T(8,128)}, f32[3,128,256]{2,1,0:T(8,128)}, f32[256,128]{1,0:T(8,128)}, f32[128,1024]{1,0:T(8,128)...) custom-call(f32[256,1024]{1,0:T(8,128)} %get-tuple-element.24.refs_0_, ...), custom_call_target="tpu_custom_call" | custom-call | tf_op jit(solution)/shard_map/hand_over/pallas_call | solution.py:1339

commit v7 on v6

--- a/solution.py
+++ b/solution.py
@@ -1086,11 +1086,16 @@
         plan = {key: at for key, at in plan.items() if at < size}
 
         def arrive_back(k, carry):
+            if size > 2:
+                @pl.when(k == 0)
+                def _():
+                    gas.step(2, True)
+
             for n in range(1, size):
                 @pl.when(k == n)
                 def _():
                     if n == 1 and size > 2:
-                        gas.step(2)
+                        gas.step(2, False)
                     for key, at in plan.items():
                         if at == n:
                             line_step(*key)

time: 219 us -> 219 us (level)
  no operation moved by 1% of the time
where the time goes in v7:
time: 219 us
  Pallas kernels  218 us (100%)
    pallas_call x1, Pallas kernels, block_kernel(): pl.pallas_call(functools.partial(block_body, geo), out_shape=(jax.ShapeDt...  215 us

profile of v7, /device:TPU:0, one launch (start us, length us, event | category | flops | bytes accessed | tf_op | source)
XLA Modules:
  0.0 218.8 jit_solution(17924408015807297155)
XLA Ops:
  0.6 214.8 %block.1 = (bf16[2,2,4,1024,512]{4,3,2,1,0:T(8,128)(2,1)}, f32[256,1024]{1,0:T(8,128)}, f32[256,1024]{1,0:T(8,128)}, f32[3,128,256]{2,1,0:T(8,128)}, f32[256,128...) custom-call(bf16[256,1024]{1,0:T(8,128)(2,1)} %x_ref.1, ...), custom_call_target="tpu_custom_call" | custom-call | tf_op jit(solution)/shard_map/block/pallas_call | solution.py:1274
  215.4 3.2 %hand_over.1 = (f32[256,1024]{1,0:T(8,128)}, f32[256,1024]{1,0:T(8,128)}, f32[3,128,256]{2,1,0:T(8,128)}, f32[256,128]{1,0:T(8,128)}, f32[128,1024]{1,0:T(8,128)...) custom-call(f32[256,1024]{1,0:T(8,128)} %get-tuple-element.24.refs_0_, ...), custom_call_target="tpu_custom_call" | custom-call | tf_op jit(solution)/shard_map/hand_over/pallas_call | solution.py:1344
